TPU v7x, 128 devices: a whole 4x4x4 slice. The times are simulated.
128 devices in a mesh: clip: 16 (over y, x), cap: 8 (over z, core).
Axes of the slice: x: 4, y: 4, z: 4, core: 2. Of those that a mesh axis runs over, the one named last changes fastest.
Arguments:
- teacher_audio: bfloat16 [24576, 512], P(('clip', 'cap')), may hold values from -2 to 2
- teacher_text: bfloat16 [24576, 512], P(('cap', 'clip')), may hold values from -2 to 2
- student_audio: bfloat16 [24576, 512], P(('clip', 'cap')), may hold values from -2 to 2
- student_text: bfloat16 [24576, 512], P(('cap', 'clip')), may hold values from -2 to 2
Outputs:
- audio_grad: float32 [24576, 512], P(('clip', 'cap'))
- text_grad: float32 [24576, 512], P(('cap', 'clip'))
All inputs are finite; a program needn't handle non-finite values.
Results may differ from a plain program's by a relative error of at most 0.0026.
Values may be sent and summed in bfloat16 or wider, within the bound.
No kernel may reach another device: no remote copies, remote signals or barrier semaphores. Data moves between devices by JAX's collectives and lax.ppermute only.
A program may use at most 128 MiB of HBM per device.

v0:
```python
import jax
import jax.numpy as jnp
from jax import lax
from jax.sharding import PartitionSpec as P

ITERS = 3


def contract_rows(left_mat, right_mat):
    return lax.dot_general(
        left_mat, right_mat, (((1,), (1,)), ((), ())), preferred_element_type=jnp.float32
    )


def contract_first(left_mat, right_mat):
    return lax.dot_general(
        left_mat, right_mat, (((0,), (0,)), ((), ())), preferred_element_type=jnp.float32
    )


def body(teacher_audio, teacher_text, student_audio, student_text):
    audio_teacher, audio_student = (
        lax.all_gather(teacher_audio, "cap", axis=0, tiled=True),
        lax.all_gather(student_audio, "cap", axis=0, tiled=True),
    )
    text_teacher, text_student = (
        lax.all_gather(teacher_text, "clip", axis=0, tiled=True),
        lax.all_gather(student_text, "clip", axis=0, tiled=True),
    )
    teacher_logits = 10.0 * contract_rows(audio_teacher, text_teacher)
    student_logits = 10.0 * contract_rows(audio_student, text_student)
    teacher_max, student_max = lax.pmax(
        (jnp.max(teacher_logits, axis=1), jnp.max(student_logits, axis=1)), "cap"
    )
    student_exp = jnp.exp(student_logits - student_max[:, None])
    student_total = lax.psum(jnp.sum(student_exp, axis=1), "cap")
    kernel = jnp.exp(teacher_logits - teacher_max[:, None])
    weights_row = jnp.ones((kernel.shape[0],), jnp.float32)
    column_scale = jnp.ones((kernel.shape[1],), jnp.float32)
    for sweep_index in range(ITERS):
        column = lax.psum(jnp.dot(weights_row, kernel, precision=lax.Precision.HIGHEST), "clip")
        column_scale = 1.0 / column
        row_total = lax.psum(jnp.dot(kernel, column_scale, precision=lax.Precision.HIGHEST), "cap")
        weights_row = 1.0 / row_total
    target = weights_row[:, None] * kernel * column_scale[None, :]
    student_prob = student_exp / student_total[:, None]
    residual = (student_prob - target).astype(jnp.bfloat16)
    audio_grad = lax.psum_scatter(
        10.0 * jnp.dot(residual, text_student, preferred_element_type=jnp.float32),
        "cap",
        scatter_dimension=0,
        tiled=True,
    )
    text_grad = lax.psum_scatter(
        10.0 * contract_first(residual, audio_student), "clip", scatter_dimension=0, tiled=True
    )
    return (audio_grad, text_grad)


def solution(mesh):
    placed = (
        P(("clip", "cap"), None),
        P(("cap", "clip"), None),
        P(("clip", "cap"), None),
        P(("cap", "clip"), None),
    )
    return jax.shard_map(
        body,
        mesh=mesh,
        in_specs=placed,
        out_specs=(P(("clip", "cap"), None), P(("cap", "clip"), None)),
        check_vma=False,
    )
```

profile of v0, /device:TPU:0, one launch (start us, length us, event | category | flops | bytes accessed | tf_op | source)
XLA Modules:
  0.0 724.7 jit_solution(157814558022835361)
XLA Ops:
  7.2 0.0 all-gather.9.cloned.1.call-start
  7.2 0.7 all-gather.9.cloned.1.call-update
  7.9 0.0 all-gather.11.cloned.1.call-start
  7.9 0.7 all-gather.11.cloned.1.call-update
  8.6 0.0 all-gather.5.cloned.1.call-start
  8.7 0.7 all-gather.5.cloned.1.call-update
  9.4 0.0 all-gather.7.cloned.1.call-start
  9.4 0.5 all-gather.7.cloned.1.call-update
  10.0 0.0 reduce-scatter.3.cloned.1.call-start
  10.0 26.7 %all-gather.9.cloned.1.call-done = bf16[1536,512]{1,0:T(8,128)(2,1)} async-done(((bf16[192,512]{1,0:T(8,128)(2,1)}), bf16[1536,512]{1,0:T(8,128)(2,1)}) %all-gather.9.cloned.1.call-update) | async-done | bytes 1572880 | tf_op jit(solution)/shard_map/all_gather | solution.py:23
  36.7 50.0 %all-gather.11.cloned.1.call-done = bf16[3072,512]{1,0:T(8,128)(2,1)} async-done(((bf16[192,512]{1,0:T(8,128)(2,1)}), bf16[3072,512]{1,0:T(8,128)(2,1)}) %all-gather.11.cloned.1.call-update) | async-done | bytes 3145744 | tf_op jit(solution)/shard_map/all_gather | solution.py:27
  86.7 11.3 %multiply_reduce_fusion = (f32[1536]{0:T(1024)S(1)}, f32[1536,3072]{1,0:T(8,128)}) fusion(bf16[1536,512]{1,0:T(8,128)(2,1)} %all-gather.9.cloned.1.call-done, bf16[3072,512]{1,0:T(8,128)(2,1)} %all-gather.11.cloned.1.call-done), kind=kOutput, calls=%fused_computation.3 | convolution fusion | flops 4841273856 | bytes 23599104 | tf_op jit(solution)/shard_map/dot_general | solution.py:10
  98.0 14.0 %all-gather.5.cloned.1.call-done = bf16[1536,512]{1,0:T(8,128)(2,1)} async-done(((bf16[192,512]{1,0:T(8,128)(2,1)}), bf16[1536,512]{1,0:T(8,128)(2,1)}) %all-gather.5.cloned.1.call-update) | async-done | bytes 1572880 | tf_op jit(solution)/shard_map/all_gather | solution.py:24
  112.0 49.9 %all-gather.7.cloned.1.call-done = bf16[3072,512]{1,0:T(8,128)(2,1)} async-done(((bf16[192,512]{1,0:T(8,128)(2,1)}), bf16[3072,512]{1,0:T(8,128)(2,1)}) %all-gather.7.cloned.1.call-update) | async-done | bytes 3145744 | tf_op jit(solution)/shard_map/all_gather | solution.py:28
  161.9 11.0 %multiply_reduce_fusion.1 = (f32[1536]{0:T(1024)S(1)}, f32[1536,3072]{1,0:T(8,128)}) fusion(bf16[1536,512]{1,0:T(8,128)(2,1)} %all-gather.5.cloned.1.call-done, bf16[3072,512]{1,0:T(8,128)(2,1)} %all-gather.7.cloned.1.call-done), kind=kOutput, calls=%fused_computation.4 | convolution fusion | flops 4841273856 | bytes 23599104 | tf_op jit(solution)/shard_map/dot_general | solution.py:10
  172.8 25.5 %all-reduce.1 = (f32[1536]{0:T(1024)S(1)}, f32[1536]{0:T(1024)S(1)}) all-reduce(f32[1536]{0:T(1024)S(1)} %get-tuple-element.6, f32[1536]{0:T(1024)S(1)} %get-tuple-element.8), channel_id=1, replica_groups=mesh['clip'=16,'cap'=8] {'cap'}, use_global_device_ids=true, to_apply=%region_5.0 | all-reduce | flops 3072 | bytes 24576 | tf_op jit(solution)/shard_map/pmax | solution.py:32
  198.3 14.5 %fusion.1 = f32[1,3072]{1,0:T(1,128)S(1)} fusion(f32[1536,3072]{1,0:T(8,128)} %get-tuple-element.7, f32[1536]{0:T(1024)S(1)} %get-tuple-element.4), kind=kOutput, calls=%fused_computation.17 | convolution fusion | flops 66060288 | bytes 18892800 | tf_op jit(solution)/shard_map/dot_general | solution.py:41
  212.8 72.6 %psum.50 = f32[3072]{0:T(1024)S(1)} all-reduce(f32[3072]{0:T(1024)S(1)} %bitcast.22), channel_id=1, replica_groups=mesh['clip'=16,'cap'=8] {'clip'}, use_global_device_ids=true, to_apply=%region_6.0 | all-reduce | flops 3072 | bytes 24576 | tf_op jit(solution)/shard_map/psum | solution.py:41
  285.5 21.5 %convolution_reduce_fusion.2 = f32[1536]{0:T(1024)S(1)} fusion(f32[3072,1]{0,1:T(1,128)S(1)} %bitcast.20, f32[1536,3072]{1,0:T(8,128)} %get-tuple-element.7, f32[1536]{0:T(1024)S(1)} %get-tuple-element.4), kind=kOutput, calls=%fused_computation.10 | convolution fusion | flops 66060288 | bytes 18898944 | tf_op jit(solution)/shard_map/dot_general | solution.py:43
  307.0 12.7 %psum.51 = f32[1536]{0:T(1024)S(1)} all-reduce(f32[1536]{0:T(1024)S(1)} %convolution_reduce_fusion.2), channel_id=1, replica_groups=mesh['clip'=16,'cap'=8] {'cap'}, use_global_device_ids=true, to_apply=%region_7.0 | all-reduce | flops 1536 | bytes 12288 | tf_op jit(solution)/shard_map/psum | solution.py:43
  319.7 14.5 %fusion.5 = f32[1,3072]{1,0:T(1,128)S(1)} fusion(f32[1536,1]{0,1:T(1,128)S(1)} %reshape.13, f32[1536,3072]{1,0:T(8,128)} %get-tuple-element.7, f32[1536]{0:T(1024)S(1)} %get-tuple-element.4), kind=kOutput, calls=%fused_computation.21 | convolution fusion | flops 66060288 | bytes 18898944 | tf_op jit(solution)/shard_map/dot_general | solution.py:41
  334.2 69.7 %psum.52 = f32[3072]{0:T(1024)S(1)} all-reduce(f32[3072]{0:T(1024)S(1)} %bitcast.23), channel_id=1, replica_groups=mesh['clip'=16,'cap'=8] {'clip'}, use_global_device_ids=true, to_apply=%region_8.0 | all-reduce | flops 3072 | bytes 24576 | tf_op jit(solution)/shard_map/psum | solution.py:41
  403.9 21.5 %convolution_reduce_fusion.1 = f32[1536]{0:T(1024)S(1)} fusion(f32[3072,1]{0,1:T(1,128)S(1)} %bitcast.21, f32[1536,3072]{1,0:T(8,128)} %get-tuple-element.7, f32[1536]{0:T(1024)S(1)} %get-tuple-element.4), kind=kOutput, calls=%fused_computation.9 | convolution fusion | flops 66060288 | bytes 18898944 | tf_op jit(solution)/shard_map/dot_general | solution.py:43
  425.4 12.7 %psum.53 = f32[1536]{0:T(1024)S(1)} all-reduce(f32[1536]{0:T(1024)S(1)} %convolution_reduce_fusion.1), channel_id=1, replica_groups=mesh['clip'=16,'cap'=8] {'cap'}, use_global_device_ids=true, to_apply=%region_9.0 | all-reduce | flops 1536 | bytes 12288 | tf_op jit(solution)/shard_map/psum | solution.py:43
  438.1 14.5 %fusion.4 = f32[1,3072]{1,0:T(1,128)S(1)} fusion(f32[1536,1]{0,1:T(1,128)S(1)} %reshape.17, f32[1536,3072]{1,0:T(8,128)} %get-tuple-element.7, f32[1536]{0:T(1024)S(1)} %get-tuple-element.4), kind=kOutput, calls=%fused_computation.20 | convolution fusion | flops 66060288 | bytes 18898944 | tf_op jit(solution)/shard_map/dot_general | solution.py:41
  452.6 69.7 %psum.54 = f32[3072]{0:T(1024)S(1)} all-reduce(f32[3072]{0:T(1024)S(1)} %bitcast.24), channel_id=1, replica_groups=mesh['clip'=16,'cap'=8] {'clip'}, use_global_device_ids=true, to_apply=%region_10.0 | all-reduce | flops 3072 | bytes 24576 | tf_op jit(solution)/shard_map/psum | solution.py:41
  522.4 21.5 %convolution_reduce_fusion = f32[1536]{0:T(1024)S(1)} fusion(f32[3072,1]{0,1:T(1,128)S(1)} %bitcast.19, f32[1536,3072]{1,0:T(8,128)} %get-tuple-element.7, f32[1536]{0:T(1024)S(1)} %get-tuple-element.4), kind=kOutput, calls=%fused_computation.8 | convolution fusion | flops 66060288 | bytes 18898944 | tf_op jit(solution)/shard_map/dot_general | solution.py:43
  543.9 9.5 %fusion = f32[1536]{0:T(1024)S(1)} fusion(f32[1536,3072]{1,0:T(8,128)} %get-tuple-element.9, f32[1536]{0:T(1024)S(1)} %get-tuple-element.5), kind=kLoop, calls=%fused_computation.5 | loop fusion | flops 14154240 | bytes 18886656 | tf_op jit(solution)/shard_map/reduce_sum | solution.py:36
  553.4 23.8 %all-reduce = (f32[1536]{0:T(1024)S(1)}, f32[1536]{0:T(1024)S(1)}) all-reduce(f32[1536]{0:T(1024)S(1)} %convolution_reduce_fusion, f32[1536]{0:T(1024)S(1)} %fusion), channel_id=1, replica_groups=mesh['clip'=16,'cap'=8] {'cap'}, use_global_device_ids=true, to_apply=%region_11.0 | all-reduce | flops 3072 | bytes 24576 | tf_op jit(solution)/shard_map/psum | solution.py:43
  577.3 0.0 copy-start.1
  577.3 16.3 %subtract_convert_fusion = bf16[1536,3072]{1,0:T(8,128)(2,1)S(1)} fusion(f32[1536,3072]{1,0:T(8,128)} %get-tuple-element.9, f32[3072]{0:T(1024)S(1)} %broadcast_divide_fusion, f32[1536]{0:T(1024)S(1)} %broadcast_divide_fusion.5, f32[1536]{0:T(1024)S(1)} %get-tuple-element.3, f32[1536]{0:T(1024)S(1)} %get-tuple-element.5, f32[1536]{0:T(1024)S(1)} %get-tuple-element.4, ...), kind=kLoop, calls=%fused_computation | loop fusion | flops 42467328 | bytes 47222784 | tf_op jit(solution)/shard_map/convert_element_type | solution.py:47
  593.6 0.0 copy-start
  593.6 3.6 copy-done
  597.3 0.0 copy-done.1
  597.3 0.0 copy-start.2
  597.3 6.8 convolution_multiply_fusion.1
  604.1 0.0 reduce-scatter.3.cloned.1.call-update
  604.1 0.0 reduce-scatter.5.cloned.1.call-start
  604.2 0.0 copy-done.2
  604.2 11.3 %convolution_multiply_fusion = f32[3072,512]{1,0:T(8,128)} fusion(bf16[1536,3072]{1,0:T(8,128)(2,1)} %copy-done, bf16[1536,512]{1,0:T(8,128)(2,1)S(1)} %copy-done.2), kind=kOutput, calls=%fused_computation.6 | convolution fusion | flops 4833411072 | bytes 17301504 | tf_op jit(solution)/shard_map/dot_general | solution.py:16
  615.5 0.0 reduce-scatter.5.cloned.1.call-update
  615.5 18.1 %reduce-scatter.3.cloned.1.call-done = f32[192,512]{1,0:T(8,128)} async-done(((f32[1536,512]{1,0:T(8,128)}), f32[192,512]{1,0:T(8,128)}) %reduce-scatter.3.cloned.1.call-update) | async-done | bytes 393232 | tf_op jit(solution)/shard_map/reduce_scatter | solution.py:48
  633.6 83.8 %reduce-scatter.5.cloned.1.call-done = f32[192,512]{1,0:T(8,128)} async-done(((f32[3072,512]{1,0:T(8,128)}), f32[192,512]{1,0:T(8,128)}) %reduce-scatter.5.cloned.1.call-update) | async-done | bytes 393232 | tf_op jit(solution)/shard_map/reduce_scatter | solution.py:54
  (8 shorter events, 0.0 us)
Async XLA Ops:
  7.2 29.6 %all-gather.9.cloned.1.call-start = ((), (), s32[]{:S(2)}) async-start(), calls=%async_computation.4 | async-start | bytes 1769472 | tf_op jit(solution)/shard_map/all_gather | solution.py:23
  7.9 78.9 %all-gather.11.cloned.1.call-start = ((), (), s32[]{:S(2)}) async-start(), calls=%async_computation.5 | async-start | bytes 3342336 | tf_op jit(solution)/shard_map/all_gather | solution.py:27
  8.6 103.3 %all-gather.5.cloned.1.call-start = ((), (), s32[]{:S(2)}) async-start(), calls=%async_computation.2 | async-start | bytes 1769472 | tf_op jit(solution)/shard_map/all_gather | solution.py:24
  9.4 152.5 %all-gather.7.cloned.1.call-start = ((), (), s32[]{:S(2)}) async-start(), calls=%async_computation.3 | async-start | bytes 3342336 | tf_op jit(solution)/shard_map/all_gather | solution.py:28
  10.0 623.6 %reduce-scatter.3.cloned.1.call-start = ((), (), s32[]{:S(2)}) async-start(), calls=%async_computation.6 | async-start | bytes 3538944 | tf_op jit(solution)/shard_map/reduce_scatter | solution.py:48
  577.3 20.0 %copy-start.1 = (bf16[3072,512]{1,0:T(8,128)(2,1)S(1)}, bf16[3072,512]{1,0:T(8,128)(2,1)}, u32[]{:S(2)}) copy-start(bf16[3072,512]{1,0:T(8,128)(2,1)} %all-gather.7.cloned.1.call-done) | copy-start | bytes 9437188
  593.6 3.6 copy-start
  597.3 6.9 copy-start.2
  604.1 113.3 %reduce-scatter.5.cloned.1.call-start = ((), (), s32[]{:S(2)}) async-start(), calls=%async_computation.7 | async-start | bytes 6684672 | tf_op jit(solution)/shard_map/reduce_scatter | solution.py:54
Sparse Core Ops, SparseCore 0:
  9.7 26.9 all-gather.8
  38.8 47.8 all-gather.10
  88.4 23.4 all-gather.4
  114.0 47.8 all-gather.6
  604.2 29.2 reduce-scatter.2
  637.4 79.9 reduce-scatter.4
where the time goes:
time: 731 us; the launch traced here: 725 us
  blocking collectives  287 us (39%)
  waiting for transfers between devices  245 us (34%)
  matrix products  148 us (20%)
  other arithmetic  25.9 us (4%)
  between operations  14.6 us (2%)
    psum x3, blocking collectives, body(): lax.psum(jnp.dot(weights_row, kernel, precision=lax.Precision.HIGHEST), '...  212 us
    reduce_scatter x1, waiting for transfers between devices, body(): lax.psum_scatter(10.0 * contract_first(residual, audio_student), 'clip',...  83.8 us
    dot_general x3, matrix products, body(): jnp.dot(kernel, column_scale, precision=lax.Precision.HIGHEST)  64.5 us
    all_gather x1, waiting for transfers between devices, body(): lax.all_gather(teacher_text, 'clip', axis=0, tiled=True)  50 us
    all_gather x1, waiting for transfers between devices, body(): lax.all_gather(student_text, 'clip', axis=0, tiled=True)  49.9 us
    psum x3, blocking collectives, body(): lax.psum(jnp.dot(kernel, column_scale, precision=lax.Precision.HIGHEST),...  49.2 us
    dot_general x3, matrix products, body(): jnp.dot(weights_row, kernel, precision=lax.Precision.HIGHEST)  43.5 us
    all_gather x1, waiting for transfers between devices, body(): lax.all_gather(teacher_audio, 'cap', axis=0, tiled=True)  26.7 us
  transfers between devices with their start and end apart: 6, of which 6 were waited for; matrix products, arithmetic and copies ran while one was open for 3% of the time, Pallas kernels for 0%

commit v1 on v0

v1 whole, which is shorter than its diff:
```python
import functools

import jax
import jax.numpy as jnp
from jax import lax
from jax.experimental import pallas as pl
from jax.experimental.pallas import tpu as pltpu
from jax.sharding import PartitionSpec as P

ITERS = 3
LANES = 128
VMEM = pl.BlockSpec(memory_space=pltpu.VMEM)
LIMIT = 8 * 1024 * 1024


def params(limit=LIMIT):
    return pltpu.CompilerParams(vmem_limit_bytes=limit)


def lanes_of(ref, block):
    return ref[pl.ds(block * LANES, LANES), :].T


def spread_rows(vec, ref):
    for block in range(vec.shape[0]):
        row = jnp.broadcast_to(vec[block : block + 1, :], (LANES, LANES))
        ref[pl.ds(block * LANES, LANES), :] = row.T


def spread_cols(vec):
    return jnp.concatenate(
        [jnp.broadcast_to(vec[g : g + 1, :], (8, LANES)) for g in range(vec.shape[0])], axis=1
    )


def repeat_lanes(col, groups):
    return jnp.concatenate([col] * groups, axis=1)


def fold_lanes(x, op):
    parts = [x[:, g * LANES : (g + 1) * LANES] for g in range(x.shape[1] // LANES)]
    while len(parts) > 1:
        parts = [op(*parts[k : k + 2]) if k + 1 < len(parts) else parts[k] for k in range(0, len(parts), 2)]
    return parts[0]


def logits_kernel(audio_ref, text_ref, logits_ref, max_ref, part_ref):
    rows, columns = logits_ref.shape
    step, width = 256, 512

    def block(i, _):
        base = pl.multiple_of(i * step, step)
        left = audio_ref[pl.ds(base, step), :]
        best = None
        for j in range(columns // width):
            x = 10.0 * lax.dot_general(
                left,
                text_ref[pl.ds(j * width, width), :],
                (((1,), (1,)), ((), ())),
                preferred_element_type=jnp.float32,
            )
            logits_ref[pl.ds(base, step), pl.ds(j * width, width)] = x
            folded = fold_lanes(x, jnp.maximum)
            best = folded if best is None else jnp.maximum(best, folded)
        part_ref[pl.ds(base, step), :] = best
        return 0

    lax.fori_loop(0, rows // step, block, 0)
    for b in range(rows // LANES):
        top = jnp.max(lanes_of(part_ref, b), axis=0, keepdims=True)
        for k in range(max_ref.shape[0]):
            max_ref[k, b : b + 1, :] = top


def teacher_logits(audio, text, peers):
    rows, columns = audio.shape[0], text.shape[0]
    return pl.pallas_call(
        logits_kernel,
        out_shape=(
            pltpu.VMEM((rows, columns), jnp.float32),
            jax.ShapeDtypeStruct((peers, rows // LANES, LANES), jnp.float32),
        ),
        in_specs=[VMEM, VMEM],
        out_specs=(VMEM, VMEM),
        scratch_shapes=[pltpu.VMEM((rows, LANES), jnp.float32)],
        compiler_params=params(),
        name="logits",
    )(audio, text)


def put_columns(acc, sum_ref, out_ref):
    groups = sum_ref.shape[0]
    for g in range(groups):
        sum_ref[g : g + 1, :] = jnp.sum(acc[:, g * LANES : (g + 1) * LANES], axis=0, keepdims=True)
    total = sum_ref[...]
    for k in range(out_ref.shape[0]):
        out_ref[k] = total


def exp_kernel(max_ref, logits_ref, kernel_ref, out_ref, col_ref, sum_ref):
    rows, columns = logits_ref.shape
    spread_rows(jnp.max(max_ref[...], axis=0), col_ref)

    def step(i, acc):
        at = pl.ds(pl.multiple_of(i * 8, 8), 8)
        k = jnp.exp(logits_ref[at, :] - repeat_lanes(col_ref[at, :], columns // LANES))
        kernel_ref[at, :] = k
        return acc + k

    acc = lax.fori_loop(0, rows // 8, step, jnp.zeros((8, columns), jnp.float32), unroll=4)
    put_columns(acc, sum_ref, out_ref)


def exp_columns(maxima, logits, peers):
    rows, columns = logits.shape
    return pl.pallas_call(
        exp_kernel,
        out_shape=(
            pltpu.VMEM((rows, columns), jnp.float32),
            jax.ShapeDtypeStruct((peers, columns // LANES, LANES), jnp.float32),
        ),
        in_specs=[VMEM, VMEM],
        out_specs=(VMEM, VMEM),
        scratch_shapes=[
            pltpu.VMEM((rows, LANES), jnp.float32),
            pltpu.VMEM((columns // LANES, LANES), jnp.float32),
        ],
        input_output_aliases={1: 0},
        compiler_params=params(),
        name="exp_columns",
    )(maxima, resident(logits))


def row_kernel(*refs):
    parts_ref, kernel_ref = refs[:2]
    stat_ref = refs[2] if len(refs) == 6 else None
    out_ref, scale_ref, part_ref = refs[-3:]
    rows, columns = kernel_ref.shape
    blocks = rows // LANES
    scale_ref[...] = 1.0 / jnp.sum(parts_ref[...], axis=0)
    scale = spread_cols(scale_ref[...])

    def step(i, _):
        at = pl.ds(pl.multiple_of(i * 8, 8), 8)
        part_ref[at, :] = fold_lanes(kernel_ref[at, :] * scale, jnp.add)
        return 0

    lax.fori_loop(0, rows // 8, step, 0, unroll=4)
    for b in range(blocks):
        total = jnp.sum(lanes_of(part_ref, b), axis=0, keepdims=True)
        for k in range(out_ref.shape[0]):
            out_ref[k, b : b + 1, :] = total
    if stat_ref is not None:
        for k in range(out_ref.shape[0]):
            out_ref[k, blocks:, :] = stat_ref[...]


def row_sums(parts, kernel, peers, stats=None):
    rows, columns = kernel.shape
    extra = () if stats is None else (stats,)
    return pl.pallas_call(
        row_kernel,
        out_shape=(
            jax.ShapeDtypeStruct((peers, rows // LANES * (3 if extra else 1), LANES), jnp.float32),
            jax.ShapeDtypeStruct((columns // LANES, LANES), jnp.float32),
        ),
        in_specs=[VMEM, VMEM] + [VMEM] * len(extra),
        out_specs=(VMEM, VMEM),
        scratch_shapes=[pltpu.VMEM((rows, LANES), jnp.float32)],
        compiler_params=params(),
        name="row_sums",
    )(parts, resident(kernel), *extra)


def column_kernel(parts_ref, kernel_ref, out_ref, col_ref, sum_ref):
    rows, columns = kernel_ref.shape
    spread_rows(1.0 / jnp.sum(parts_ref[...], axis=0), col_ref)

    def step(i, acc):
        at = pl.ds(pl.multiple_of(i * 8, 8), 8)
        return acc + kernel_ref[at, :] * repeat_lanes(col_ref[at, :], columns // LANES)

    acc = lax.fori_loop(0, rows // 8, step, jnp.zeros((8, columns), jnp.float32), unroll=4)
    put_columns(acc, sum_ref, out_ref)


def column_sums(parts, kernel, peers):
    rows, columns = kernel.shape
    return pl.pallas_call(
        column_kernel,
        out_shape=jax.ShapeDtypeStruct((peers, columns // LANES, LANES), jnp.float32),
        in_specs=[VMEM, VMEM],
        out_specs=VMEM,
        scratch_shapes=[
            pltpu.VMEM((rows, LANES), jnp.float32),
            pltpu.VMEM((columns // LANES, LANES), jnp.float32),
        ],
        compiler_params=params(),
        name="column_sums",
    )(parts, resident(kernel))


def student_kernel(audio_ref, text_ref, exp_ref, stat_ref, part_ref):
    step, columns = exp_ref.shape
    width = 512
    here = step // LANES
    blocks = stat_ref.shape[0] // 2
    i = pl.program_id(0)
    best = None
    for j in range(columns // width):
        x = 10.0 * lax.dot_general(
            audio_ref[...],
            text_ref[pl.ds(j * width, width), :],
            (((1,), (1,)), ((), ())),
            preferred_element_type=jnp.float32,
        )
        exp_ref[:, pl.ds(j * width, width)] = x
        folded = fold_lanes(x, jnp.maximum)
        best = folded if best is None else jnp.maximum(best, folded)
    part_ref[...] = best
    for b in range(here):
        top = jnp.max(lanes_of(part_ref, b), axis=0, keepdims=True)
        stat_ref[pl.ds(i * here + b, 1), :] = top
        part_ref[pl.ds(b * LANES, LANES), :] = jnp.broadcast_to(top, (LANES, LANES)).T

    def exps(r, _):
        at = pl.ds(pl.multiple_of(r * 8, 8), 8)
        e = jnp.exp(exp_ref[at, :] - repeat_lanes(part_ref[at, :], columns // LANES))
        exp_ref[at, :] = e
        part_ref[at, :] = fold_lanes(e, jnp.add)
        return 0

    lax.fori_loop(0, step // 8, exps, 0, unroll=4)
    for b in range(here):
        total = jnp.sum(lanes_of(part_ref, b), axis=0, keepdims=True)
        stat_ref[pl.ds(blocks + i * here + b, 1), :] = total


def student_softmax(audio, text):
    rows, columns, depth = audio.shape[0], text.shape[0], audio.shape[1]
    step = 256
    return pl.pallas_call(
        student_kernel,
        grid=(rows // step,),
        out_shape=(
            jax.ShapeDtypeStruct((rows, columns), jnp.float32),
            jax.ShapeDtypeStruct((2 * (rows // LANES), LANES), jnp.float32),
        ),
        in_specs=[
            pl.BlockSpec((step, depth), lambda i: (i, 0)),
            pl.BlockSpec((columns, depth), lambda i: (0, 0), pipeline_mode=pl.Buffered(1)),
        ],
        out_specs=(
            pl.BlockSpec((step, columns), lambda i: (i, 0)),
            pl.BlockSpec((2 * (rows // LANES), LANES), lambda i: (0, 0)),
        ),
        scratch_shapes=[pltpu.VMEM((step, LANES), jnp.float32)],
        compiler_params=params(16 * 1024 * 1024),
        cost_estimate=pl.CostEstimate(
            flops=2 * rows * columns * depth, bytes_accessed=4 * rows * columns, transcendentals=rows * columns
        ),
        name="student_softmax",
    )(audio, text)


def residual_kernel(
    rows_ref, scale_ref, own_ref, kernel_ref, exp_ref, audio_ref, text_ref,
    audio_out_ref, text_out_ref, weight_ref, prob_ref, residual_ref, acc_ref,
):
    step, columns = exp_ref.shape
    blocks = own_ref.shape[0] // 2
    i = pl.program_id(0)

    @pl.when(i == 0)
    def _():
        spread_rows(1.0 / jnp.sum(rows_ref[:, :blocks, :], axis=0), weight_ref)
        tops = rows_ref[:, blocks : 2 * blocks, :]
        top = jnp.max(tops, axis=0)
        total = jnp.sum(jnp.exp(tops - top[None]) * rows_ref[:, 2 * blocks :, :], axis=0)
        spread_rows(jnp.exp(own_ref[:blocks, :] - top) / total, prob_ref)

        def clear(k, _):
            acc_ref[pl.ds(pl.multiple_of(k * 64, 64), 64), :] = jnp.zeros((64, acc_ref.shape[1]), jnp.float32)
            return 0

        lax.fori_loop(0, columns // 64, clear, 0)

    scale = spread_cols(scale_ref[...])

    def part(j, _):
        out = []
        for half in range(2):
            off = pl.multiple_of(j * 16 + half * 8, 8)
            at = pl.ds(off, 8)
            whole = pl.ds(pl.multiple_of(i * step + off, 8), 8)
            weight = repeat_lanes(weight_ref[whole, :], columns // LANES)
            prob = repeat_lanes(prob_ref[whole, :], columns // LANES)
            out.append(exp_ref[at, :] * prob - (weight * kernel_ref[whole, :]) * scale)
        residual_ref[pl.ds(pl.multiple_of(j * 16, 16), 16), :] = jnp.concatenate(out, axis=0).astype(jnp.bfloat16)
        return 0

    lax.fori_loop(0, step // 16, part, 0)
    for j in range(columns // 512):
        acc_ref[pl.ds(j * 512, 512), :] += lax.dot_general(
            residual_ref[:, pl.ds(j * 512, 512)],
            audio_ref[...],
            (((0,), (0,)), ((), ())),
            preferred_element_type=jnp.float32,
        )
    audio_out_ref[...] = 10.0 * jnp.dot(residual_ref[...], text_ref[...], preferred_element_type=jnp.float32)

    @pl.when(i == pl.num_programs(0) - 1)
    def _():
        def finish(k, _):
            at = pl.ds(pl.multiple_of(k * 64, 64), 64)
            text_out_ref[at, :] = (10.0 * acc_ref[at, :]).astype(text_out_ref.dtype)
            return 0

        lax.fori_loop(0, columns // 64, finish, 0)


def residual_grads(row_parts, scale, own, kernel, exps, audio, text, dtype):
    rows, columns = kernel.shape
    depth = audio.shape[1]
    step = 256
    return pl.pallas_call(
        residual_kernel,
        grid=(rows // step,),
        out_shape=(
            jax.ShapeDtypeStruct((rows, depth), jnp.float32),
            jax.ShapeDtypeStruct((columns, depth), dtype),
        ),
        in_specs=[VMEM] * 4
        + [
            pl.BlockSpec((step, columns), lambda i: (i, 0)),
            pl.BlockSpec((step, depth), lambda i: (i, 0)),
            pl.BlockSpec((columns, depth), lambda i: (0, 0), pipeline_mode=pl.Buffered(1)),
        ],
        out_specs=(
            pl.BlockSpec((step, depth), lambda i: (i, 0)),
            pl.BlockSpec((columns, depth), lambda i: (0, 0)),
        ),
        scratch_shapes=[
            pltpu.VMEM((rows, LANES), jnp.float32),
            pltpu.VMEM((rows, LANES), jnp.float32),
            pltpu.VMEM((step, columns), jnp.bfloat16),
            pltpu.VMEM((columns, depth), jnp.float32),
        ],
        compiler_params=params(36 * 1024 * 1024),
        name="residual_grads",
    )(row_parts, scale, own, resident(kernel), exps, audio, text)


def resident(x):
    return pltpu.with_memory_space_constraint(x, pltpu.VMEM)


def gather_a2a(x, axis, n):
    spread = jnp.broadcast_to(x[None], (n, *x.shape))
    return lax.all_to_all(spread, axis, 0, 0).reshape(n * x.shape[0], x.shape[1])


def swap(x, axis):
    return lax.all_to_all(x, axis, 0, 0)


def body(clips, caps, teacher_audio, teacher_text, student_audio, student_text):
    audio_t = lax.all_gather(teacher_audio, "cap", axis=0, tiled=True)
    text_t = gather_a2a(teacher_text, "clip", clips)
    text_s = lax.all_gather(student_text, "clip", axis=0, tiled=True)
    audio_s = lax.all_gather(student_audio, "cap", axis=0, tiled=True)
    logits, maxima = teacher_logits(audio_t, text_t, caps)
    kernel, columns = exp_columns(swap(maxima, "cap"), logits, clips)
    stats = None
    for sweep_index in range(ITERS):
        last = sweep_index + 1 == ITERS
        if last:
            exps, stats = student_softmax(audio_s, text_s)
        row_parts, scale = row_sums(swap(columns, "clip"), kernel, caps, stats)
        row_parts = swap(row_parts, "cap")
        if not last:
            columns = column_sums(row_parts, kernel, clips)
    audio_part, text_part = residual_grads(row_parts, scale, stats, kernel, exps, audio_s, text_s, jnp.bfloat16)
    audio_grad = lax.psum_scatter(audio_part, "cap", scatter_dimension=0, tiled=True)
    text_parts = swap(text_part.reshape(clips, -1, text_part.shape[1]), "clip")
    text_grad = jnp.sum(text_parts.astype(jnp.float32), axis=0)
    return audio_grad, text_grad


def solution(mesh):
    placed = (
        P(("clip", "cap"), None),
        P(("cap", "clip"), None),
        P(("clip", "cap"), None),
        P(("cap", "clip"), None),
    )
    return jax.shard_map(
        functools.partial(body, mesh.shape["clip"], mesh.shape["cap"]),
        mesh=mesh,
        in_specs=placed,
        out_specs=(P(("clip", "cap"), None), P(("cap", "clip"), None)),
        check_vma=False,
    )
```

time: 731 us -> 263 us (0.36)
  waiting for transfers between devices: 245 us -> 49.6 us
  blocking collectives: 287 us -> 109 us
  matrix products: 148 us -> 0 us
  Pallas kernels: 0 us -> 56 us
  other arithmetic: 25.9 us -> 1.18 us
  local copies, waits for them, and re-layouts: 3.64 us -> 22.2 us
  starting transfers between devices: 0.23 us -> 10.8 us
    psum x6 -> x0, blocking collectives: 261 us -> none  [the longest x3 212 us: body(): lax.psum(jnp.dot(weights_row, kernel, precision=lax.Precision.HIGHEST), '...]
    dot_general x10 -> x0, matrix products: 148 us -> none  [the longest x3 64.5 us: body(): jnp.dot(kernel, column_scale, precision=lax.Precision.HIGHEST)]
    all_gather x4 -> x3, waiting for transfers between devices: 141 us -> 17.6 us  [the longest x1 17.5 us: body(): audio_t = lax.all_gather(teacher_audio, 'cap', axis=0, tiled=True)]
    all_to_all x0 -> x7, blocking collectives: none -> 109 us  [swap(): return lax.all_to_all(x, axis, 0, 0)]
    reduce_scatter x2 -> x1, waiting for transfers between devices: 102 us -> 0.01 us  [body(): lax.psum_scatter(audio_part, 'cap', scatter_dimension=0, tiled=True)]
    pallas_call x0 -> x9, Pallas kernels: none -> 56 us  [the longest x1 21.7 us: residual_grads(): pl.pallas_call(residual_kernel, grid=(rows // step,), out_shape=(jax.Shap...]
    all_to_all x0 -> x2, waiting for transfers between devices: none -> 30 us  [the longest x1 30 us: gather_a2a(): lax.all_to_all(spread, axis, 0, 0).reshape(n * x.shape[0], x.shape[1])]
    pmax x1 -> x0, blocking collectives: 25.5 us -> none  [body(): lax.pmax((jnp.max(teacher_logits, axis=1), jnp.max(student_logits, axis=1...]
  transfers between devices with their start and end apart: 6 -> 6, of which waited for: 6 -> 2; matrix products, arithmetic and copies ran while one was open for 3% -> 2% of each run, Pallas kernels for 0% -> 12%
where the time goes in v1:
time: 263 us; the launch traced here: 262 us
  blocking collectives  109 us (41%)
  Pallas kernels  56 us (21%)
  waiting for transfers between devices  49.6 us (19%)
  local copies, waits for them, and re-layouts  22.2 us (8%)
  between operations  13.9 us (5%)
  starting transfers between devices  10.8 us (4%)
    all_to_all x7, blocking collectives, swap(): return lax.all_to_all(x, axis, 0, 0)  109 us
    all_to_all x1, waiting for transfers between devices, gather_a2a(): lax.all_to_all(spread, axis, 0, 0).reshape(n * x.shape[0], x.shape[1])  30 us
    pallas_call x1, Pallas kernels, residual_grads(): pl.pallas_call(residual_kernel, grid=(rows // step,), out_shape=(jax.Shap...  21.7 us
    unnamed x20, local copies, waits for them, and re-layouts  19.4 us
    all_gather x1, waiting for transfers between devices, body(): audio_t = lax.all_gather(teacher_audio, 'cap', axis=0, tiled=True)  17.5 us
    pallas_call x1, Pallas kernels, student_softmax(): pl.pallas_call(student_kernel, grid=(rows // step,), out_shape=(jax.Shape...  12.6 us
    all_to_all x1, starting transfers between devices, gather_a2a(): lax.all_to_all(spread, axis, 0, 0).reshape(n * x.shape[0], x.shape[1])  7.12 us
    pallas_call x1, Pallas kernels, teacher_logits(): pl.pallas_call(logits_kernel, out_shape=(pltpu.VMEM((rows, columns), jnp....  6.39 us
  transfers between devices with their start and end apart: 6, of which 2 were waited for; matrix products, arithmetic and copies ran while one was open for 2% of the time, Pallas kernels for 12%

profile of v1, /device:TPU:0, one launch (start us, length us, event | category | flops | bytes accessed | tf_op | source)
XLA Modules:
  0.0 262.2 jit_solution(2110258026492882094)
XLA Ops:
  7.2 0.0 all-gather.4.cloned.1.call-start
  7.2 0.7 all-gather.4.cloned.1.call-update
  7.9 0.0 all-gather.6.cloned.1.call-start
  7.9 0.7 all-gather.6.cloned.1.call-update
  8.6 0.0 all-gather.8.cloned.1.call-start
  8.7 0.7 all-gather.8.cloned.1.call-update
  9.4 2.9 %broadcast_in_dim.2 = bf16[16,192,512]{2,1,0:T(8,128)(2,1)} broadcast(bf16[192,512]{1,0:T(8,128)(2,1)} %param.5), dimensions={1,2} | broadcast | bytes 3342336 | tf_op jit(solution)/shard_map/broadcast_in_dim | solution.py:359
  12.2 7.1 %all-to-all-start = ((bf16[16,192,512]{2,1,0:T(8,128)(2,1)}), bf16[16,192,512]{2,1,0:T(8,128)(2,1)S(1)}, u32[]{:S(2)}, u32[]{:S(2)}) async-start(bf16[16,192,512]{2,1,0:T(8,128)(2,1)} %broadcast_in_dim.2), calls=%async_computation | async-start | bytes 6291456 | tf_op jit(solution)/shard_map/all_to_all | solution.py:360
  19.4 17.5 %all-gather.4.cloned.1.call-done.audio_ref = bf16[1536,512]{1,0:T(8,128)(2,1)} async-done(((bf16[192,512]{1,0:T(8,128)(2,1)}), bf16[1536,512]{1,0:T(8,128)(2,1)}) %all-gather.4.cloned.1.call-update) | async-done | bytes 1572880 | tf_op jit(solution)/shard_map/all_gather | solution.py:368
  36.9 30.0 %all-to-all-done = bf16[16,192,512]{2,1,0:T(8,128)(2,1)S(1)} async-done(((bf16[16,192,512]{2,1,0:T(8,128)(2,1)}), bf16[16,192,512]{2,1,0:T(8,128)(2,1)S(1)}, u32[]{:S(2)}, u32[]{:S(2)}) %all-to-all-start) | async-done | bytes 3145760 | tf_op jit(solution)/shard_map/all_to_all | solution.py:360
  66.9 1.4 copy-done.6
  68.3 6.4 %logits.1 = (f32[1536,3072]{1,0:T(8,128)S(1)}, f32[8,12,128]{2,1,0:T(8,128)S(1)}) custom-call(bf16[1536,512]{1,0:T(8,128)(2,1)S(1)} %copy-done.6, bf16[3072,512]{1,0:T(8,128)(2,1)S(1)} %bitcast.2), custom_call_target="tpu_custom_call" | custom-call | tf_op jit(solution)/shard_map/logits/pallas_call | solution.py:77
  74.7 10.7 %all_to_all.45.max_ref = f32[8,12,128]{2,1,0:T(8,128)S(1)} all-to-all(f32[8,12,128]{2,1,0:T(8,128)S(1)} %get-tuple-element.14), channel_id=1, replica_groups=mesh['clip'=16,'cap'=8] {'cap'}, dimensions={0} | all-to-all | bytes 98304 | tf_op jit(solution)/shard_map/all_to_all | solution.py:364
  85.4 4.6 %exp_columns.1 = (f32[1536,3072]{1,0:T(8,128)S(1)}, f32[16,24,128]{2,1,0:T(8,128)S(1)}) custom-call(f32[8,12,128]{2,1,0:T(8,128)S(1)} %all_to_all.45.max_ref, f32[1536,3072]{1,0:T(8,128)S(1)} %get-tuple-element.15.logits_ref), custom_call_target="tpu_custom_call", output_to_operand_aliasing={{0}: (1, {})} | custom-call | tf_op jit(solution)/shard_map/exp_columns/pallas_call | solution.py:116
  90.1 0.0 copy-start
  90.1 14.4 %all_to_all.46.refs_0_ = f32[16,24,128]{2,1,0:T(8,128)S(1)} all-to-all(f32[16,24,128]{2,1,0:T(8,128)S(1)} %get-tuple-element.16), channel_id=1, replica_groups=mesh['clip'=16,'cap'=8] {'clip'}, dimensions={0} | all-to-all | bytes 393216 | tf_op jit(solution)/shard_map/all_to_all | solution.py:364
  104.5 2.1 row_sums.3
  106.7 8.0 %all_to_all.47.parts_ref = f32[8,12,128]{2,1,0:T(8,128)S(1)} all-to-all(f32[8,12,128]{2,1,0:T(8,128)S(1)} %get-tuple-element.18), channel_id=1, replica_groups=mesh['clip'=16,'cap'=8] {'cap'}, dimensions={0} | all-to-all | bytes 98304 | tf_op jit(solution)/shard_map/all_to_all | solution.py:364
  114.6 2.0 column_sums.2
  116.6 11.0 %all_to_all.48.refs_0_ = f32[16,24,128]{2,1,0:T(8,128)S(1)} all-to-all(f32[16,24,128]{2,1,0:T(8,128)S(1)} %column_sums.2), channel_id=1, replica_groups=mesh['clip'=16,'cap'=8] {'clip'}, dimensions={0} | all-to-all | bytes 393216 | tf_op jit(solution)/shard_map/all_to_all | solution.py:364
  127.6 2.1 row_sums.4
  129.7 8.0 %all_to_all.49.parts_ref = f32[8,12,128]{2,1,0:T(8,128)S(1)} all-to-all(f32[8,12,128]{2,1,0:T(8,128)S(1)} %get-tuple-element.19), channel_id=1, replica_groups=mesh['clip'=16,'cap'=8] {'cap'}, dimensions={0} | all-to-all | bytes 98304 | tf_op jit(solution)/shard_map/all_to_all | solution.py:364
  137.7 0.0 copy-done
  137.7 2.7 %column_sums.3 = f32[16,24,128]{2,1,0:T(8,128)} custom-call(f32[8,12,128]{2,1,0:T(8,128)S(1)} %all_to_all.49.parts_ref, f32[1536,3072]{1,0:T(8,128)S(1)} %get-tuple-element.17.refs_1_.kernel_ref), custom_call_target="tpu_custom_call" | custom-call | tf_op jit(solution)/shard_map/column_sums/pallas_call | solution.py:189
  140.4 3.5 %all-to-all-start.6 = ((f32[16,24,128]{2,1,0:T(8,128)}), f32[16,24,128]{2,1,0:T(8,128)S(1)}, u32[]{:S(2)}, u32[]{:S(2)}) async-start(f32[16,24,128]{2,1,0:T(8,128)} %column_sums.3), calls=%async_computation.6 | async-start | bytes 393216 | tf_op jit(solution)/shard_map/all_to_all | solution.py:364
  143.9 0.0 reduce-scatter.2.cloned.1.call-start
  144.0 0.0 all-gather.6.cloned.1.call-done.audio_ref
  144.0 0.0 all-gather.8.cloned.1.call-done.text_ref
  144.0 0.0 copy-start.4
  144.0 1.9 copy-done.4
  145.9 0.0 copy-start.5
  145.9 1.4 copy-done.5
  147.3 12.6 %student_softmax.1 = (f32[1536,3072]{1,0:T(8,128)S(1)}, f32[24,128]{1,0:T(8,128)S(1)}) custom-call(bf16[1536,512]{1,0:T(8,128)(2,1)S(1)} %copy-done.5, bf16[3072,512]{1,0:T(8,128)(2,1)S(1)} %copy-done.4), custom_call_target="tpu_custom_call" | custom-call | flops 4831838208 | bytes 18874368 | tf_op jit(solution)/shard_map/student_softmax/pallas_call | solution.py:242
  159.9 0.0 copy-start.3
  159.9 6.4 %copy-done.3 = f32[1536,3072]{1,0:T(8,128)} copy-done((f32[1536,3072]{1,0:T(8,128)}, f32[1536,3072]{1,0:T(8,128)S(1)}, u32[]{:S(2)}) %copy-start.3) | copy-done | bytes 18874392
  166.3 0.0 all-to-all-done.6.refs_0_
  166.3 6.4 %copy-done.1 = f32[1536,3072]{1,0:T(8,128)S(1)} copy-done((f32[1536,3072]{1,0:T(8,128)S(1)}, f32[1536,3072]{1,0:T(8,128)}, u32[]{:S(2)}) %copy-start.1) | copy-done | bytes 18874392
  172.7 1.8 row_sums.5
  174.5 0.0 copy-done.7
  174.5 0.0 copy-start.8
  174.6 10.1 %all_to_all.50.rows_ref = f32[8,36,128]{2,1,0:T(8,128)} all-to-all(f32[8,36,128]{2,1,0:T(8,128)S(1)} %get-tuple-element.21), channel_id=1, replica_groups=mesh['clip'=16,'cap'=8] {'cap'}, dimensions={0} | all-to-all | bytes 294912 | tf_op jit(solution)/shard_map/all_to_all | solution.py:364
  184.6 0.0 copy-done.8
  184.6 0.0 copy-done.2
  184.6 21.7 %residual_grads.1 = (f32[1536,512]{1,0:T(8,128)}, bf16[3072,512]{1,0:T(8,128)(2,1)}) custom-call(f32[8,36,128]{2,1,0:T(8,128)} %all_to_all.50.rows_ref, f32[24,128]{1,0:T(8,128)} %copy-done.8, f32[24,128]{1,0:T(8,128)} %copy-done.7, f32[1536,3072]{1,0:T(8,128)S(1)} %copy-done.2, f32[1536,3072]{1,0:T(8,128)} %copy-done.3, ...), custom_call_target="tpu_custom_call" | custom-call | tf_op jit(solution)/shard_map/residual_grads/pallas_call | solution.py:326
  206.3 0.0 reduce-scatter.2.cloned.1.call-update
  206.3 1.9 copy-done.9
  208.2 46.3 %all_to_all.51 = bf16[16,192,512]{2,1,0:T(8,128)(2,1)S(1)} all-to-all(bf16[16,192,512]{2,1,0:T(8,128)(2,1)S(1)} %bitcast.3), channel_id=1, replica_groups=mesh['clip'=16,'cap'=8] {'clip'}, dimensions={0} | all-to-all | bytes 6291456 | tf_op jit(solution)/shard_map/all_to_all | solution.py:364
  254.5 1.2 convert_reduce_fusion
  (6 shorter events, 0.0 us)
Async XLA Ops:
  7.2 29.7 %all-gather.4.cloned.1.call-start = ((), (), s32[]{:S(2)}) async-start(), calls=%async_computation.10 | async-start | bytes 1769472 | tf_op jit(solution)/shard_map/all_gather | solution.py:368
  7.9 136.1 %all-gather.6.cloned.1.call-start = ((), (), s32[]{:S(2)}) async-start(), calls=%async_computation.11 | async-start | bytes 1769472 | tf_op jit(solution)/shard_map/all_gather | solution.py:371
  8.6 135.4 %all-gather.8.cloned.1.call-start = ((), (), s32[]{:S(2)}) async-start(), calls=%async_computation.12 | async-start | bytes 3342336 | tf_op jit(solution)/shard_map/all_gather | solution.py:370
  12.2 54.6 %all-to-all-start = ((bf16[16,192,512]{2,1,0:T(8,128)(2,1)}), bf16[16,192,512]{2,1,0:T(8,128)(2,1)S(1)}, u32[]{:S(2)}, u32[]{:S(2)}) async-start(bf16[16,192,512]{2,1,0:T(8,128)(2,1)} %broadcast_in_dim.2), calls=%async_computation | async-start | bytes 6291456 | tf_op jit(solution)/shard_map/all_to_all | solution.py:360
  66.9 1.4 copy-start.6
  90.1 47.7 %copy-start = (f32[1536,3072]{1,0:T(8,128)}, f32[1536,3072]{1,0:T(8,128)S(1)}, u32[]{:S(2)}) copy-start(f32[1536,3072]{1,0:T(8,128)S(1)} %get-tuple-element.17.refs_1_.kernel_ref) | copy-start | bytes 56623108
  140.4 26.0 %all-to-all-start.6 = ((f32[16,24,128]{2,1,0:T(8,128)}), f32[16,24,128]{2,1,0:T(8,128)S(1)}, u32[]{:S(2)}, u32[]{:S(2)}) async-start(f32[16,24,128]{2,1,0:T(8,128)} %column_sums.3), calls=%async_computation.6 | async-start | bytes 393216 | tf_op jit(solution)/shard_map/all_to_all | solution.py:364
  143.9 111.8 %reduce-scatter.2.cloned.1.call-start = ((), (), s32[]{:S(2)}) async-start(), calls=%async_computation.13 | async-start | bytes 3538944 | tf_op jit(solution)/shard_map/reduce_scatter | solution.py:384
  144.0 1.9 copy-start.4
  145.9 1.4 copy-start.5
  159.9 6.4 %copy-start.3 = (f32[1536,3072]{1,0:T(8,128)}, f32[1536,3072]{1,0:T(8,128)S(1)}, u32[]{:S(2)}) copy-start(f32[1536,3072]{1,0:T(8,128)S(1)} %get-tuple-element.23.exp_ref) | copy-start | bytes 56623108
  166.3 8.2 %copy-start.7 = (f32[24,128]{1,0:T(8,128)}, f32[24,128]{1,0:T(8,128)S(1)}, u32[]{:S(2)}) copy-start(f32[24,128]{1,0:T(8,128)S(1)} %get-tuple-element.20.refs_2_.own_ref) | copy-start | bytes 36868
  166.3 6.4 %copy-start.1 = (f32[1536,3072]{1,0:T(8,128)S(1)}, f32[1536,3072]{1,0:T(8,128)}, u32[]{:S(2)}) copy-start(f32[1536,3072]{1,0:T(8,128)} %copy-done) | copy-start | bytes 56623108
  172.7 11.9 %copy-start.2 = (f32[1536,3072]{1,0:T(8,128)S(1)}, f32[1536,3072]{1,0:T(8,128)}, u32[]{:S(2)}) copy-start(f32[1536,3072]{1,0:T(8,128)} %copy-done) | copy-start | bytes 56623108
  174.5 10.1 %copy-start.8 = (f32[24,128]{1,0:T(8,128)}, f32[24,128]{1,0:T(8,128)S(1)}, u32[]{:S(2)}) copy-start(f32[24,128]{1,0:T(8,128)S(1)} %get-tuple-element.22.scale_ref) | copy-start | bytes 36868
  206.3 1.9 copy-start.9
Sparse Core Ops, SparseCore 0:
  9.7 27.1 all-gather.3
  38.6 24.6 all-gather.5
  65.4 48.8 all-gather.7
  206.5 36.2 reduce-scatter.1

commit v2 on v1

v2 whole, which is shorter than its diff:
```python
import functools

import jax
import jax.numpy as jnp
from jax import lax
from jax.experimental import pallas as pl
from jax.experimental.pallas import tpu as pltpu
from jax.sharding import PartitionSpec as P

ITERS = 3
LANES = 128
WIDTH = 512
VMEM = pl.BlockSpec(memory_space=pltpu.VMEM)
LIMIT = 8 * 1024 * 1024


def params(limit=LIMIT):
    return pltpu.CompilerParams(vmem_limit_bytes=limit)


def lanes_of(ref, block):
    return ref[pl.ds(block * LANES, LANES), :].T


def spread_rows(vec, ref):
    for block in range(vec.shape[0]):
        row = jnp.broadcast_to(vec[block : block + 1, :], (LANES, LANES))
        ref[pl.ds(block * LANES, LANES), :] = row.T


def spread_cols(vec):
    return jnp.concatenate(
        [jnp.broadcast_to(vec[g : g + 1, :], (8, LANES)) for g in range(vec.shape[0])], axis=1
    )


def repeat_lanes(col, groups):
    return jnp.concatenate([col] * groups, axis=1)


def fold_lanes(x, op):
    parts = [x[:, g * LANES : (g + 1) * LANES] for g in range(x.shape[1] // LANES)]
    while len(parts) > 1:
        parts = [op(*parts[k : k + 2]) if k + 1 < len(parts) else parts[k] for k in range(0, len(parts), 2)]
    return parts[0]


def contract_last(left, right):
    return lax.dot_general(left, right, (((1,), (1,)), ((), ())), preferred_element_type=jnp.float32)


def logits_kernel(audio_ref, text_ref, logits_ref, max_ref, part_ref):
    rows, columns = logits_ref.shape
    step = 256

    def block(i, _):
        base = pl.multiple_of(i * step, step)
        left = audio_ref[pl.ds(base, step), :]
        best = None
        for j in range(columns // WIDTH):
            at = j * WIDTH
            x = 10.0 * contract_last(left, text_ref[pl.ds(at, WIDTH), :])
            logits_ref[pl.ds(base, step), pl.ds(at, WIDTH)] = x
            folded = fold_lanes(x, jnp.maximum)
            best = folded if best is None else jnp.maximum(best, folded)
        part_ref[pl.ds(base, step), :] = best
        return 0

    lax.fori_loop(0, rows // step, block, 0)
    for b in range(rows // LANES):
        top = jnp.max(lanes_of(part_ref, b), axis=0, keepdims=True)
        for k in range(max_ref.shape[0]):
            max_ref[k, b : b + 1, :] = top


def teacher_logits(audio, text, peers):
    rows, columns = audio.shape[0], text.shape[0]
    return pl.pallas_call(
        logits_kernel,
        out_shape=(
            pltpu.VMEM((rows, columns), jnp.float32),
            jax.ShapeDtypeStruct((peers, rows // LANES, LANES), jnp.float32),
        ),
        in_specs=[VMEM, VMEM],
        out_specs=(VMEM, VMEM),
        scratch_shapes=[pltpu.VMEM((rows, LANES), jnp.float32)],
        compiler_params=params(),
        name="logits",
    )(audio, text)


def put_columns(acc, sum_ref, out_ref):
    groups = sum_ref.shape[0]
    for g in range(groups):
        sum_ref[g : g + 1, :] = jnp.sum(acc[:, g * LANES : (g + 1) * LANES], axis=0, keepdims=True)
    total = sum_ref[...]
    for k in range(out_ref.shape[0]):
        out_ref[k] = total


def exp_kernel(max_ref, logits_ref, kernel_ref, out_ref, col_ref, sum_ref):
    rows, columns = logits_ref.shape
    spread_rows(jnp.max(max_ref[...], axis=0), col_ref)

    def step(i, acc):
        at = pl.ds(pl.multiple_of(i * 8, 8), 8)
        k = jnp.exp(logits_ref[at, :] - repeat_lanes(col_ref[at, :], columns // LANES))
        kernel_ref[at, :] = k
        return acc + k

    acc = lax.fori_loop(0, rows // 8, step, jnp.zeros((8, columns), jnp.float32), unroll=4)
    put_columns(acc, sum_ref, out_ref)


def exp_columns(maxima, logits, peers):
    rows, columns = logits.shape
    return pl.pallas_call(
        exp_kernel,
        out_shape=(
            pltpu.VMEM((rows, columns), jnp.float32),
            jax.ShapeDtypeStruct((peers, columns // LANES, LANES), jnp.float32),
        ),
        in_specs=[VMEM, VMEM],
        out_specs=(VMEM, VMEM),
        scratch_shapes=[
            pltpu.VMEM((rows, LANES), jnp.float32),
            pltpu.VMEM((columns // LANES, LANES), jnp.float32),
        ],
        input_output_aliases={1: 0},
        compiler_params=params(),
        name="exp_columns",
    )(maxima, resident(logits))


def row_kernel(parts_ref, kernel_ref, out_ref, part_ref):
    rows = kernel_ref.shape[0]
    scale = spread_cols(1.0 / jnp.sum(parts_ref[...], axis=0))

    def step(i, _):
        at = pl.ds(pl.multiple_of(i * 8, 8), 8)
        part_ref[at, :] = fold_lanes(kernel_ref[at, :] * scale, jnp.add)
        return 0

    lax.fori_loop(0, rows // 8, step, 0, unroll=4)
    for b in range(rows // LANES):
        total = jnp.sum(lanes_of(part_ref, b), axis=0, keepdims=True)
        for k in range(out_ref.shape[0]):
            out_ref[k, b : b + 1, :] = total


def row_sums(parts, kernel, peers):
    rows = kernel.shape[0]
    return pl.pallas_call(
        row_kernel,
        out_shape=jax.ShapeDtypeStruct((peers, rows // LANES, LANES), jnp.float32),
        in_specs=[VMEM, VMEM],
        out_specs=VMEM,
        scratch_shapes=[pltpu.VMEM((rows, LANES), jnp.float32)],
        compiler_params=params(),
        name="row_sums",
    )(parts, resident(kernel))


def last_row_kernel(parts_ref, kernel_ref, stat_ref, out_ref, scale_ref, keep_ref, part_ref):
    step, columns = kernel_ref.shape
    here = step // LANES
    blocks = stat_ref.shape[0] // 2
    i = pl.program_id(0)

    @pl.when(i == 0)
    def _():
        scale_ref[...] = 1.0 / jnp.sum(parts_ref[...], axis=0)
        for k in range(out_ref.shape[0]):
            out_ref[k, blocks:, :] = stat_ref[...]

    scale = spread_cols(scale_ref[...])

    def rows(r, _):
        at = pl.ds(pl.multiple_of(r * 8, 8), 8)
        k = kernel_ref[at, :]
        keep_ref[pl.ds(pl.multiple_of(i * step + r * 8, 8), 8), :] = k
        part_ref[at, :] = fold_lanes(k * scale, jnp.add)
        return 0

    lax.fori_loop(0, step // 8, rows, 0, unroll=4)
    for b in range(here):
        total = jnp.sum(lanes_of(part_ref, b), axis=0, keepdims=True)
        for k in range(out_ref.shape[0]):
            out_ref[k, pl.ds(i * here + b, 1), :] = total


def last_row_sums(parts, kernel, stats, peers):
    rows, columns = kernel.shape
    step = 256
    return pl.pallas_call(
        last_row_kernel,
        grid=(rows // step,),
        out_shape=(
            jax.ShapeDtypeStruct((peers, 3 * (rows // LANES), LANES), jnp.float32),
            jax.ShapeDtypeStruct((columns // LANES, LANES), jnp.float32),
            pltpu.VMEM((rows, columns), jnp.float32),
        ),
        in_specs=[VMEM, pl.BlockSpec((step, columns), lambda i: (i, 0)), VMEM],
        out_specs=(
            pl.BlockSpec((peers, 3 * (rows // LANES), LANES), lambda i: (0, 0, 0)),
            pl.BlockSpec((columns // LANES, LANES), lambda i: (0, 0)),
            VMEM,
        ),
        scratch_shapes=[pltpu.VMEM((step, LANES), jnp.float32)],
        compiler_params=params(12 * 1024 * 1024),
        name="last_row_sums",
    )(parts, streamed(kernel), stats)


def column_kernel(parts_ref, kernel_ref, out_ref, col_ref, sum_ref):
    rows, columns = kernel_ref.shape
    spread_rows(1.0 / jnp.sum(parts_ref[...], axis=0), col_ref)

    def step(i, acc):
        at = pl.ds(pl.multiple_of(i * 8, 8), 8)
        return acc + kernel_ref[at, :] * repeat_lanes(col_ref[at, :], columns // LANES)

    acc = lax.fori_loop(0, rows // 8, step, jnp.zeros((8, columns), jnp.float32), unroll=4)
    put_columns(acc, sum_ref, out_ref)


def column_sums(parts, kernel, peers):
    rows, columns = kernel.shape
    return pl.pallas_call(
        column_kernel,
        out_shape=jax.ShapeDtypeStruct((peers, columns // LANES, LANES), jnp.float32),
        in_specs=[VMEM, VMEM],
        out_specs=VMEM,
        scratch_shapes=[
            pltpu.VMEM((rows, LANES), jnp.float32),
            pltpu.VMEM((columns // LANES, LANES), jnp.float32),
        ],
        compiler_params=params(),
        name="column_sums",
    )(parts, resident(kernel))


def student_kernel(audio_ref, text_ref, exp_ref, stat_ref, logits_ref):
    step, columns = exp_ref.shape
    here = step // LANES
    blocks = stat_ref.shape[0] // 2
    i = pl.program_id(0)
    best = None
    for j in range(columns // WIDTH):
        x = 10.0 * contract_last(audio_ref[...], text_ref[pl.ds(j * WIDTH, WIDTH), :])
        logits_ref[:, pl.ds(j * WIDTH, WIDTH)] = x
        folded = fold_lanes(x, jnp.maximum)
        best = folded if best is None else jnp.maximum(best, folded)
    for b in range(here):
        rows = pl.ds(b * LANES, LANES)
        top = jnp.max(best[b * LANES : (b + 1) * LANES, :].T, axis=0, keepdims=True)
        stat_ref[pl.ds(i * here + b, 1), :] = top
        top = repeat_lanes(jnp.broadcast_to(top, (LANES, LANES)).T, WIDTH // LANES)
        total = None
        for j in range(columns // WIDTH):
            e = jnp.exp(logits_ref[rows, pl.ds(j * WIDTH, WIDTH)] - top)
            exp_ref[rows, pl.ds(j * WIDTH, WIDTH)] = e
            folded = fold_lanes(e, jnp.add)
            total = folded if total is None else total + folded
        stat_ref[pl.ds(blocks + i * here + b, 1), :] = jnp.sum(total.T, axis=0, keepdims=True)


def student_softmax(audio, text):
    rows, columns, depth = audio.shape[0], text.shape[0], audio.shape[1]
    step = 256
    return pl.pallas_call(
        student_kernel,
        grid=(rows // step,),
        out_shape=(
            pltpu.HBM((rows, columns), jnp.float32),
            jax.ShapeDtypeStruct((2 * (rows // LANES), LANES), jnp.float32),
        ),
        in_specs=[
            pl.BlockSpec((step, depth), lambda i: (i, 0)),
            pl.BlockSpec((columns, depth), lambda i: (0, 0), pipeline_mode=pl.Buffered(1)),
        ],
        out_specs=(
            pl.BlockSpec((step, columns), lambda i: (i, 0)),
            pl.BlockSpec((2 * (rows // LANES), LANES), lambda i: (0, 0)),
        ),
        scratch_shapes=[pltpu.VMEM((step, columns), jnp.float32)],
        compiler_params=params(20 * 1024 * 1024),
        cost_estimate=pl.CostEstimate(
            flops=2 * rows * columns * depth, bytes_accessed=4 * rows * columns, transcendentals=rows * columns
        ),
        name="student_softmax",
    )(streamed(audio), streamed(text))


def residual_kernel(
    rows_ref, scale_ref, own_ref, kernel_ref, exp_ref, audio_ref, text_ref,
    audio_out_ref, text_out_ref, weight_ref, prob_ref, residual_ref,
):
    rows, width = exp_ref.shape
    blocks = own_ref.shape[0] // 2
    step = 256
    i = pl.program_id(0)

    @pl.when(i == 0)
    def _():
        spread_rows(1.0 / jnp.sum(rows_ref[:, :blocks, :], axis=0), weight_ref)
        tops = rows_ref[:, blocks : 2 * blocks, :]
        top = jnp.max(tops, axis=0)
        total = jnp.sum(jnp.exp(tops - top[None]) * rows_ref[:, 2 * blocks :, :], axis=0)
        spread_rows(jnp.exp(own_ref[:blocks, :] - top) / total, prob_ref)
        audio_out_ref[...] = jnp.zeros_like(audio_out_ref)

    groups = width // LANES
    columns = pl.ds(pl.multiple_of(i * width, width), width)
    scale = jnp.concatenate(
        [jnp.broadcast_to(scale_ref[pl.ds(i * groups + g, 1), :], (8, LANES)) for g in range(groups)], axis=1
    )
    scale = jnp.concatenate([scale] * (step // 8), axis=0)

    def block(k, _):
        at = pl.ds(pl.multiple_of(k * step, step), step)
        target = (repeat_lanes(weight_ref[at, :], groups) * kernel_ref[at, columns]) * scale
        residual = (exp_ref[at, :] * repeat_lanes(prob_ref[at, :], groups) - target).astype(jnp.bfloat16)
        residual_ref[at, :] = residual
        audio_out_ref[at, :] += jnp.dot(residual, text_ref[...], preferred_element_type=jnp.float32)
        return 0

    lax.fori_loop(0, rows // step, block, 0)
    grad = lax.dot_general(
        residual_ref[...], audio_ref[...], (((0,), (0,)), ((), ())), preferred_element_type=jnp.float32
    )
    text_out_ref[columns, :] = (10.0 * grad).astype(text_out_ref.dtype)

    @pl.when(i == pl.num_programs(0) - 1)
    def _():
        audio_out_ref[...] = 10.0 * audio_out_ref[...]


def residual_grads(row_parts, scale, own, kernel, exps, audio, text, dtype):
    rows, columns = kernel.shape
    depth = audio.shape[1]
    width = 2 * WIDTH
    return pl.pallas_call(
        residual_kernel,
        grid=(columns // width,),
        out_shape=(
            jax.ShapeDtypeStruct((rows, depth), jnp.float32),
            pltpu.VMEM((columns, depth), dtype),
        ),
        in_specs=[VMEM] * 4
        + [
            pl.BlockSpec((rows, width), lambda i: (0, i)),
            pl.BlockSpec((rows, depth), lambda i: (0, 0), pipeline_mode=pl.Buffered(1)),
            pl.BlockSpec((width, depth), lambda i: (i, 0)),
        ],
        out_specs=(pl.BlockSpec((rows, depth), lambda i: (0, 0)), VMEM),
        scratch_shapes=[
            pltpu.VMEM((rows, LANES), jnp.float32),
            pltpu.VMEM((rows, LANES), jnp.float32),
            pltpu.VMEM((rows, width), jnp.bfloat16),
        ],
        compiler_params=params(36 * 1024 * 1024),
        name="residual_grads",
    )(row_parts, scale, own, resident(kernel), streamed(exps), audio, text)


def streamed(x):
    return pltpu.with_memory_space_constraint(x, pltpu.HBM)


def resident(x):
    return pltpu.with_memory_space_constraint(x, pltpu.VMEM)


def gather_a2a(x, axis, n):
    spread = jnp.broadcast_to(x[None], (n, *x.shape))
    return lax.all_to_all(spread, axis, 0, 0).reshape(n * x.shape[0], x.shape[1])


def swap(x, axis):
    return lax.all_to_all(x, axis, 0, 0)


def body(clips, caps, teacher_audio, teacher_text, student_audio, student_text):
    text_t = lax.all_gather(teacher_text, "clip", axis=0, tiled=True)
    audio_t = gather_a2a(teacher_audio, "cap", caps)
    student_audio, student_text, audio_t = lax.optimization_barrier((student_audio, student_text, audio_t))
    audio_s = gather_a2a(student_audio, "cap", caps)
    audio_s, text_t = lax.optimization_barrier((audio_s, text_t))
    text_s = lax.all_gather(student_text, "clip", axis=0, tiled=True)
    logits, maxima = teacher_logits(audio_t, text_t, caps)
    kernel, columns = exp_columns(swap(maxima, "cap"), logits, clips)
    for _ in range(ITERS - 1):
        row_parts = row_sums(swap(columns, "clip"), kernel, caps)
        columns = column_sums(swap(row_parts, "cap"), kernel, clips)
    exps, stats = student_softmax(audio_s, text_s)
    row_parts, scale, kernel = last_row_sums(swap(columns, "clip"), kernel, stats, caps)
    row_parts = swap(row_parts, "cap")
    audio_part, text_part = residual_grads(
        row_parts, scale, stats, kernel, exps, audio_s, text_s, jnp.bfloat16
    )
    audio_grad = lax.psum_scatter(audio_part, "cap", scatter_dimension=0, tiled=True)
    text_parts = swap(text_part.reshape(clips, -1, text_part.shape[1]), "clip")
    text_grad = jnp.sum(text_parts.astype(jnp.float32), axis=0)
    return audio_grad, text_grad


def solution(mesh):
    placed = (
        P(("clip", "cap"), None),
        P(("cap", "clip"), None),
        P(("clip", "cap"), None),
        P(("cap", "clip"), None),
    )
    return jax.shard_map(
        functools.partial(body, mesh.shape["clip"], mesh.shape["cap"]),
        mesh=mesh,
        in_specs=placed,
        out_specs=(P(("clip", "cap"), None), P(("cap", "clip"), None)),
        check_vma=False,
    )
```

time: 263 us -> 244 us (0.928)
  blocking collectives: 109 us -> 158 us
  waiting for transfers between devices: 49.6 us -> 0.74 us
  local copies, waits for them, and re-layouts: 22.2 us -> 3.09 us
  starting transfers between devices: 10.8 us -> 3.64 us
  Pallas kernels: 56 us -> 62.2 us
    all_to_all x0 -> x2, blocking collectives: none -> 51.9 us  [gather_a2a(): lax.all_to_all(spread, axis, 0, 0).reshape(n * x.shape[0], x.shape[1])]
    all_to_all x1 -> x0, waiting for transfers between devices: 30 us -> none  [gather_a2a(): lax.all_to_all(spread, axis, 0, 0).reshape(n * x.shape[0], x.shape[1])]
    all_gather x2 -> x1, waiting for transfers between devices: 17.5 us -> 0.01 us  [body(): text_t = lax.all_gather(teacher_text, 'clip', axis=0, tiled=True)]
    unnamed x20 -> x10, local copies, waits for them, and re-layouts: 19.4 us -> 1.91 us
    all_to_all x1 -> x0, starting transfers between devices: 7.12 us -> none  [gather_a2a(): lax.all_to_all(spread, axis, 0, 0).reshape(n * x.shape[0], x.shape[1])]
    pallas_call x5, Pallas kernels: 40.3 us -> 46.5 us  [the longest x1 20.3 us: residual_grads(): pl.pallas_call(residual_kernel, grid=(columns // width,), out_shape=(jax....]
  transfers between devices with their start and end apart: 6 -> 4, of which waited for: 2 -> 0; matrix products, arithmetic and copies ran while one was open for 2% -> 1% of each run, Pallas kernels for 12% -> 14%
where the time goes in v2:
time: 244 us; the launch traced here: 243 us
  blocking collectives  158 us (65%)
  Pallas kernels  62.2 us (25%)
  between operations  13.9 us (6%)
  starting transfers between devices  3.64 us (1%)
  local copies, waits for them, and re-layouts  3.09 us (1%)
    all_to_all x7, blocking collectives, swap(): return lax.all_to_all(x, axis, 0, 0)  106 us
    all_to_all x2, blocking collectives, gather_a2a(): lax.all_to_all(spread, axis, 0, 0).reshape(n * x.shape[0], x.shape[1])  51.9 us
    pallas_call x1, Pallas kernels, residual_grads(): pl.pallas_call(residual_kernel, grid=(columns // width,), out_shape=(jax....  20.3 us
    pallas_call x1, Pallas kernels, student_softmax(): pl.pallas_call(student_kernel, grid=(rows // step,), out_shape=(pltpu.HBM...  14 us
    pallas_call x1, Pallas kernels, last_row_sums(): pl.pallas_call(last_row_kernel, grid=(rows // step,), out_shape=(jax.Shap...  8.55 us
    pallas_call x1, Pallas kernels, teacher_logits(): pl.pallas_call(logits_kernel, out_shape=(pltpu.VMEM((rows, columns), jnp....  6.4 us
  transfers between devices with their start and end apart: 4, of which 0 were waited for; matrix products, arithmetic and copies ran while one was open for 1% of the time, Pallas kernels for 14%

profile of v2, /device:TPU:0, one launch (start us, length us, event | category | flops | bytes accessed | tf_op | source)
XLA Modules:
  0.0 243.0 jit_solution(8161693692272082611)
XLA Ops:
  7.2 0.0 copy-start.4
  7.2 0.0 all-gather.3.cloned.1.call-start
  7.2 0.7 all-gather.3.cloned.1.call-update
  7.9 0.0 all-gather.5.cloned.1.call-start
  8.0 1.1 broadcast_in_dim.4
  9.0 27.0 %all_to_all.50 = bf16[8,192,512]{2,1,0:T(8,128)(2,1)S(1)} all-to-all(bf16[8,192,512]{2,1,0:T(8,128)(2,1)S(1)} %broadcast_in_dim.4), channel_id=1, replica_groups=mesh['clip'=16,'cap'=8] {'cap'}, dimensions={0} | all-to-all | bytes 3145728 | tf_op jit(solution)/shard_map/all_to_all | solution.py:377
  36.0 0.0 all-gather.5.cloned.1.call-update
  36.0 0.0 copy-done.4
  36.1 0.1 broadcast_in_dim.5
  36.2 24.9 %all_to_all.51 = bf16[8,192,512]{2,1,0:T(8,128)(2,1)} all-to-all(bf16[8,192,512]{2,1,0:T(8,128)(2,1)S(1)} %broadcast_in_dim.5), channel_id=1, replica_groups=mesh['clip'=16,'cap'=8] {'cap'}, dimensions={0} | all-to-all | bytes 3145728 | tf_op jit(solution)/shard_map/all_to_all | solution.py:377
  61.1 0.0 all-gather.3.cloned.1.call-done.text_ref
  61.1 0.0 copy-start.1
  61.1 1.9 copy-done.1
  63.0 6.4 %logits.1 = (f32[1536,3072]{1,0:T(8,128)S(1)}, f32[8,12,128]{2,1,0:T(8,128)S(1)}) custom-call(bf16[1536,512]{1,0:T(8,128)(2,1)S(1)} %bitcast.3, bf16[3072,512]{1,0:T(8,128)(2,1)S(1)} %copy-done.1), custom_call_target="tpu_custom_call" | custom-call | tf_op jit(solution)/shard_map/logits/pallas_call | solution.py:78
  69.4 9.2 %all_to_all.52.max_ref = f32[8,12,128]{2,1,0:T(8,128)S(1)} all-to-all(f32[8,12,128]{2,1,0:T(8,128)S(1)} %get-tuple-element.21), channel_id=1, replica_groups=mesh['clip'=16,'cap'=8] {'cap'}, dimensions={0} | all-to-all | bytes 98304 | tf_op jit(solution)/shard_map/all_to_all | solution.py:381
  78.6 4.6 %exp_columns.1 = (f32[1536,3072]{1,0:T(8,128)S(1)}, f32[16,24,128]{2,1,0:T(8,128)S(1)}) custom-call(f32[8,12,128]{2,1,0:T(8,128)S(1)} %all_to_all.52.max_ref, f32[1536,3072]{1,0:T(8,128)S(1)} %get-tuple-element.22.logits_ref), custom_call_target="tpu_custom_call", output_to_operand_aliasing={{0}: (1, {})} | custom-call | tf_op jit(solution)/shard_map/exp_columns/pallas_call | solution.py:117
  83.2 0.0 copy-start
  83.3 14.0 %all_to_all.53.parts_ref = f32[16,24,128]{2,1,0:T(8,128)S(1)} all-to-all(f32[16,24,128]{2,1,0:T(8,128)S(1)} %get-tuple-element.23), channel_id=1, replica_groups=mesh['clip'=16,'cap'=8] {'clip'}, dimensions={0} | all-to-all | bytes 393216 | tf_op jit(solution)/shard_map/all_to_all | solution.py:381
  97.3 1.8 row_sums.2
  99.1 8.0 %all_to_all.54.parts_ref = f32[8,12,128]{2,1,0:T(8,128)S(1)} all-to-all(f32[8,12,128]{2,1,0:T(8,128)S(1)} %row_sums.2), channel_id=1, replica_groups=mesh['clip'=16,'cap'=8] {'cap'}, dimensions={0} | all-to-all | bytes 98304 | tf_op jit(solution)/shard_map/all_to_all | solution.py:381
  107.1 2.0 column_sums.2
  109.1 11.3 %all_to_all.55.parts_ref = f32[16,24,128]{2,1,0:T(8,128)S(1)} all-to-all(f32[16,24,128]{2,1,0:T(8,128)S(1)} %column_sums.2), channel_id=1, replica_groups=mesh['clip'=16,'cap'=8] {'clip'}, dimensions={0} | all-to-all | bytes 393216 | tf_op jit(solution)/shard_map/all_to_all | solution.py:381
  120.4 1.8 row_sums.3
  122.2 8.0 %all_to_all.56.parts_ref = f32[8,12,128]{2,1,0:T(8,128)S(1)} all-to-all(f32[8,12,128]{2,1,0:T(8,128)S(1)} %row_sums.3), channel_id=1, replica_groups=mesh['clip'=16,'cap'=8] {'cap'}, dimensions={0} | all-to-all | bytes 98304 | tf_op jit(solution)/shard_map/all_to_all | solution.py:381
  130.2 0.0 copy-done
  130.2 2.7 %column_sums.3 = f32[16,24,128]{2,1,0:T(8,128)} custom-call(f32[8,12,128]{2,1,0:T(8,128)S(1)} %all_to_all.56.parts_ref, f32[1536,3072]{1,0:T(8,128)S(1)} %get-tuple-element.24.kernel_ref), custom_call_target="tpu_custom_call" | custom-call | tf_op jit(solution)/shard_map/column_sums/pallas_call | solution.py:229
  132.9 3.5 %all-to-all-start.7 = ((f32[16,24,128]{2,1,0:T(8,128)}), f32[16,24,128]{2,1,0:T(8,128)S(1)}, u32[]{:S(2)}, u32[]{:S(2)}) async-start(f32[16,24,128]{2,1,0:T(8,128)} %column_sums.3), calls=%async_computation.7 | async-start | bytes 393216 | tf_op jit(solution)/shard_map/all_to_all | solution.py:381
  136.4 0.0 reduce-scatter.2.cloned.1.call-start
  136.5 0.0 all-gather.5.cloned.1.call-done.text_ref
  136.5 14.0 %student_softmax.1 = (f32[1536,3072]{1,0:T(8,128)}, f32[24,128]{1,0:T(8,128)S(1)}) custom-call(bf16[1536,512]{1,0:T(8,128)(2,1)} %bitcast.5, bf16[3072,512]{1,0:T(8,128)(2,1)} %all-gather.5.cloned.1.call-done.text_ref), custom_call_target="tpu_custom_call" | custom-call | flops 4831838208 | bytes 18874368 | tf_op jit(solution)/shard_map/student_softmax/pallas_call | solution.py:271
  150.5 0.0 copy-start.2
  150.5 0.0 all-to-all-done.7.parts_ref
  150.5 8.5 %last_row_sums.1 = (f32[8,36,128]{2,1,0:T(8,128)S(1)}, f32[24,128]{1,0:T(8,128)S(1)}, f32[1536,3072]{1,0:T(8,128)S(1)}) custom-call(f32[16,24,128]{2,1,0:T(8,128)S(1)} %all-to-all-done.7.parts_ref, f32[1536,3072]{1,0:T(8,128)} %copy-done, f32[24,128]{1,0:T(8,128)S(1)} %get-tuple-element.27.stat_ref.own_ref), custom_call_target="tpu_custom_call" | custom-call | tf_op jit(solution)/shard_map/last_row_sums/pallas_call | solution.py:195
  159.1 0.0 copy-done.2
  159.1 0.0 copy-start.3
  159.1 9.5 %all_to_all.57.rows_ref = f32[8,36,128]{2,1,0:T(8,128)} all-to-all(f32[8,36,128]{2,1,0:T(8,128)S(1)} %get-tuple-element.28), channel_id=1, replica_groups=mesh['clip'=16,'cap'=8] {'cap'}, dimensions={0} | all-to-all | bytes 294912 | tf_op jit(solution)/shard_map/all_to_all | solution.py:381
  168.7 0.0 copy-done.3
  168.7 20.3 %residual_grads.1 = (f32[1536,512]{1,0:T(8,128)}, bf16[3072,512]{1,0:T(8,128)(2,1)S(1)}) custom-call(f32[8,36,128]{2,1,0:T(8,128)} %all_to_all.57.rows_ref, f32[24,128]{1,0:T(8,128)} %copy-done.3, f32[24,128]{1,0:T(8,128)} %copy-done.2, f32[1536,3072]{1,0:T(8,128)S(1)} %get-tuple-element.30.kernel_ref, f32[1536,3072]{1,0:T(8,128)} %get-tuple-element.31.exp_ref, ...), custom_call_target="tpu_custom_call" | custom-call | tf_op jit(solution)/shard_map/residual_grads/pallas_call | solution.py:343
  189.0 0.0 reduce-scatter.2.cloned.1.call-update
  189.0 46.3 %all_to_all.58 = bf16[16,192,512]{2,1,0:T(8,128)(2,1)S(1)} all-to-all(bf16[16,192,512]{2,1,0:T(8,128)(2,1)S(1)} %bitcast.4), channel_id=1, replica_groups=mesh['clip'=16,'cap'=8] {'clip'}, dimensions={0} | all-to-all | bytes 6291456 | tf_op jit(solution)/shard_map/all_to_all | solution.py:381
  235.3 1.2 convert_reduce_fusion
  236.5 0.0 reduce-scatter.2.cloned.1.call-done
Async XLA Ops:
  7.2 28.9 %copy-start.4 = (bf16[192,512]{1,0:T(8,128)(2,1)S(1)}, bf16[192,512]{1,0:T(8,128)(2,1)}, u32[]{:S(2)}) copy-start(bf16[192,512]{1,0:T(8,128)(2,1)} %param.6) | copy-start | bytes 589828
  7.2 54.0 %all-gather.3.cloned.1.call-start = ((), (), s32[]{:S(2)}) async-start(), calls=%async_computation.11 | async-start | bytes 3342336 | tf_op jit(solution)/shard_map/all_gather | solution.py:385
  7.9 128.6 %all-gather.5.cloned.1.call-start = ((), (), s32[]{:S(2)}) async-start(), calls=%async_computation.12 | async-start | bytes 3342336 | tf_op jit(solution)/shard_map/all_gather | solution.py:390
  61.1 1.9 copy-start.1
  83.2 47.0 %copy-start = (f32[1536,3072]{1,0:T(8,128)}, f32[1536,3072]{1,0:T(8,128)S(1)}, u32[]{:S(2)}) copy-start(f32[1536,3072]{1,0:T(8,128)S(1)} %get-tuple-element.24.kernel_ref) | copy-start | bytes 56623108
  132.9 17.6 %all-to-all-start.7 = ((f32[16,24,128]{2,1,0:T(8,128)}), f32[16,24,128]{2,1,0:T(8,128)S(1)}, u32[]{:S(2)}, u32[]{:S(2)}) async-start(f32[16,24,128]{2,1,0:T(8,128)} %column_sums.3), calls=%async_computation.7 | async-start | bytes 393216 | tf_op jit(solution)/shard_map/all_to_all | solution.py:381
  136.4 100.1 %reduce-scatter.2.cloned.1.call-start = ((), (), s32[]{:S(2)}) async-start(), calls=%async_computation.13 | async-start | bytes 3538944 | tf_op jit(solution)/shard_map/reduce_scatter | solution.py:402
  150.5 8.6 %copy-start.2 = (f32[24,128]{1,0:T(8,128)}, f32[24,128]{1,0:T(8,128)S(1)}, u32[]{:S(2)}) copy-start(f32[24,128]{1,0:T(8,128)S(1)} %get-tuple-element.27.stat_ref.own_ref) | copy-start | bytes 36868
  159.1 9.6 %copy-start.3 = (f32[24,128]{1,0:T(8,128)}, f32[24,128]{1,0:T(8,128)S(1)}, u32[]{:S(2)}) copy-start(f32[24,128]{1,0:T(8,128)S(1)} %get-tuple-element.29.scale_ref) | copy-start | bytes 36868
Sparse Core Ops, SparseCore 0:
  10.1 50.2 all-gather.2
  62.6 46.7 all-gather.4
  189.1 36.2 reduce-scatter.1

commit v3 on v1

v3 whole, which is shorter than its diff:
```python
import functools

import jax
import jax.numpy as jnp
from jax import lax
from jax.experimental import pallas as pl
from jax.experimental.pallas import tpu as pltpu
from jax.sharding import PartitionSpec as P

ITERS = 3
LANES = 128
WIDTH = 512
VMEM = pl.BlockSpec(memory_space=pltpu.VMEM)
HBM = pl.BlockSpec(memory_space=pltpu.HBM)
LIMIT = 19 * 1024 * 1024


def params(limit=LIMIT):
    return pltpu.CompilerParams(vmem_limit_bytes=limit)


def lanes_of(ref, block):
    return ref[pl.ds(block * LANES, LANES), :].T


def spread_rows(vec, ref):
    for block in range(vec.shape[0]):
        row = jnp.broadcast_to(vec[block : block + 1, :], (LANES, LANES))
        ref[pl.ds(block * LANES, LANES), :] = row.T


def spread_cols(vec):
    return jnp.concatenate(
        [jnp.broadcast_to(vec[g : g + 1, :], (8, LANES)) for g in range(vec.shape[0])], axis=1
    )


def repeat_lanes(col, groups):
    return jnp.concatenate([col] * groups, axis=1)


def fold_lanes(x, op):
    parts = [x[:, g * LANES : (g + 1) * LANES] for g in range(x.shape[1] // LANES)]
    while len(parts) > 1:
        parts = [op(*parts[k : k + 2]) if k + 1 < len(parts) else parts[k] for k in range(0, len(parts), 2)]
    return parts[0]


def contract_last(left, right):
    return lax.dot_general(left, right, (((1,), (1,)), ((), ())), preferred_element_type=jnp.float32)


def text_copies(from_ref, to_ref, sems):
    chunks = [pl.ds(j * WIDTH, WIDTH) for j in range(to_ref.shape[0] // WIDTH)]
    copies = [pltpu.make_async_copy(from_ref.at[c], to_ref.at[c], sems.at[j]) for j, c in enumerate(chunks)]
    for copy in copies:
        copy.start()
    return copies


def multiply_chunk(j, audio_ref, text_ref, logits_ref, best_ref):
    step = 256
    at = pl.ds(j * WIDTH, WIDTH)

    def block(i, _):
        rows = pl.ds(pl.multiple_of(i * step, step), step)
        x = 10.0 * contract_last(audio_ref[rows, :], text_ref[at, :])
        logits_ref[rows, at] = x
        folded = fold_lanes(x, jnp.maximum)
        best_ref[rows, :] = folded if j == 0 else jnp.maximum(best_ref[rows, :], folded)
        return 0

    lax.fori_loop(0, audio_ref.shape[0] // step, block, 0)


def logits_kernel(audio_ref, text_hbm_ref, logits_ref, max_ref, text_ref, part_ref, sems):
    rows = logits_ref.shape[0]
    for j, copy in enumerate(text_copies(text_hbm_ref, text_ref, sems)):
        copy.wait()
        multiply_chunk(j, audio_ref, text_ref, logits_ref, part_ref)
    for b in range(rows // LANES):
        top = jnp.max(lanes_of(part_ref, b), axis=0, keepdims=True)
        for k in range(max_ref.shape[0]):
            max_ref[k, b : b + 1, :] = top


def teacher_logits(audio, text, peers):
    rows, columns = audio.shape[0], text.shape[0]
    return pl.pallas_call(
        logits_kernel,
        out_shape=(
            pltpu.VMEM((rows, columns), jnp.float32),
            jax.ShapeDtypeStruct((peers, rows // LANES, LANES), jnp.float32),
        ),
        in_specs=[VMEM, HBM],
        out_specs=(VMEM, VMEM),
        scratch_shapes=[
            pltpu.VMEM(text.shape, text.dtype),
            pltpu.VMEM((rows, LANES), jnp.float32),
            pltpu.SemaphoreType.DMA((columns // WIDTH,)),
        ],
        compiler_params=params(),
        name="logits",
    )(audio, streamed(text))


def put_columns(acc, sum_ref, out_ref):
    groups = sum_ref.shape[0]
    for g in range(groups):
        sum_ref[g : g + 1, :] = jnp.sum(acc[:, g * LANES : (g + 1) * LANES], axis=0, keepdims=True)
    total = sum_ref[...]
    for k in range(out_ref.shape[0]):
        out_ref[k] = total


def exp_kernel(max_ref, logits_ref, kernel_ref, out_ref, col_ref, sum_ref):
    rows, columns = logits_ref.shape
    spread_rows(jnp.max(max_ref[...], axis=0), col_ref)

    def step(i, acc):
        at = pl.ds(pl.multiple_of(i * 8, 8), 8)
        k = jnp.exp(logits_ref[at, :] - repeat_lanes(col_ref[at, :], columns // LANES))
        kernel_ref[at, :] = k
        return acc + k

    acc = lax.fori_loop(0, rows // 8, step, jnp.zeros((8, columns), jnp.float32), unroll=4)
    put_columns(acc, sum_ref, out_ref)


def exp_columns(maxima, logits, peers):
    rows, columns = logits.shape
    return pl.pallas_call(
        exp_kernel,
        out_shape=(
            pltpu.VMEM((rows, columns), jnp.float32),
            jax.ShapeDtypeStruct((peers, columns // LANES, LANES), jnp.float32),
        ),
        in_specs=[VMEM, VMEM],
        out_specs=(VMEM, VMEM),
        scratch_shapes=[
            pltpu.VMEM((rows, LANES), jnp.float32),
            pltpu.VMEM((columns // LANES, LANES), jnp.float32),
        ],
        input_output_aliases={1: 0},
        compiler_params=params(),
        name="exp_columns",
    )(maxima, resident(logits))


def row_kernel(parts_ref, kernel_ref, stat_ref, out_ref, scale_ref, part_ref):
    if stat_ref is not None:
        kernel_ref = kernel_ref.at[0]
    rows = kernel_ref.shape[0]
    blocks = rows // LANES
    scale_ref[...] = 1.0 / jnp.sum(parts_ref[...], axis=0)
    scale = spread_cols(scale_ref[...])

    def step(i, _):
        at = pl.ds(pl.multiple_of(i * 8, 8), 8)
        part_ref[at, :] = fold_lanes(kernel_ref[at, :] * scale, jnp.add)
        return 0

    lax.fori_loop(0, rows // 8, step, 0, unroll=4)
    for b in range(blocks):
        total = jnp.sum(lanes_of(part_ref, b), axis=0, keepdims=True)
        for k in range(out_ref.shape[0]):
            out_ref[k, b : b + 1, :] = total
    if stat_ref is not None:
        for k in range(out_ref.shape[0]):
            out_ref[k, blocks:, :] = stat_ref[...]


def row_sums(parts, kernel, peers, stats=None):
    rows, columns = kernel.shape[-2:]
    if stats is None:
        extra, body = (), lambda parts_ref, kernel_ref, *refs: row_kernel(parts_ref, kernel_ref, None, *refs)
    else:
        extra, body = (stats,), row_kernel
    return pl.pallas_call(
        body,
        out_shape=(
            jax.ShapeDtypeStruct((peers, rows // LANES * (3 if extra else 1), LANES), jnp.float32),
            jax.ShapeDtypeStruct((columns // LANES, LANES), jnp.float32),
        ),
        in_specs=[VMEM] * (2 + len(extra)),
        out_specs=(VMEM, VMEM),
        scratch_shapes=[pltpu.VMEM((rows, LANES), jnp.float32)],
        compiler_params=params(),
        name="row_sums",
    )(parts, resident(kernel), *extra)


def column_kernel(parts_ref, kernel_ref, out_ref, col_ref, sum_ref):
    rows, columns = kernel_ref.shape
    spread_rows(1.0 / jnp.sum(parts_ref[...], axis=0), col_ref)

    def step(i, acc):
        at = pl.ds(pl.multiple_of(i * 8, 8), 8)
        return acc + kernel_ref[at, :] * repeat_lanes(col_ref[at, :], columns // LANES)

    acc = lax.fori_loop(0, rows // 8, step, jnp.zeros((8, columns), jnp.float32), unroll=4)
    put_columns(acc, sum_ref, out_ref)


def column_sums(parts, kernel, peers):
    rows, columns = kernel.shape
    return pl.pallas_call(
        column_kernel,
        out_shape=jax.ShapeDtypeStruct((peers, columns // LANES, LANES), jnp.float32),
        in_specs=[VMEM, VMEM],
        out_specs=VMEM,
        scratch_shapes=[
            pltpu.VMEM((rows, LANES), jnp.float32),
            pltpu.VMEM((columns // LANES, LANES), jnp.float32),
        ],
        compiler_params=params(),
        name="column_sums",
    )(parts, resident(kernel))


def student_kernel(
    audio_ref, text_hbm_ref, kernel_hbm_ref, pair_ref, stat_ref, text_ref, part_ref, sems, kernel_sem
):
    kernel_ref, exp_ref = pair_ref.at[0], pair_ref.at[1]
    rows, columns = exp_ref.shape
    blocks = rows // LANES
    kernel_copy = pltpu.make_async_copy(kernel_hbm_ref, kernel_ref, kernel_sem)
    for j, copy in enumerate(text_copies(text_hbm_ref, text_ref, sems)):
        copy.wait()
        if j == 0:
            kernel_copy.start()
        multiply_chunk(j, audio_ref, text_ref, exp_ref, part_ref)
    for b in range(blocks):
        top = jnp.max(lanes_of(part_ref, b), axis=0, keepdims=True)
        stat_ref[b : b + 1, :] = top
        part_ref[pl.ds(b * LANES, LANES), :] = jnp.broadcast_to(top, (LANES, LANES)).T

    def step(i, _):
        at = pl.ds(pl.multiple_of(i * 8, 8), 8)
        e = jnp.exp(exp_ref[at, :] - repeat_lanes(part_ref[at, :], columns // LANES))
        exp_ref[at, :] = e
        part_ref[at, :] = fold_lanes(e, jnp.add)
        return 0

    lax.fori_loop(0, rows // 8, step, 0, unroll=4)
    for b in range(blocks):
        total = jnp.sum(lanes_of(part_ref, b), axis=0, keepdims=True)
        stat_ref[blocks + b : blocks + b + 1, :] = total
    kernel_copy.wait()


def student_softmax(audio, text, kernel):
    rows, columns = audio.shape[0], text.shape[0]
    return pl.pallas_call(
        student_kernel,
        out_shape=(
            pltpu.VMEM((2, rows, columns), jnp.float32),
            jax.ShapeDtypeStruct((2 * (rows // LANES), LANES), jnp.float32),
        ),
        in_specs=[VMEM, HBM, HBM],
        out_specs=(VMEM, VMEM),
        scratch_shapes=[
            pltpu.VMEM(text.shape, text.dtype),
            pltpu.VMEM((rows, LANES), jnp.float32),
            pltpu.SemaphoreType.DMA((columns // WIDTH,)),
            pltpu.SemaphoreType.DMA,
        ],
        compiler_params=params(),
        name="student_softmax",
    )(audio, streamed(text), streamed(kernel))


def residual_kernel(
    rows_ref, scale_ref, own_ref, pair_ref, audio_hbm_ref, text_hbm_ref,
    audio_out_ref, text_out_ref, weight_ref, prob_ref, residual_ref, audio_ref, text_ref, audio_sem, text_sem,
):
    kernel_ref, exp_ref = pair_ref.at[0], pair_ref.at[1]
    step, depth = audio_out_ref.shape
    rows, columns = pair_ref.shape[1:]
    blocks = own_ref.shape[0] // 2
    groups = WIDTH // LANES
    i = pl.program_id(0)
    audio_copy = pltpu.make_async_copy(audio_hbm_ref, audio_ref, audio_sem)
    text_copy = pltpu.make_async_copy(text_hbm_ref, text_ref, text_sem)

    @pl.when(i == 0)
    def _():
        text_copy.start()
        audio_copy.start()
        spread_rows(1.0 / jnp.sum(rows_ref[:, :blocks, :], axis=0), weight_ref)
        tops = rows_ref[:, blocks : 2 * blocks, :]
        top = jnp.max(tops, axis=0)
        total = jnp.sum(jnp.exp(tops - top[None]) * rows_ref[:, 2 * blocks :, :], axis=0)
        spread_rows(jnp.exp(own_ref[:blocks, :] - top) / total, prob_ref)

    at = pl.ds(pl.multiple_of(i * step, step), step)
    for j in range(columns // WIDTH):
        lanes = pl.ds(j * WIDTH, WIDTH)
        scale = spread_cols(scale_ref[j * groups : (j + 1) * groups, :])
        scale = jnp.concatenate([scale] * (step // 8), axis=0)
        target = (repeat_lanes(weight_ref[at, :], groups) * kernel_ref[at, lanes]) * scale
        prob = exp_ref[at, lanes] * repeat_lanes(prob_ref[at, :], groups)
        residual_ref[at, lanes] = (prob - target).astype(jnp.bfloat16)
    pl.when(i == 0)(text_copy.wait)
    audio_out_ref[...] = 10.0 * jnp.dot(residual_ref[at, :], text_ref[...], preferred_element_type=jnp.float32)

    @pl.when(i == pl.num_programs(0) - 1)
    def _():
        audio_copy.wait()
        for j in range(columns // WIDTH):
            grad = lax.dot_general(
                residual_ref[:, pl.ds(j * WIDTH, WIDTH)],
                audio_ref[...],
                (((0,), (0,)), ((), ())),
                preferred_element_type=jnp.float32,
            )
            text_out_ref[pl.ds(j * WIDTH, WIDTH), :] = (10.0 * grad).astype(text_out_ref.dtype)


def residual_grads(row_parts, scale, own, pair, audio, text, dtype):
    rows, columns = pair.shape[1:]
    depth = audio.shape[1]
    step = 256
    return pl.pallas_call(
        residual_kernel,
        grid=(rows // step,),
        out_shape=(
            jax.ShapeDtypeStruct((rows, depth), jnp.float32),
            pltpu.VMEM((columns, depth), dtype),
        ),
        in_specs=[VMEM] * 4 + [HBM] * 2,
        out_specs=(pl.BlockSpec((step, depth), lambda i: (i, 0)), VMEM),
        scratch_shapes=[
            pltpu.VMEM((rows, LANES), jnp.float32),
            pltpu.VMEM((rows, LANES), jnp.float32),
            pltpu.VMEM((rows, columns), jnp.bfloat16),
            pltpu.VMEM(audio.shape, audio.dtype),
            pltpu.VMEM(text.shape, text.dtype),
            pltpu.SemaphoreType.DMA,
            pltpu.SemaphoreType.DMA,
        ],
        compiler_params=params(),
        name="residual_grads",
    )(row_parts, scale, own, resident(pair), streamed(audio), streamed(text))


def resident(x):
    return pltpu.with_memory_space_constraint(x, pltpu.VMEM)


def streamed(x):
    return pltpu.with_memory_space_constraint(x, pltpu.HBM)


def gather_a2a(x, axis, n):
    spread = jnp.broadcast_to(x[None], (n, *x.shape))
    return lax.all_to_all(spread, axis, 0, 0).reshape(n * x.shape[0], x.shape[1])


def swap(x, axis):
    return lax.all_to_all(x, axis, 0, 0)


def body(clips, caps, teacher_audio, teacher_text, student_audio, student_text):
    text_t = lax.all_gather(teacher_text, "clip", axis=0, tiled=True)
    audio_t = gather_a2a(teacher_audio, "cap", caps)
    student_audio, student_text, audio_t = lax.optimization_barrier((student_audio, student_text, audio_t))
    audio_s = gather_a2a(student_audio, "cap", caps)
    audio_s, text_t = lax.optimization_barrier((audio_s, text_t))
    text_s = lax.all_gather(student_text, "clip", axis=0, tiled=True)
    logits, maxima = teacher_logits(audio_t, text_t, caps)
    kernel, columns = exp_columns(swap(maxima, "cap"), logits, clips)
    for _ in range(ITERS - 1):
        row_parts, _ = row_sums(swap(columns, "clip"), kernel, caps)
        columns = column_sums(swap(row_parts, "cap"), kernel, clips)
    columns, text_s = lax.optimization_barrier((columns, text_s))
    columns, audio_s = lax.optimization_barrier((swap(columns, "clip"), audio_s))
    pair, stats = student_softmax(audio_s, text_s, kernel)
    row_parts, scale = row_sums(columns, pair, caps, stats)
    row_parts = swap(row_parts, "cap")
    audio_part, text_part = residual_grads(
        row_parts, scale, stats, pair, audio_s, text_s, jnp.bfloat16
    )
    audio_grad = lax.psum_scatter(audio_part, "cap", scatter_dimension=0, tiled=True)
    text_parts = swap(text_part.reshape(clips, -1, text_part.shape[1]), "clip")
    text_grad = jnp.sum(text_parts.astype(jnp.float32), axis=0)
    return audio_grad, text_grad


def solution(mesh):
    placed = (
        P(("clip", "cap"), None),
        P(("cap", "clip"), None),
        P(("clip", "cap"), None),
        P(("cap", "clip"), None),
    )
    return jax.shard_map(
        functools.partial(body, mesh.shape["clip"], mesh.shape["cap"]),
        mesh=mesh,
        in_specs=placed,
        out_specs=(P(("clip", "cap"), None), P(("cap", "clip"), None)),
        check_vma=False,
    )
```

time: 263 us -> 255 us (0.970)
  blocking collectives: 109 us -> 169 us
  waiting for transfers between devices: 49.6 us -> 0.74 us
  local copies, waits for them, and re-layouts: 22.2 us -> 1.19 us
  Pallas kernels: 56 us -> 67.7 us
  starting transfers between devices: 10.8 us -> 0.12 us
    all_to_all x0 -> x2, blocking collectives: none -> 52 us  [gather_a2a(): lax.all_to_all(spread, axis, 0, 0).reshape(n * x.shape[0], x.shape[1])]
    all_to_all x2 -> x0, waiting for transfers between devices: 30 us -> none  [the longest x1 30 us: gather_a2a(): lax.all_to_all(spread, axis, 0, 0).reshape(n * x.shape[0], x.shape[1])]
    unnamed x20 -> x4, local copies, waits for them, and re-layouts: 19.4 us -> 0.01 us
    all_gather x2 -> x1, waiting for transfers between devices: 17.5 us -> 0.01 us  [body(): text_t = lax.all_gather(teacher_text, 'clip', axis=0, tiled=True)]
    all_to_all x2 -> x0, starting transfers between devices: 10.6 us -> none  [the longest x1 7.12 us: gather_a2a(): lax.all_to_all(spread, axis, 0, 0).reshape(n * x.shape[0], x.shape[1])]
    pallas_call x4, Pallas kernels: 18.7 us -> 28.6 us  [the longest x1 20.9 us: student_softmax(): pl.pallas_call(student_kernel, out_shape=(pltpu.VMEM((2, rows, columns),...]
    all_to_all x7 -> x8, blocking collectives: 109 us -> 117 us  [swap(): return lax.all_to_all(x, axis, 0, 0)]
    pallas_call x1, Pallas kernels: 6.39 us -> 13.5 us  [teacher_logits(): pl.pallas_call(logits_kernel, out_shape=(pltpu.VMEM((rows, columns), jnp....]
  transfers between devices with their start and end apart: 6 -> 3, of which waited for: 2 -> 0; matrix products, arithmetic and copies ran while one was open for 2% -> 1% of each run, Pallas kernels for 12% -> 10%
where the time goes in v3:
time: 255 us; the launch traced here: 254 us
  blocking collectives  169 us (66%)
  Pallas kernels  67.7 us (27%)
  between operations  13.8 us (5%)
    all_to_all x8, blocking collectives, swap(): return lax.all_to_all(x, axis, 0, 0)  117 us
    all_to_all x2, blocking collectives, gather_a2a(): lax.all_to_all(spread, axis, 0, 0).reshape(n * x.shape[0], x.shape[1])  52 us
    pallas_call x1, Pallas kernels, student_softmax(): pl.pallas_call(student_kernel, out_shape=(pltpu.VMEM((2, rows, columns),...  20.9 us
    pallas_call x1, Pallas kernels, residual_grads(): pl.pallas_call(residual_kernel, grid=(rows // step,), out_shape=(jax.Shap...  17 us
    pallas_call x1, Pallas kernels, teacher_logits(): pl.pallas_call(logits_kernel, out_shape=(pltpu.VMEM((rows, columns), jnp....  13.5 us
    pallas_call x3, Pallas kernels, row_sums(): pl.pallas_call(body, out_shape=(jax.ShapeDtypeStruct((peers, rows // LANE...  7.7 us
  transfers between devices with their start and end apart: 3, of which 0 were waited for; matrix products, arithmetic and copies ran while one was open for 1% of the time, Pallas kernels for 10%

profile of v3, /device:TPU:0, one launch (start us, length us, event | category | flops | bytes accessed | tf_op | source)
XLA Modules:
  0.0 253.9 jit_solution(9861186582356622112)
XLA Ops:
  7.2 0.0 copy-start.1
  7.2 0.0 all-gather.3.cloned.1.call-start
  7.2 0.7 all-gather.3.cloned.1.call-update
  7.9 0.0 all-gather.5.cloned.1.call-start
  8.0 1.1 broadcast_in_dim.4
  9.0 27.0 %all_to_all.50 = bf16[8,192,512]{2,1,0:T(8,128)(2,1)S(1)} all-to-all(bf16[8,192,512]{2,1,0:T(8,128)(2,1)S(1)} %broadcast_in_dim.4), channel_id=1, replica_groups=mesh['clip'=16,'cap'=8] {'cap'}, dimensions={0} | all-to-all | bytes 3145728 | tf_op jit(solution)/shard_map/all_to_all | solution.py:357
  36.0 0.0 all-gather.5.cloned.1.call-update
  36.0 0.0 reduce-scatter.2.cloned.1.call-start
  36.1 0.0 copy-done.1
  36.1 0.1 broadcast_in_dim.5
  36.2 25.0 %all_to_all.51 = bf16[8,192,512]{2,1,0:T(8,128)(2,1)} all-to-all(bf16[8,192,512]{2,1,0:T(8,128)(2,1)S(1)} %broadcast_in_dim.5), channel_id=1, replica_groups=mesh['clip'=16,'cap'=8] {'cap'}, dimensions={0} | all-to-all | bytes 3145728 | tf_op jit(solution)/shard_map/all_to_all | solution.py:357
  61.2 0.0 all-gather.3.cloned.1.call-done.text_hbm_ref
  61.2 13.5 %logits.1 = (f32[1536,3072]{1,0:T(8,128)S(1)}, f32[8,12,128]{2,1,0:T(8,128)S(1)}) custom-call(bf16[1536,512]{1,0:T(8,128)(2,1)S(1)} %bitcast.3, bf16[3072,512]{1,0:T(8,128)(2,1)} %all-gather.3.cloned.1.call-done.text_hbm_ref), custom_call_target="tpu_custom_call" | custom-call | tf_op jit(solution)/shard_map/logits/pallas_call | solution.py:89
  74.7 9.1 %all_to_all.52.max_ref = f32[8,12,128]{2,1,0:T(8,128)S(1)} all-to-all(f32[8,12,128]{2,1,0:T(8,128)S(1)} %get-tuple-element.26), channel_id=1, replica_groups=mesh['clip'=16,'cap'=8] {'cap'}, dimensions={0} | all-to-all | bytes 98304 | tf_op jit(solution)/shard_map/all_to_all | solution.py:361
  83.8 4.6 %exp_columns.1 = (f32[1536,3072]{1,0:T(8,128)S(1)}, f32[16,24,128]{2,1,0:T(8,128)S(1)}) custom-call(f32[8,12,128]{2,1,0:T(8,128)S(1)} %all_to_all.52.max_ref, f32[1536,3072]{1,0:T(8,128)S(1)} %get-tuple-element.27.logits_ref), custom_call_target="tpu_custom_call", output_to_operand_aliasing={{0}: (1, {})} | custom-call | tf_op jit(solution)/shard_map/exp_columns/pallas_call | solution.py:132
  88.5 0.0 copy-start
  88.5 16.7 %all_to_all.53.parts_ref = f32[16,24,128]{2,1,0:T(8,128)S(1)} all-to-all(f32[16,24,128]{2,1,0:T(8,128)S(1)} %get-tuple-element.28), channel_id=1, replica_groups=mesh['clip'=16,'cap'=8] {'clip'}, dimensions={0} | all-to-all | bytes 393216 | tf_op jit(solution)/shard_map/all_to_all | solution.py:361
  105.2 2.1 row_sums.3
  107.3 8.0 %all_to_all.54.parts_ref = f32[8,12,128]{2,1,0:T(8,128)S(1)} all-to-all(f32[8,12,128]{2,1,0:T(8,128)S(1)} %get-tuple-element.30), channel_id=1, replica_groups=mesh['clip'=16,'cap'=8] {'cap'}, dimensions={0} | all-to-all | bytes 98304 | tf_op jit(solution)/shard_map/all_to_all | solution.py:361
  115.3 2.0 column_sums.2
  117.3 11.0 %all_to_all.55.parts_ref = f32[16,24,128]{2,1,0:T(8,128)S(1)} all-to-all(f32[16,24,128]{2,1,0:T(8,128)S(1)} %column_sums.2), channel_id=1, replica_groups=mesh['clip'=16,'cap'=8] {'clip'}, dimensions={0} | all-to-all | bytes 393216 | tf_op jit(solution)/shard_map/all_to_all | solution.py:361
  128.3 2.1 row_sums.4
  130.4 8.0 %all_to_all.56.parts_ref = f32[8,12,128]{2,1,0:T(8,128)S(1)} all-to-all(f32[8,12,128]{2,1,0:T(8,128)S(1)} %get-tuple-element.31), channel_id=1, replica_groups=mesh['clip'=16,'cap'=8] {'cap'}, dimensions={0} | all-to-all | bytes 98304 | tf_op jit(solution)/shard_map/all_to_all | solution.py:361
  138.4 0.0 copy-done
  138.4 2.0 column_sums.3
  140.4 0.0 all-gather.5.cloned.1.call-done.text_hbm_ref
  140.4 11.6 %all_to_all.57.parts_ref = f32[16,24,128]{2,1,0:T(8,128)} all-to-all(f32[16,24,128]{2,1,0:T(8,128)S(1)} %column_sums.3), channel_id=1, replica_groups=mesh['clip'=16,'cap'=8] {'clip'}, dimensions={0} | all-to-all | bytes 393216 | tf_op jit(solution)/shard_map/all_to_all | solution.py:361
  152.0 20.9 %student_softmax.1 = (f32[2,1536,3072]{2,1,0:T(8,128)S(1)}, f32[24,128]{1,0:T(8,128)}) custom-call(bf16[1536,512]{1,0:T(8,128)(2,1)} %bitcast.5, bf16[3072,512]{1,0:T(8,128)(2,1)} %all-gather.5.cloned.1.call-done.text_hbm_ref, f32[1536,3072]{1,0:T(8,128)} %copy-done), custom_call_target="tpu_custom_call" | custom-call | tf_op jit(solution)/shard_map/student_softmax/pallas_call | solution.py:254
  172.9 3.4 %row_sums.5 = (f32[8,36,128]{2,1,0:T(8,128)}, f32[24,128]{1,0:T(8,128)}) custom-call(f32[16,24,128]{2,1,0:T(8,128)} %all_to_all.57.parts_ref, f32[2,1536,3072]{2,1,0:T(8,128)S(1)} %get-tuple-element.38.kernel_ref.pair_ref, f32[24,128]{1,0:T(8,128)} %get-tuple-element.39.stat_ref.own_ref), custom_call_target="tpu_custom_call" | custom-call | tf_op jit(solution)/shard_map/row_sums/pallas_call | solution.py:179
  176.3 10.5 %all_to_all.58.rows_ref = f32[8,36,128]{2,1,0:T(8,128)} all-to-all(f32[8,36,128]{2,1,0:T(8,128)} %get-tuple-element.40), channel_id=1, replica_groups=mesh['clip'=16,'cap'=8] {'cap'}, dimensions={0} | all-to-all | bytes 294912 | tf_op jit(solution)/shard_map/all_to_all | solution.py:361
  186.8 17.0 %residual_grads.1 = (f32[1536,512]{1,0:T(8,128)}, bf16[3072,512]{1,0:T(8,128)(2,1)S(1)}) custom-call(f32[8,36,128]{2,1,0:T(8,128)} %all_to_all.58.rows_ref, f32[24,128]{1,0:T(8,128)} %get-tuple-element.41.scale_ref, f32[24,128]{1,0:T(8,128)} %get-tuple-element.39.stat_ref.own_ref, f32[2,1536,3072]{2,1,0:T(8,128)S(1)} %get-tuple-element.38.kernel_ref.pair_ref, ...), custom_call_target="tpu_custom_call" | custom-call | tf_op jit(solution)/shard_map/residual_grads/pallas_call | solution.py:324
  203.8 0.0 reduce-scatter.2.cloned.1.call-update
  203.8 42.4 %all_to_all.59 = bf16[16,192,512]{2,1,0:T(8,128)(2,1)S(1)} all-to-all(bf16[16,192,512]{2,1,0:T(8,128)(2,1)S(1)} %bitcast.4), channel_id=1, replica_groups=mesh['clip'=16,'cap'=8] {'clip'}, dimensions={0} | all-to-all | bytes 6291456 | tf_op jit(solution)/shard_map/all_to_all | solution.py:361
  246.2 1.2 convert_reduce_fusion
  247.4 0.0 reduce-scatter.2.cloned.1.call-done
Async XLA Ops:
  7.2 28.9 %copy-start.1 = (bf16[192,512]{1,0:T(8,128)(2,1)S(1)}, bf16[192,512]{1,0:T(8,128)(2,1)}, u32[]{:S(2)}) copy-start(bf16[192,512]{1,0:T(8,128)(2,1)} %param.6) | copy-start | bytes 589828
  7.2 54.0 %all-gather.3.cloned.1.call-start = ((), (), s32[]{:S(2)}) async-start(), calls=%async_computation.11 | async-start | bytes 3342336 | tf_op jit(solution)/shard_map/all_gather | solution.py:365
  7.9 132.5 %all-gather.5.cloned.1.call-start = ((), (), s32[]{:S(2)}) async-start(), calls=%async_computation.12 | async-start | bytes 3342336 | tf_op jit(solution)/shard_map/all_gather | solution.py:370
  36.0 211.3 %reduce-scatter.2.cloned.1.call-start = ((), (), s32[]{:S(2)}) async-start(), calls=%async_computation.13 | async-start | bytes 3538944 | tf_op jit(solution)/shard_map/reduce_scatter | solution.py:384
  88.5 49.9 %copy-start = (f32[1536,3072]{1,0:T(8,128)}, f32[1536,3072]{1,0:T(8,128)S(1)}, u32[]{:S(2)}) copy-start(f32[1536,3072]{1,0:T(8,128)S(1)} %get-tuple-element.29.kernel_ref.kernel_hbm_ref) | copy-start | bytes 56623108
Sparse Core Ops, SparseCore 0:
  10.1 50.2 all-gather.2
  62.6 48.8 all-gather.4
  203.9 32.2 reduce-scatter.1

commit v4 on v3

--- a/solution.py
+++ b/solution.py
@@ -58,26 +58,33 @@
     return copies
 
 
-def multiply_chunk(j, audio_ref, text_ref, logits_ref, best_ref):
+def multiply_rows(audio_ref, text_ref, logits_ref, best_ref, copies, after_first):
     step = 256
-    at = pl.ds(j * WIDTH, WIDTH)
-
-    def block(i, _):
+
+    def block(i, waits):
         rows = pl.ds(pl.multiple_of(i * step, step), step)
-        x = 10.0 * contract_last(audio_ref[rows, :], text_ref[at, :])
-        logits_ref[rows, at] = x
-        folded = fold_lanes(x, jnp.maximum)
-        best_ref[rows, :] = folded if j == 0 else jnp.maximum(best_ref[rows, :], folded)
+        left = audio_ref[rows, :]
+        best = None
+        for j, copy in enumerate(copies):
+            if waits:
+                copy.wait()
+            at = pl.ds(j * WIDTH, WIDTH)
+            x = 10.0 * contract_last(left, text_ref[at, :])
+            logits_ref[rows, at] = x
+            folded = fold_lanes(x, jnp.maximum)
+            best = folded if best is None else jnp.maximum(best, folded)
+        best_ref[rows, :] = best
         return 0
 
-    lax.fori_loop(0, audio_ref.shape[0] // step, block, 0)
+    block(0, True)
+    after_first()
+    lax.fori_loop(1, audio_ref.shape[0] // step, lambda i, _: block(i, False), 0)
 
 
 def logits_kernel(audio_ref, text_hbm_ref, logits_ref, max_ref, text_ref, part_ref, sems):
     rows = logits_ref.shape[0]
-    for j, copy in enumerate(text_copies(text_hbm_ref, text_ref, sems)):
-        copy.wait()
-        multiply_chunk(j, audio_ref, text_ref, logits_ref, part_ref)
+    copies = text_copies(text_hbm_ref, text_ref, sems)
+    multiply_rows(audio_ref, text_ref, logits_ref, part_ref, copies, lambda: None)
     for b in range(rows // LANES):
         top = jnp.max(lanes_of(part_ref, b), axis=0, keepdims=True)
         for k in range(max_ref.shape[0]):
@@ -225,11 +232,8 @@
     rows, columns = exp_ref.shape
     blocks = rows // LANES
     kernel_copy = pltpu.make_async_copy(kernel_hbm_ref, kernel_ref, kernel_sem)
-    for j, copy in enumerate(text_copies(text_hbm_ref, text_ref, sems)):
-        copy.wait()
-        if j == 0:
-            kernel_copy.start()
-        multiply_chunk(j, audio_ref, text_ref, exp_ref, part_ref)
+    copies = text_copies(text_hbm_ref, text_ref, sems)
+    multiply_rows(audio_ref, text_ref, exp_ref, part_ref, copies, kernel_copy.start)
     for b in range(blocks):
         top = jnp.max(lanes_of(part_ref, b), axis=0, keepdims=True)
         stat_ref[b : b + 1, :] = top
@@ -271,8 +275,8 @@
 
 
 def residual_kernel(
-    rows_ref, scale_ref, own_ref, pair_ref, audio_hbm_ref, text_hbm_ref,
-    audio_out_ref, text_out_ref, weight_ref, prob_ref, residual_ref, audio_ref, text_ref, audio_sem, text_sem,
+    rows_ref, scale_ref, own_ref, pair_ref, audio_ref, text_ref,
+    audio_out_ref, text_out_ref, weight_ref, prob_ref, residual_ref,
 ):
     kernel_ref, exp_ref = pair_ref.at[0], pair_ref.at[1]
     step, depth = audio_out_ref.shape
@@ -280,13 +284,9 @@
     blocks = own_ref.shape[0] // 2
     groups = WIDTH // LANES
     i = pl.program_id(0)
-    audio_copy = pltpu.make_async_copy(audio_hbm_ref, audio_ref, audio_sem)
-    text_copy = pltpu.make_async_copy(text_hbm_ref, text_ref, text_sem)
 
     @pl.when(i == 0)
     def _():
-        text_copy.start()
-        audio_copy.start()
         spread_rows(1.0 / jnp.sum(rows_ref[:, :blocks, :], axis=0), weight_ref)
         tops = rows_ref[:, blocks : 2 * blocks, :]
         top = jnp.max(tops, axis=0)
@@ -301,12 +301,10 @@
         target = (repeat_lanes(weight_ref[at, :], groups) * kernel_ref[at, lanes]) * scale
         prob = exp_ref[at, lanes] * repeat_lanes(prob_ref[at, :], groups)
         residual_ref[at, lanes] = (prob - target).astype(jnp.bfloat16)
-    pl.when(i == 0)(text_copy.wait)
     audio_out_ref[...] = 10.0 * jnp.dot(residual_ref[at, :], text_ref[...], preferred_element_type=jnp.float32)
 
     @pl.when(i == pl.num_programs(0) - 1)
     def _():
-        audio_copy.wait()
         for j in range(columns // WIDTH):
             grad = lax.dot_general(
                 residual_ref[:, pl.ds(j * WIDTH, WIDTH)],
@@ -328,20 +326,16 @@
             jax.ShapeDtypeStruct((rows, depth), jnp.float32),
             pltpu.VMEM((columns, depth), dtype),
         ),
-        in_specs=[VMEM] * 4 + [HBM] * 2,
+        in_specs=[VMEM] * 6,
         out_specs=(pl.BlockSpec((step, depth), lambda i: (i, 0)), VMEM),
         scratch_shapes=[
             pltpu.VMEM((rows, LANES), jnp.float32),
             pltpu.VMEM((rows, LANES), jnp.float32),
             pltpu.VMEM((rows, columns), jnp.bfloat16),
-            pltpu.VMEM(audio.shape, audio.dtype),
-            pltpu.VMEM(text.shape, text.dtype),
-            pltpu.SemaphoreType.DMA,
-            pltpu.SemaphoreType.DMA,
         ],
         compiler_params=params(),
         name="residual_grads",
-    )(row_parts, scale, own, resident(pair), streamed(audio), streamed(text))
+    )(row_parts, scale, own, resident(pair), audio, text)
 
 
 def resident(x):

time: 255 us -> 240 us (0.941)
  Pallas kernels: 67.7 us -> 55.6 us
    pallas_call x1, Pallas kernels: 20.9 us -> 15.9 us  [student_softmax(): pl.pallas_call(student_kernel, out_shape=(pltpu.VMEM((2, rows, columns),...]
    pallas_call x1, Pallas kernels: 13.5 us -> 8.5 us  [teacher_logits(): pl.pallas_call(logits_kernel, out_shape=(pltpu.VMEM((rows, columns), jnp....]
  transfers between devices with their start and end apart: 3 -> 3, of which waited for: 0 -> 0; matrix products, arithmetic and copies ran while one was open for 1% -> 1% of each run, Pallas kernels for 10% -> 9%
where the time goes in v4:
time: 240 us
  blocking collectives  167 us (70%)
  Pallas kernels  55.6 us (23%)
  between operations  13.8 us (6%)
    all_to_all x8, blocking collectives, swap(): return lax.all_to_all(x, axis, 0, 0)  115 us
    all_to_all x2, blocking collectives, gather_a2a(): lax.all_to_all(spread, axis, 0, 0).reshape(n * x.shape[0], x.shape[1])  52 us
    pallas_call x1, Pallas kernels, student_softmax(): pl.pallas_call(student_kernel, out_shape=(pltpu.VMEM((2, rows, columns),...  15.9 us
    pallas_call x1, Pallas kernels, residual_grads(): pl.pallas_call(residual_kernel, grid=(rows // step,), out_shape=(jax.Shap...  14.9 us
    pallas_call x1, Pallas kernels, teacher_logits(): pl.pallas_call(logits_kernel, out_shape=(pltpu.VMEM((rows, columns), jnp....  8.5 us
    pallas_call x3, Pallas kernels, row_sums(): pl.pallas_call(body, out_shape=(jax.ShapeDtypeStruct((peers, rows // LANE...  7.7 us
  transfers between devices with their start and end apart: 3, of which 0 were waited for; matrix products, arithmetic and copies ran while one was open for 1% of the time, Pallas kernels for 9%

profile of v4, /device:TPU:0, one launch (start us, length us, event | category | flops | bytes accessed | tf_op | source)
XLA Modules:
  0.0 239.6 jit_solution(17806954452122134315)
XLA Ops:
  7.2 0.0 copy-start.1
  7.2 0.0 all-gather.3.cloned.1.call-start
  7.2 0.7 all-gather.3.cloned.1.call-update
  7.9 0.0 all-gather.5.cloned.1.call-start
  8.0 1.1 broadcast_in_dim.4
  9.0 27.0 %all_to_all.50 = bf16[8,192,512]{2,1,0:T(8,128)(2,1)S(1)} all-to-all(bf16[8,192,512]{2,1,0:T(8,128)(2,1)S(1)} %broadcast_in_dim.4), channel_id=1, replica_groups=mesh['clip'=16,'cap'=8] {'cap'}, dimensions={0} | all-to-all | bytes 3145728 | tf_op jit(solution)/shard_map/all_to_all | solution.py:351
  36.0 0.0 all-gather.5.cloned.1.call-update
  36.0 0.0 reduce-scatter.2.cloned.1.call-start
  36.1 0.0 copy-done.1
  36.1 0.1 broadcast_in_dim.5
  36.2 25.0 %all_to_all.51 = bf16[8,192,512]{2,1,0:T(8,128)(2,1)} all-to-all(bf16[8,192,512]{2,1,0:T(8,128)(2,1)S(1)} %broadcast_in_dim.5), channel_id=1, replica_groups=mesh['clip'=16,'cap'=8] {'cap'}, dimensions={0} | all-to-all | bytes 3145728 | tf_op jit(solution)/shard_map/all_to_all | solution.py:351
  61.2 0.0 all-gather.3.cloned.1.call-done.text_hbm_ref
  61.2 8.5 %logits.1 = (f32[1536,3072]{1,0:T(8,128)S(1)}, f32[8,12,128]{2,1,0:T(8,128)S(1)}) custom-call(bf16[1536,512]{1,0:T(8,128)(2,1)S(1)} %bitcast.3, bf16[3072,512]{1,0:T(8,128)(2,1)} %all-gather.3.cloned.1.call-done.text_hbm_ref), custom_call_target="tpu_custom_call" | custom-call | tf_op jit(solution)/shard_map/logits/pallas_call | solution.py:96
  69.7 9.1 %all_to_all.52.max_ref = f32[8,12,128]{2,1,0:T(8,128)S(1)} all-to-all(f32[8,12,128]{2,1,0:T(8,128)S(1)} %get-tuple-element.26), channel_id=1, replica_groups=mesh['clip'=16,'cap'=8] {'cap'}, dimensions={0} | all-to-all | bytes 98304 | tf_op jit(solution)/shard_map/all_to_all | solution.py:355
  78.8 4.6 %exp_columns.1 = (f32[1536,3072]{1,0:T(8,128)S(1)}, f32[16,24,128]{2,1,0:T(8,128)S(1)}) custom-call(f32[8,12,128]{2,1,0:T(8,128)S(1)} %all_to_all.52.max_ref, f32[1536,3072]{1,0:T(8,128)S(1)} %get-tuple-element.27.logits_ref), custom_call_target="tpu_custom_call", output_to_operand_aliasing={{0}: (1, {})} | custom-call | tf_op jit(solution)/shard_map/exp_columns/pallas_call | solution.py:139
  83.5 0.0 copy-start
  83.5 14.1 %all_to_all.53.parts_ref = f32[16,24,128]{2,1,0:T(8,128)S(1)} all-to-all(f32[16,24,128]{2,1,0:T(8,128)S(1)} %get-tuple-element.28), channel_id=1, replica_groups=mesh['clip'=16,'cap'=8] {'clip'}, dimensions={0} | all-to-all | bytes 393216 | tf_op jit(solution)/shard_map/all_to_all | solution.py:355
  97.6 2.1 row_sums.3
  99.7 8.0 %all_to_all.54.parts_ref = f32[8,12,128]{2,1,0:T(8,128)S(1)} all-to-all(f32[8,12,128]{2,1,0:T(8,128)S(1)} %get-tuple-element.30), channel_id=1, replica_groups=mesh['clip'=16,'cap'=8] {'cap'}, dimensions={0} | all-to-all | bytes 98304 | tf_op jit(solution)/shard_map/all_to_all | solution.py:355
  107.7 2.0 column_sums.2
  109.7 11.3 %all_to_all.55.parts_ref = f32[16,24,128]{2,1,0:T(8,128)S(1)} all-to-all(f32[16,24,128]{2,1,0:T(8,128)S(1)} %column_sums.2), channel_id=1, replica_groups=mesh['clip'=16,'cap'=8] {'clip'}, dimensions={0} | all-to-all | bytes 393216 | tf_op jit(solution)/shard_map/all_to_all | solution.py:355
  121.0 2.1 row_sums.4
  123.2 8.0 %all_to_all.56.parts_ref = f32[8,12,128]{2,1,0:T(8,128)S(1)} all-to-all(f32[8,12,128]{2,1,0:T(8,128)S(1)} %get-tuple-element.31), channel_id=1, replica_groups=mesh['clip'=16,'cap'=8] {'cap'}, dimensions={0} | all-to-all | bytes 98304 | tf_op jit(solution)/shard_map/all_to_all | solution.py:355
  131.1 0.0 copy-done
  131.1 2.0 column_sums.3
  133.1 0.0 all-gather.5.cloned.1.call-done.text_hbm_ref.text_ref
  133.2 11.6 %all_to_all.57.parts_ref = f32[16,24,128]{2,1,0:T(8,128)} all-to-all(f32[16,24,128]{2,1,0:T(8,128)S(1)} %column_sums.3), channel_id=1, replica_groups=mesh['clip'=16,'cap'=8] {'clip'}, dimensions={0} | all-to-all | bytes 393216 | tf_op jit(solution)/shard_map/all_to_all | solution.py:355
  144.8 15.9 %student_softmax.1 = (f32[2,1536,3072]{2,1,0:T(8,128)S(1)}, f32[24,128]{1,0:T(8,128)}) custom-call(bf16[1536,512]{1,0:T(8,128)(2,1)} %bitcast.5, bf16[3072,512]{1,0:T(8,128)(2,1)} %all-gather.5.cloned.1.call-done.text_hbm_ref.text_ref, f32[1536,3072]{1,0:T(8,128)} %copy-done), custom_call_target="tpu_custom_call" | custom-call | tf_op jit(solution)/shard_map/student_softmax/pallas_call | solution.py:258
  160.6 3.4 %row_sums.5 = (f32[8,36,128]{2,1,0:T(8,128)}, f32[24,128]{1,0:T(8,128)}) custom-call(f32[16,24,128]{2,1,0:T(8,128)} %all_to_all.57.parts_ref, f32[2,1536,3072]{2,1,0:T(8,128)S(1)} %get-tuple-element.38.kernel_ref.pair_ref, f32[24,128]{1,0:T(8,128)} %get-tuple-element.39.stat_ref.own_ref), custom_call_target="tpu_custom_call" | custom-call | tf_op jit(solution)/shard_map/row_sums/pallas_call | solution.py:186
  164.0 10.5 %all_to_all.58.rows_ref = f32[8,36,128]{2,1,0:T(8,128)} all-to-all(f32[8,36,128]{2,1,0:T(8,128)} %get-tuple-element.40), channel_id=1, replica_groups=mesh['clip'=16,'cap'=8] {'cap'}, dimensions={0} | all-to-all | bytes 294912 | tf_op jit(solution)/shard_map/all_to_all | solution.py:355
  174.5 14.9 %residual_grads.1 = (f32[1536,512]{1,0:T(8,128)}, bf16[3072,512]{1,0:T(8,128)(2,1)S(1)}) custom-call(f32[8,36,128]{2,1,0:T(8,128)} %all_to_all.58.rows_ref, f32[24,128]{1,0:T(8,128)} %get-tuple-element.41.scale_ref, f32[24,128]{1,0:T(8,128)} %get-tuple-element.39.stat_ref.own_ref, f32[2,1536,3072]{2,1,0:T(8,128)S(1)} %get-tuple-element.38.kernel_ref.pair_ref, ...), custom_call_target="tpu_custom_call" | custom-call | tf_op jit(solution)/shard_map/residual_grads/pallas_call | solution.py:322
  189.5 0.0 reduce-scatter.2.cloned.1.call-update
  189.5 42.4 %all_to_all.59 = bf16[16,192,512]{2,1,0:T(8,128)(2,1)S(1)} all-to-all(bf16[16,192,512]{2,1,0:T(8,128)(2,1)S(1)} %bitcast.4), channel_id=1, replica_groups=mesh['clip'=16,'cap'=8] {'clip'}, dimensions={0} | all-to-all | bytes 6291456 | tf_op jit(solution)/shard_map/all_to_all | solution.py:355
  231.9 1.2 convert_reduce_fusion
  233.0 0.0 reduce-scatter.2.cloned.1.call-done
Async XLA Ops:
  7.2 28.9 %copy-start.1 = (bf16[192,512]{1,0:T(8,128)(2,1)S(1)}, bf16[192,512]{1,0:T(8,128)(2,1)}, u32[]{:S(2)}) copy-start(bf16[192,512]{1,0:T(8,128)(2,1)} %param.6) | copy-start | bytes 589828
  7.2 54.0 %all-gather.3.cloned.1.call-start = ((), (), s32[]{:S(2)}) async-start(), calls=%async_computation.11 | async-start | bytes 3342336 | tf_op jit(solution)/shard_map/all_gather | solution.py:359
  7.9 125.2 %all-gather.5.cloned.1.call-start = ((), (), s32[]{:S(2)}) async-start(), calls=%async_computation.12 | async-start | bytes 3342336 | tf_op jit(solution)/shard_map/all_gather | solution.py:364
  36.0 197.0 %reduce-scatter.2.cloned.1.call-start = ((), (), s32[]{:S(2)}) async-start(), calls=%async_computation.13 | async-start | bytes 3538944 | tf_op jit(solution)/shard_map/reduce_scatter | solution.py:378
  83.5 47.7 %copy-start = (f32[1536,3072]{1,0:T(8,128)}, f32[1536,3072]{1,0:T(8,128)S(1)}, u32[]{:S(2)}) copy-start(f32[1536,3072]{1,0:T(8,128)S(1)} %get-tuple-element.29.kernel_ref.kernel_hbm_ref) | copy-start | bytes 56623108
Sparse Core Ops, SparseCore 0:
  10.1 50.2 all-gather.2
  62.6 46.9 all-gather.4
  189.6 32.2 reduce-scatter.1

commit v5 on v4

--- a/solution.py
+++ b/solution.py
@@ -11,7 +11,6 @@
 LANES = 128
 WIDTH = 512
 VMEM = pl.BlockSpec(memory_space=pltpu.VMEM)
-HBM = pl.BlockSpec(memory_space=pltpu.HBM)
 LIMIT = 19 * 1024 * 1024
 
 
@@ -50,48 +49,31 @@
     return lax.dot_general(left, right, (((1,), (1,)), ((), ())), preferred_element_type=jnp.float32)
 
 
-def text_copies(from_ref, to_ref, sems):
-    chunks = [pl.ds(j * WIDTH, WIDTH) for j in range(to_ref.shape[0] // WIDTH)]
-    copies = [pltpu.make_async_copy(from_ref.at[c], to_ref.at[c], sems.at[j]) for j, c in enumerate(chunks)]
-    for copy in copies:
-        copy.start()
-    return copies
-
-
-def multiply_rows(audio_ref, text_ref, logits_ref, best_ref, copies, after_first):
+def logits_kernel(audio_ref, text_ref, probe_ref, logits_ref, max_ref, part_ref):
+    rows, columns = logits_ref.shape
     step = 256
 
-    def block(i, waits):
-        rows = pl.ds(pl.multiple_of(i * step, step), step)
-        left = audio_ref[rows, :]
+    def block(i, _):
+        base = pl.multiple_of(i * step, step)
+        left = audio_ref[pl.ds(base, step), :]
         best = None
-        for j, copy in enumerate(copies):
-            if waits:
-                copy.wait()
-            at = pl.ds(j * WIDTH, WIDTH)
-            x = 10.0 * contract_last(left, text_ref[at, :])
-            logits_ref[rows, at] = x
+        for j in range(columns // WIDTH):
+            at = j * WIDTH
+            x = 10.0 * contract_last(left, text_ref[pl.ds(at, WIDTH), :])
+            logits_ref[pl.ds(base, step), pl.ds(at, WIDTH)] = x
             folded = fold_lanes(x, jnp.maximum)
             best = folded if best is None else jnp.maximum(best, folded)
-        best_ref[rows, :] = best
+        part_ref[pl.ds(base, step), :] = best
         return 0
 
-    block(0, True)
-    after_first()
-    lax.fori_loop(1, audio_ref.shape[0] // step, lambda i, _: block(i, False), 0)
-
-
-def logits_kernel(audio_ref, text_hbm_ref, logits_ref, max_ref, text_ref, part_ref, sems):
-    rows = logits_ref.shape[0]
-    copies = text_copies(text_hbm_ref, text_ref, sems)
-    multiply_rows(audio_ref, text_ref, logits_ref, part_ref, copies, lambda: None)
+    lax.fori_loop(0, rows // step, block, 0)
     for b in range(rows // LANES):
         top = jnp.max(lanes_of(part_ref, b), axis=0, keepdims=True)
         for k in range(max_ref.shape[0]):
             max_ref[k, b : b + 1, :] = top
 
 
-def teacher_logits(audio, text, peers):
+def teacher_logits(audio, text, probe, peers):
     rows, columns = audio.shape[0], text.shape[0]
     return pl.pallas_call(
         logits_kernel,
@@ -99,16 +81,12 @@
             pltpu.VMEM((rows, columns), jnp.float32),
             jax.ShapeDtypeStruct((peers, rows // LANES, LANES), jnp.float32),
         ),
-        in_specs=[VMEM, HBM],
+        in_specs=[VMEM, VMEM, VMEM],
         out_specs=(VMEM, VMEM),
-        scratch_shapes=[
-            pltpu.VMEM(text.shape, text.dtype),
-            pltpu.VMEM((rows, LANES), jnp.float32),
-            pltpu.SemaphoreType.DMA((columns // WIDTH,)),
-        ],
+        scratch_shapes=[pltpu.VMEM((rows, LANES), jnp.float32)],
         compiler_params=params(),
         name="logits",
-    )(audio, streamed(text))
+    )(audio, text, probe)
 
 
 def put_columns(acc, sum_ref, out_ref):
@@ -225,50 +203,56 @@
     )(parts, resident(kernel))
 
 
-def student_kernel(
-    audio_ref, text_hbm_ref, kernel_hbm_ref, pair_ref, stat_ref, text_ref, part_ref, sems, kernel_sem
-):
+def student_kernel(audio_ref, text_hbm_ref, kernel_hbm_ref, pair_ref, stat_ref, text_ref, text_sem, kernel_sem):
     kernel_ref, exp_ref = pair_ref.at[0], pair_ref.at[1]
-    rows, columns = exp_ref.shape
+    rows, columns = pair_ref.shape[1:]
+    text_copy = pltpu.make_async_copy(text_hbm_ref, text_ref, text_sem)
+    kernel_copy = pltpu.make_async_copy(kernel_hbm_ref, kernel_ref, kernel_sem)
+    text_copy.start()
+    text_copy.wait()
+    kernel_copy.start()
+    step = 256
+    here = step // LANES
     blocks = rows // LANES
-    kernel_copy = pltpu.make_async_copy(kernel_hbm_ref, kernel_ref, kernel_sem)
-    copies = text_copies(text_hbm_ref, text_ref, sems)
-    multiply_rows(audio_ref, text_ref, exp_ref, part_ref, copies, kernel_copy.start)
-    for b in range(blocks):
-        top = jnp.max(lanes_of(part_ref, b), axis=0, keepdims=True)
-        stat_ref[b : b + 1, :] = top
-        part_ref[pl.ds(b * LANES, LANES), :] = jnp.broadcast_to(top, (LANES, LANES)).T
-
-    def step(i, _):
-        at = pl.ds(pl.multiple_of(i * 8, 8), 8)
-        e = jnp.exp(exp_ref[at, :] - repeat_lanes(part_ref[at, :], columns // LANES))
-        exp_ref[at, :] = e
-        part_ref[at, :] = fold_lanes(e, jnp.add)
+
+    def block(i, _):
+        base = pl.multiple_of(i * step, step)
+        left = audio_ref[pl.ds(base, step), :]
+        best = None
+        for j in range(columns // WIDTH):
+            x = 10.0 * contract_last(left, text_ref[pl.ds(j * WIDTH, WIDTH), :])
+            exp_ref[pl.ds(base, step), pl.ds(j * WIDTH, WIDTH)] = x
+            folded = fold_lanes(x, jnp.maximum)
+            best = folded if best is None else jnp.maximum(best, folded)
+        for b in range(here):
+            at = pl.ds(pl.multiple_of(base + b * LANES, LANES), LANES)
+            top = jnp.max(best[b * LANES : (b + 1) * LANES, :].T, axis=0, keepdims=True)
+            stat_ref[pl.ds(i * here + b, 1), :] = top
+            top = repeat_lanes(jnp.broadcast_to(top, (LANES, LANES)).T, WIDTH // LANES)
+            total = None
+            for j in range(columns // WIDTH):
+                e = jnp.exp(exp_ref[at, pl.ds(j * WIDTH, WIDTH)] - top)
+                exp_ref[at, pl.ds(j * WIDTH, WIDTH)] = e
+                folded = fold_lanes(e, jnp.add)
+                total = folded if total is None else total + folded
+            stat_ref[pl.ds(blocks + i * here + b, 1), :] = jnp.sum(total.T, axis=0, keepdims=True)
         return 0
 
-    lax.fori_loop(0, rows // 8, step, 0, unroll=4)
-    for b in range(blocks):
-        total = jnp.sum(lanes_of(part_ref, b), axis=0, keepdims=True)
-        stat_ref[blocks + b : blocks + b + 1, :] = total
+    lax.fori_loop(0, rows // step, block, 0)
     kernel_copy.wait()
 
 
 def student_softmax(audio, text, kernel):
-    rows, columns = audio.shape[0], text.shape[0]
+    rows, columns, depth = audio.shape[0], text.shape[0], audio.shape[1]
     return pl.pallas_call(
         student_kernel,
         out_shape=(
             pltpu.VMEM((2, rows, columns), jnp.float32),
             jax.ShapeDtypeStruct((2 * (rows // LANES), LANES), jnp.float32),
         ),
-        in_specs=[VMEM, HBM, HBM],
+        in_specs=[VMEM, pl.BlockSpec(memory_space=pltpu.HBM), pl.BlockSpec(memory_space=pltpu.HBM)],
         out_specs=(VMEM, VMEM),
-        scratch_shapes=[
-            pltpu.VMEM(text.shape, text.dtype),
-            pltpu.VMEM((rows, LANES), jnp.float32),
-            pltpu.SemaphoreType.DMA((columns // WIDTH,)),
-            pltpu.SemaphoreType.DMA,
-        ],
+        scratch_shapes=[pltpu.VMEM(text.shape, text.dtype), pltpu.SemaphoreType.DMA, pltpu.SemaphoreType.DMA],
         compiler_params=params(),
         name="student_softmax",
     )(audio, streamed(text), streamed(kernel))
@@ -333,7 +317,7 @@
             pltpu.VMEM((rows, LANES), jnp.float32),
             pltpu.VMEM((rows, columns), jnp.bfloat16),
         ],
-        compiler_params=params(),
+        compiler_params=params(19 * 1024 * 1024),
         name="residual_grads",
     )(row_parts, scale, own, resident(pair), audio, text)
 
@@ -356,18 +340,21 @@
 
 
 def body(clips, caps, teacher_audio, teacher_text, student_audio, student_text):
-    text_t = lax.all_gather(teacher_text, "clip", axis=0, tiled=True)
-    audio_t = gather_a2a(teacher_audio, "cap", caps)
-    student_audio, student_text, audio_t = lax.optimization_barrier((student_audio, student_text, audio_t))
-    audio_s = gather_a2a(student_audio, "cap", caps)
-    audio_s, text_t = lax.optimization_barrier((audio_s, text_t))
+    count, depth = teacher_audio.shape
+    audio = jnp.concatenate([teacher_audio, student_audio], axis=0)
+    audio = lax.all_gather(audio, "cap", axis=0)
+    text_t = gather_a2a(teacher_text, "clip", clips)
+    probe = text_t[:16, :LANES]
+    student_text, probe = lax.optimization_barrier((student_text, probe))
     text_s = lax.all_gather(student_text, "clip", axis=0, tiled=True)
-    logits, maxima = teacher_logits(audio_t, text_t, caps)
+    audio_t = audio[:, :count].reshape(-1, depth)
+    audio_s = audio[:, count:].reshape(-1, depth)
+    logits, maxima = teacher_logits(audio_t, text_t, probe, caps)
     kernel, columns = exp_columns(swap(maxima, "cap"), logits, clips)
     for _ in range(ITERS - 1):
         row_parts, _ = row_sums(swap(columns, "clip"), kernel, caps)
         columns = column_sums(swap(row_parts, "cap"), kernel, clips)
-    columns, text_s = lax.optimization_barrier((columns, text_s))
+    columns, text_s, audio_s = lax.optimization_barrier((columns, text_s, audio_s))
     columns, audio_s = lax.optimization_barrier((swap(columns, "clip"), audio_s))
     pair, stats = student_softmax(audio_s, text_s, kernel)
     row_parts, scale = row_sums(columns, pair, caps, stats)

time: 240 us -> 235 us (0.979)
  blocking collectives: 167 us -> 162 us
  Pallas kernels: 55.6 us -> 51.4 us
  local copies, waits for them, and re-layouts: 1.19 us -> 4.6 us
    all_to_all x2 -> x1, blocking collectives: 52 us -> 46.5 us  [gather_a2a(): lax.all_to_all(spread, axis, 0, 0).reshape(n * x.shape[0], x.shape[1])]
    slice x0 -> x2, local copies, waits for them, and re-layouts: none -> 3.37 us  [the longest x1 3.37 us: body(): audio_s = audio[:, count:].reshape(-1, depth)]
  transfers between devices with their start and end apart: 3 -> 3, of which waited for: 0 -> 0; matrix products, arithmetic and copies ran while one was open for 1% -> 2% of each run, Pallas kernels for 9% -> 8%
where the time goes in v5:
time: 235 us
  blocking collectives  162 us (69%)
  Pallas kernels  51.4 us (22%)
  between operations  13.8 us (6%)
  local copies, waits for them, and re-layouts  4.6 us (2%)
  other arithmetic  2.97 us (1%)
    all_to_all x8, blocking collectives, swap(): return lax.all_to_all(x, axis, 0, 0)  115 us
    all_to_all x1, blocking collectives, gather_a2a(): lax.all_to_all(spread, axis, 0, 0).reshape(n * x.shape[0], x.shape[1])  46.5 us
    pallas_call x1, Pallas kernels, residual_grads(): pl.pallas_call(residual_kernel, grid=(rows // step,), out_shape=(jax.Shap...  14.9 us
    pallas_call x1, Pallas kernels, student_softmax(): pl.pallas_call(student_kernel, out_shape=(pltpu.VMEM((2, rows, columns),...  13.7 us
    pallas_call x3, Pallas kernels, row_sums(): pl.pallas_call(body, out_shape=(jax.ShapeDtypeStruct((peers, rows // LANE...  7.7 us
    pallas_call x1, Pallas kernels, teacher_logits(): pl.pallas_call(logits_kernel, out_shape=(pltpu.VMEM((rows, columns), jnp....  6.39 us
  transfers between devices with their start and end apart: 3, of which 0 were waited for; matrix products, arithmetic and copies ran while one was open for 2% of the time, Pallas kernels for 8%

profile of v5, /device:TPU:0, one launch (start us, length us, event | category | flops | bytes accessed | tf_op | source)
XLA Modules:
  0.0 234.8 jit_solution(18312021506427991075)
XLA Ops:
  7.2 0.0 all-gather.6.cloned.1.call-start
  7.2 1.8 pad_maximum_fusion
  9.0 0.0 all-gather.6.cloned.1.call-update
  9.0 0.0 all-gather.4.cloned.1.call-start
  9.1 1.2 broadcast_in_dim.2
  10.3 46.5 %all_to_all.45 = bf16[16,192,512]{2,1,0:T(8,128)(2,1)S(1)} all-to-all(bf16[16,192,512]{2,1,0:T(8,128)(2,1)S(1)} %broadcast_in_dim.2), channel_id=1, replica_groups=mesh['clip'=16,'cap'=8] {'clip'}, dimensions={0} | all-to-all | bytes 6291456 | tf_op jit(solution)/shard_map/all_to_all | solution.py:335
  56.9 0.0 all-gather.4.cloned.1.call-update
  56.9 0.0 reduce-scatter.2.cloned.1.call-start
  56.9 0.0 all-gather.6.cloned.1.call-done
  57.0 3.4 %fusion = (bf16[8,192,512]{2,1,0:T(8,128)(2,1)}, bf16[8,192,512]{2,1,0:T(8,128)(2,1)S(1)}) fusion(bf16[8,384,512]{2,1,0:T(8,128)(2,1)} %bitcast.11), kind=kLoop, calls=%fused_computation.2 | loop fusion | bytes 6291456 | tf_op jit(solution)/shard_map/slice | solution.py:351
  60.3 6.4 %logits.1 = (f32[1536,3072]{1,0:T(8,128)S(1)}, f32[8,12,128]{2,1,0:T(8,128)S(1)}) custom-call(bf16[1536,512]{1,0:T(8,128)(2,1)S(1)} %bitcast.7, bf16[3072,512]{1,0:T(8,128)(2,1)S(1)} %bitcast.6, bf16[16,128]{1,0:T(8,128)(2,1)S(1)} %slice.13.probe_ref), custom_call_target="tpu_custom_call" | custom-call | tf_op jit(solution)/shard_map/logits/pallas_call | solution.py:78
  66.7 10.7 %all_to_all.46.max_ref = f32[8,12,128]{2,1,0:T(8,128)S(1)} all-to-all(f32[8,12,128]{2,1,0:T(8,128)S(1)} %get-tuple-element.22), channel_id=1, replica_groups=mesh['clip'=16,'cap'=8] {'cap'}, dimensions={0} | all-to-all | bytes 98304 | tf_op jit(solution)/shard_map/all_to_all | solution.py:339
  77.5 4.6 %exp_columns.1 = (f32[1536,3072]{1,0:T(8,128)S(1)}, f32[16,24,128]{2,1,0:T(8,128)S(1)}) custom-call(f32[8,12,128]{2,1,0:T(8,128)S(1)} %all_to_all.46.max_ref, f32[1536,3072]{1,0:T(8,128)S(1)} %get-tuple-element.23.logits_ref), custom_call_target="tpu_custom_call", output_to_operand_aliasing={{0}: (1, {})} | custom-call | tf_op jit(solution)/shard_map/exp_columns/pallas_call | solution.py:117
  82.1 0.0 copy-start
  82.1 13.2 %all_to_all.47.parts_ref = f32[16,24,128]{2,1,0:T(8,128)S(1)} all-to-all(f32[16,24,128]{2,1,0:T(8,128)S(1)} %get-tuple-element.24), channel_id=1, replica_groups=mesh['clip'=16,'cap'=8] {'clip'}, dimensions={0} | all-to-all | bytes 393216 | tf_op jit(solution)/shard_map/all_to_all | solution.py:339
  95.3 2.1 row_sums.3
  97.4 8.0 %all_to_all.48.parts_ref = f32[8,12,128]{2,1,0:T(8,128)S(1)} all-to-all(f32[8,12,128]{2,1,0:T(8,128)S(1)} %get-tuple-element.26), channel_id=1, replica_groups=mesh['clip'=16,'cap'=8] {'cap'}, dimensions={0} | all-to-all | bytes 98304 | tf_op jit(solution)/shard_map/all_to_all | solution.py:339
  105.4 2.0 column_sums.2
  107.4 11.0 %all_to_all.49.parts_ref = f32[16,24,128]{2,1,0:T(8,128)S(1)} all-to-all(f32[16,24,128]{2,1,0:T(8,128)S(1)} %column_sums.2), channel_id=1, replica_groups=mesh['clip'=16,'cap'=8] {'clip'}, dimensions={0} | all-to-all | bytes 393216 | tf_op jit(solution)/shard_map/all_to_all | solution.py:339
  118.4 2.1 row_sums.4
  120.5 8.0 %all_to_all.50.parts_ref = f32[8,12,128]{2,1,0:T(8,128)S(1)} all-to-all(f32[8,12,128]{2,1,0:T(8,128)S(1)} %get-tuple-element.27), channel_id=1, replica_groups=mesh['clip'=16,'cap'=8] {'cap'}, dimensions={0} | all-to-all | bytes 98304 | tf_op jit(solution)/shard_map/all_to_all | solution.py:339
  128.5 0.0 copy-done
  128.5 2.0 column_sums.3
  130.5 0.0 all-gather.4.cloned.1.call-done.text_hbm_ref.text_ref
  130.5 11.6 %all_to_all.51.parts_ref = f32[16,24,128]{2,1,0:T(8,128)} all-to-all(f32[16,24,128]{2,1,0:T(8,128)S(1)} %column_sums.3), channel_id=1, replica_groups=mesh['clip'=16,'cap'=8] {'clip'}, dimensions={0} | all-to-all | bytes 393216 | tf_op jit(solution)/shard_map/all_to_all | solution.py:339
  142.2 13.7 %student_softmax.1 = (f32[2,1536,3072]{2,1,0:T(8,128)S(1)}, f32[24,128]{1,0:T(8,128)}) custom-call(bf16[1536,512]{1,0:T(8,128)(2,1)} %bitcast.9, bf16[3072,512]{1,0:T(8,128)(2,1)} %all-gather.4.cloned.1.call-done.text_hbm_ref.text_ref, f32[1536,3072]{1,0:T(8,128)} %copy-done), custom_call_target="tpu_custom_call" | custom-call | tf_op jit(solution)/shard_map/student_softmax/pallas_call | solution.py:247
  155.9 3.4 %row_sums.5 = (f32[8,36,128]{2,1,0:T(8,128)}, f32[24,128]{1,0:T(8,128)}) custom-call(f32[16,24,128]{2,1,0:T(8,128)} %all_to_all.51.parts_ref, f32[2,1536,3072]{2,1,0:T(8,128)S(1)} %get-tuple-element.34.kernel_ref.pair_ref, f32[24,128]{1,0:T(8,128)} %get-tuple-element.35.stat_ref.own_ref), custom_call_target="tpu_custom_call" | custom-call | tf_op jit(solution)/shard_map/row_sums/pallas_call | solution.py:164
  159.3 10.5 %all_to_all.52.rows_ref = f32[8,36,128]{2,1,0:T(8,128)} all-to-all(f32[8,36,128]{2,1,0:T(8,128)} %get-tuple-element.36), channel_id=1, replica_groups=mesh['clip'=16,'cap'=8] {'cap'}, dimensions={0} | all-to-all | bytes 294912 | tf_op jit(solution)/shard_map/all_to_all | solution.py:339
  169.8 14.9 %residual_grads.1 = (f32[1536,512]{1,0:T(8,128)}, bf16[3072,512]{1,0:T(8,128)(2,1)S(1)}) custom-call(f32[8,36,128]{2,1,0:T(8,128)} %all_to_all.52.rows_ref, f32[24,128]{1,0:T(8,128)} %get-tuple-element.37.scale_ref, f32[24,128]{1,0:T(8,128)} %get-tuple-element.35.stat_ref.own_ref, f32[2,1536,3072]{2,1,0:T(8,128)S(1)} %get-tuple-element.34.kernel_ref.pair_ref, ...), custom_call_target="tpu_custom_call" | custom-call | tf_op jit(solution)/shard_map/residual_grads/pallas_call | solution.py:306
  184.7 0.0 reduce-scatter.2.cloned.1.call-update
  184.7 42.4 %all_to_all.53 = bf16[16,192,512]{2,1,0:T(8,128)(2,1)S(1)} all-to-all(bf16[16,192,512]{2,1,0:T(8,128)(2,1)S(1)} %bitcast.8), channel_id=1, replica_groups=mesh['clip'=16,'cap'=8] {'clip'}, dimensions={0} | all-to-all | bytes 6291456 | tf_op jit(solution)/shard_map/all_to_all | solution.py:339
  227.1 1.2 convert_reduce_fusion
  228.3 0.0 reduce-scatter.2.cloned.1.call-done
  (1 shorter events, 0.0 us)
Async XLA Ops:
  7.2 49.8 %all-gather.6.cloned.1.call-start = ((), (), s32[]{:S(2)}) async-start(), calls=%async_computation.12 | async-start | bytes 3538944 | tf_op jit(solution)/shard_map/all_gather | solution.py:345
  9.0 121.5 %all-gather.4.cloned.1.call-start = ((), (), s32[]{:S(2)}) async-start(), calls=%async_computation.10 | async-start | bytes 3342336 | tf_op jit(solution)/shard_map/all_gather | solution.py:349
  56.9 171.4 %reduce-scatter.2.cloned.1.call-start = ((), (), s32[]{:S(2)}) async-start(), calls=%async_computation.11 | async-start | bytes 3538944 | tf_op jit(solution)/shard_map/reduce_scatter | solution.py:365
  82.1 46.4 %copy-start = (f32[1536,3072]{1,0:T(8,128)}, f32[1536,3072]{1,0:T(8,128)S(1)}, u32[]{:S(2)}) copy-start(f32[1536,3072]{1,0:T(8,128)S(1)} %get-tuple-element.25.kernel_ref.kernel_hbm_ref) | copy-start | bytes 56623108
Sparse Core Ops, SparseCore 0:
  10.3 30.4 all-gather.5
  57.0 47.8 all-gather.3
  184.9 32.3 reduce-scatter.1

commit v6 on v5

--- a/solution.py
+++ b/solution.py
@@ -51,11 +51,11 @@
 
 def logits_kernel(audio_ref, text_ref, probe_ref, logits_ref, max_ref, part_ref):
     rows, columns = logits_ref.shape
-    step = 256
+    step = 2 * audio_ref.shape[1]
 
     def block(i, _):
         base = pl.multiple_of(i * step, step)
-        left = audio_ref[pl.ds(base, step), :]
+        left = audio_ref[pl.ds(2 * i, 2)].reshape(step, audio_ref.shape[2])
         best = None
         for j in range(columns // WIDTH):
             at = j * WIDTH
@@ -73,20 +73,26 @@
             max_ref[k, b : b + 1, :] = top
 
 
+def audio_half(audio, half):
+    shards, count, depth = audio.shape
+    return pl.BlockSpec((shards, count // 2, depth), lambda i: (0, half, 0), pipeline_mode=pl.Buffered(1))
+
+
 def teacher_logits(audio, text, probe, peers):
-    rows, columns = audio.shape[0], text.shape[0]
+    rows, columns = audio.shape[0] * audio.shape[1] // 2, text.shape[0]
     return pl.pallas_call(
         logits_kernel,
+        grid=(1,),
         out_shape=(
             pltpu.VMEM((rows, columns), jnp.float32),
             jax.ShapeDtypeStruct((peers, rows // LANES, LANES), jnp.float32),
         ),
-        in_specs=[VMEM, VMEM, VMEM],
+        in_specs=[audio_half(audio, 0), VMEM, VMEM],
         out_specs=(VMEM, VMEM),
         scratch_shapes=[pltpu.VMEM((rows, LANES), jnp.float32)],
         compiler_params=params(),
         name="logits",
-    )(audio, text, probe)
+    )(streamed(audio), text, probe)
 
 
 def put_columns(acc, sum_ref, out_ref):
@@ -211,13 +217,13 @@
     text_copy.start()
     text_copy.wait()
     kernel_copy.start()
-    step = 256
+    step = 2 * audio_ref.shape[1]
     here = step // LANES
     blocks = rows // LANES
 
     def block(i, _):
         base = pl.multiple_of(i * step, step)
-        left = audio_ref[pl.ds(base, step), :]
+        left = audio_ref[pl.ds(2 * i, 2)].reshape(step, audio_ref.shape[2])
         best = None
         for j in range(columns // WIDTH):
             x = 10.0 * contract_last(left, text_ref[pl.ds(j * WIDTH, WIDTH), :])
@@ -243,19 +249,20 @@
 
 
 def student_softmax(audio, text, kernel):
-    rows, columns, depth = audio.shape[0], text.shape[0], audio.shape[1]
+    rows, columns = audio.shape[0] * audio.shape[1] // 2, text.shape[0]
     return pl.pallas_call(
         student_kernel,
+        grid=(1,),
         out_shape=(
             pltpu.VMEM((2, rows, columns), jnp.float32),
             jax.ShapeDtypeStruct((2 * (rows // LANES), LANES), jnp.float32),
         ),
-        in_specs=[VMEM, pl.BlockSpec(memory_space=pltpu.HBM), pl.BlockSpec(memory_space=pltpu.HBM)],
+        in_specs=[audio_half(audio, 1), pl.BlockSpec(memory_space=pltpu.HBM), pl.BlockSpec(memory_space=pltpu.HBM)],
         out_specs=(VMEM, VMEM),
         scratch_shapes=[pltpu.VMEM(text.shape, text.dtype), pltpu.SemaphoreType.DMA, pltpu.SemaphoreType.DMA],
         compiler_params=params(),
         name="student_softmax",
-    )(audio, streamed(text), streamed(kernel))
+    )(streamed(audio), streamed(text), streamed(kernel))
 
 
 def residual_kernel(
@@ -289,10 +296,11 @@
 
     @pl.when(i == pl.num_programs(0) - 1)
     def _():
+        audio = audio_ref[...].reshape(rows, depth)
         for j in range(columns // WIDTH):
             grad = lax.dot_general(
                 residual_ref[:, pl.ds(j * WIDTH, WIDTH)],
-                audio_ref[...],
+                audio,
                 (((0,), (0,)), ((), ())),
                 preferred_element_type=jnp.float32,
             )
@@ -301,7 +309,7 @@
 
 def residual_grads(row_parts, scale, own, pair, audio, text, dtype):
     rows, columns = pair.shape[1:]
-    depth = audio.shape[1]
+    depth = audio.shape[2]
     step = 256
     return pl.pallas_call(
         residual_kernel,
@@ -310,7 +318,7 @@
             jax.ShapeDtypeStruct((rows, depth), jnp.float32),
             pltpu.VMEM((columns, depth), dtype),
         ),
-        in_specs=[VMEM] * 6,
+        in_specs=[VMEM] * 4 + [audio_half(audio, 1), VMEM],
         out_specs=(pl.BlockSpec((step, depth), lambda i: (i, 0)), VMEM),
         scratch_shapes=[
             pltpu.VMEM((rows, LANES), jnp.float32),
@@ -319,7 +327,7 @@
         ],
         compiler_params=params(19 * 1024 * 1024),
         name="residual_grads",
-    )(row_parts, scale, own, resident(pair), audio, text)
+    )(row_parts, scale, own, resident(pair), streamed(audio), text)
 
 
 def resident(x):
@@ -340,27 +348,24 @@
 
 
 def body(clips, caps, teacher_audio, teacher_text, student_audio, student_text):
-    count, depth = teacher_audio.shape
     audio = jnp.concatenate([teacher_audio, student_audio], axis=0)
     audio = lax.all_gather(audio, "cap", axis=0)
     text_t = gather_a2a(teacher_text, "clip", clips)
     probe = text_t[:16, :LANES]
     student_text, probe = lax.optimization_barrier((student_text, probe))
     text_s = lax.all_gather(student_text, "clip", axis=0, tiled=True)
-    audio_t = audio[:, :count].reshape(-1, depth)
-    audio_s = audio[:, count:].reshape(-1, depth)
-    logits, maxima = teacher_logits(audio_t, text_t, probe, caps)
+    logits, maxima = teacher_logits(audio, text_t, probe, caps)
     kernel, columns = exp_columns(swap(maxima, "cap"), logits, clips)
     for _ in range(ITERS - 1):
         row_parts, _ = row_sums(swap(columns, "clip"), kernel, caps)
         columns = column_sums(swap(row_parts, "cap"), kernel, clips)
-    columns, text_s, audio_s = lax.optimization_barrier((columns, text_s, audio_s))
-    columns, audio_s = lax.optimization_barrier((swap(columns, "clip"), audio_s))
-    pair, stats = student_softmax(audio_s, text_s, kernel)
+    columns, text_s = lax.optimization_barrier((columns, text_s))
+    columns, audio = lax.optimization_barrier((swap(columns, "clip"), audio))
+    pair, stats = student_softmax(audio, text_s, kernel)
     row_parts, scale = row_sums(columns, pair, caps, stats)
     row_parts = swap(row_parts, "cap")
     audio_part, text_part = residual_grads(
-        row_parts, scale, stats, pair, audio_s, text_s, jnp.bfloat16
+        row_parts, scale, stats, pair, audio, text_s, jnp.bfloat16
     )
     audio_grad = lax.psum_scatter(audio_part, "cap", scatter_dimension=0, tiled=True)
     text_parts = swap(text_part.reshape(clips, -1, text_part.shape[1]), "clip")

time: 235 us -> 231 us (0.983)
  local copies, waits for them, and re-layouts: 4.6 us -> 1.23 us
    slice x1 -> x0, local copies, waits for them, and re-layouts: 3.37 us -> none  [body(): audio_s = audio[:, count:].reshape(-1, depth)]
  transfers between devices with their start and end apart: 3 -> 3, of which waited for: 0 -> 0; matrix products, arithmetic and copies ran while one was open for 2% -> 1% of each run, Pallas kernels for 8% -> 9%
where the time goes in v6:
time: 231 us; the launch traced here: 230 us
  blocking collectives  160 us (69%)
  Pallas kernels  51.6 us (22%)
  between operations  13.8 us (6%)
  other arithmetic  2.97 us (1%)
    all_to_all x8, blocking collectives, swap(): return lax.all_to_all(x, axis, 0, 0)  114 us
    all_to_all x1, blocking collectives, gather_a2a(): lax.all_to_all(spread, axis, 0, 0).reshape(n * x.shape[0], x.shape[1])  46.5 us
    pallas_call x1, Pallas kernels, residual_grads(): pl.pallas_call(residual_kernel, grid=(rows // step,), out_shape=(jax.Shap...  15 us
    pallas_call x1, Pallas kernels, student_softmax(): pl.pallas_call(student_kernel, grid=(1,), out_shape=(pltpu.VMEM((2, rows,...  12.8 us
    pallas_call x3, Pallas kernels, row_sums(): pl.pallas_call(body, out_shape=(jax.ShapeDtypeStruct((peers, rows // LANE...  7.7 us
    pallas_call x1, Pallas kernels, teacher_logits(): pl.pallas_call(logits_kernel, grid=(1,), out_shape=(pltpu.VMEM((rows, col...  7.39 us
    pallas_call x1, Pallas kernels, exp_columns(): pl.pallas_call(exp_kernel, out_shape=(pltpu.VMEM((rows, columns), jnp.flo...  4.65 us
  transfers between devices with their start and end apart: 3, of which 0 were waited for; matrix products, arithmetic and copies ran while one was open for 1% of the time, Pallas kernels for 9%

profile of v6, /device:TPU:0, one launch (start us, length us, event | category | flops | bytes accessed | tf_op | source)
XLA Modules:
  0.0 230.1 jit_solution(6990932987392304185)
XLA Ops:
  7.2 0.0 all-gather.6.cloned.1.call-start
  7.2 1.8 pad_maximum_fusion
  9.0 0.0 all-gather.6.cloned.1.call-update
  9.0 0.0 all-gather.4.cloned.1.call-start
  9.1 1.2 broadcast_in_dim.2
  10.3 46.5 %all_to_all.45 = bf16[16,192,512]{2,1,0:T(8,128)(2,1)S(1)} all-to-all(bf16[16,192,512]{2,1,0:T(8,128)(2,1)S(1)} %broadcast_in_dim.2), channel_id=1, replica_groups=mesh['clip'=16,'cap'=8] {'clip'}, dimensions={0} | all-to-all | bytes 6291456 | tf_op jit(solution)/shard_map/all_to_all | solution.py:343
  56.9 0.0 all-gather.4.cloned.1.call-update
  56.9 0.0 reduce-scatter.2.cloned.1.call-start
  56.9 0.0 all-gather.6.cloned.1.call-done
  57.0 7.4 %logits.1 = (f32[1536,3072]{1,0:T(8,128)S(1)}, f32[8,12,128]{2,1,0:T(8,128)S(1)}) custom-call(bf16[8,384,512]{2,1,0:T(8,128)(2,1)} %bitcast.6, bf16[3072,512]{1,0:T(8,128)(2,1)S(1)} %bitcast.4, bf16[16,128]{1,0:T(8,128)(2,1)S(1)} %slice.4.probe_ref), custom_call_target="tpu_custom_call" | custom-call | tf_op jit(solution)/shard_map/logits/pallas_call | solution.py:83
  64.3 10.7 %all_to_all.46.max_ref = f32[8,12,128]{2,1,0:T(8,128)S(1)} all-to-all(f32[8,12,128]{2,1,0:T(8,128)S(1)} %get-tuple-element.21), channel_id=1, replica_groups=mesh['clip'=16,'cap'=8] {'cap'}, dimensions={0} | all-to-all | bytes 98304 | tf_op jit(solution)/shard_map/all_to_all | solution.py:347
  75.1 4.6 %exp_columns.1 = (f32[1536,3072]{1,0:T(8,128)S(1)}, f32[16,24,128]{2,1,0:T(8,128)S(1)}) custom-call(f32[8,12,128]{2,1,0:T(8,128)S(1)} %all_to_all.46.max_ref, f32[1536,3072]{1,0:T(8,128)S(1)} %get-tuple-element.22.logits_ref), custom_call_target="tpu_custom_call", output_to_operand_aliasing={{0}: (1, {})} | custom-call | tf_op jit(solution)/shard_map/exp_columns/pallas_call | solution.py:123
  79.7 0.0 copy-start
  79.8 11.3 %all_to_all.47.parts_ref = f32[16,24,128]{2,1,0:T(8,128)S(1)} all-to-all(f32[16,24,128]{2,1,0:T(8,128)S(1)} %get-tuple-element.23), channel_id=1, replica_groups=mesh['clip'=16,'cap'=8] {'clip'}, dimensions={0} | all-to-all | bytes 393216 | tf_op jit(solution)/shard_map/all_to_all | solution.py:347
  91.0 2.1 row_sums.3
  93.2 8.0 %all_to_all.48.parts_ref = f32[8,12,128]{2,1,0:T(8,128)S(1)} all-to-all(f32[8,12,128]{2,1,0:T(8,128)S(1)} %get-tuple-element.25), channel_id=1, replica_groups=mesh['clip'=16,'cap'=8] {'cap'}, dimensions={0} | all-to-all | bytes 98304 | tf_op jit(solution)/shard_map/all_to_all | solution.py:347
  101.2 2.0 column_sums.2
  103.2 11.3 %all_to_all.49.parts_ref = f32[16,24,128]{2,1,0:T(8,128)S(1)} all-to-all(f32[16,24,128]{2,1,0:T(8,128)S(1)} %column_sums.2), channel_id=1, replica_groups=mesh['clip'=16,'cap'=8] {'clip'}, dimensions={0} | all-to-all | bytes 393216 | tf_op jit(solution)/shard_map/all_to_all | solution.py:347
  114.5 2.1 row_sums.4
  116.7 8.0 %all_to_all.50.parts_ref = f32[8,12,128]{2,1,0:T(8,128)S(1)} all-to-all(f32[8,12,128]{2,1,0:T(8,128)S(1)} %get-tuple-element.26), channel_id=1, replica_groups=mesh['clip'=16,'cap'=8] {'cap'}, dimensions={0} | all-to-all | bytes 98304 | tf_op jit(solution)/shard_map/all_to_all | solution.py:347
  124.7 0.0 copy-done
  124.7 2.0 column_sums.3
  126.7 0.0 all-gather.4.cloned.1.call-done.text_hbm_ref.text_ref
  126.7 11.6 %all_to_all.51.parts_ref = f32[16,24,128]{2,1,0:T(8,128)} all-to-all(f32[16,24,128]{2,1,0:T(8,128)S(1)} %column_sums.3), channel_id=1, replica_groups=mesh['clip'=16,'cap'=8] {'clip'}, dimensions={0} | all-to-all | bytes 393216 | tf_op jit(solution)/shard_map/all_to_all | solution.py:347
  138.3 12.8 %student_softmax.1 = (f32[2,1536,3072]{2,1,0:T(8,128)S(1)}, f32[24,128]{1,0:T(8,128)}) custom-call(bf16[8,384,512]{2,1,0:T(8,128)(2,1)} %bitcast.7, bf16[3072,512]{1,0:T(8,128)(2,1)} %all-gather.4.cloned.1.call-done.text_hbm_ref.text_ref, f32[1536,3072]{1,0:T(8,128)} %copy-done), custom_call_target="tpu_custom_call" | custom-call | tf_op jit(solution)/shard_map/student_softmax/pallas_call | solution.py:253
  151.1 3.4 %row_sums.5 = (f32[8,36,128]{2,1,0:T(8,128)}, f32[24,128]{1,0:T(8,128)}) custom-call(f32[16,24,128]{2,1,0:T(8,128)} %all_to_all.51.parts_ref, f32[2,1536,3072]{2,1,0:T(8,128)S(1)} %get-tuple-element.32.kernel_ref.pair_ref, f32[24,128]{1,0:T(8,128)} %get-tuple-element.33.stat_ref.own_ref), custom_call_target="tpu_custom_call" | custom-call | tf_op jit(solution)/shard_map/row_sums/pallas_call | solution.py:170
  154.5 10.5 %all_to_all.52.rows_ref = f32[8,36,128]{2,1,0:T(8,128)} all-to-all(f32[8,36,128]{2,1,0:T(8,128)} %get-tuple-element.34), channel_id=1, replica_groups=mesh['clip'=16,'cap'=8] {'cap'}, dimensions={0} | all-to-all | bytes 294912 | tf_op jit(solution)/shard_map/all_to_all | solution.py:347
  165.0 15.0 %residual_grads.1 = (f32[1536,512]{1,0:T(8,128)}, bf16[3072,512]{1,0:T(8,128)(2,1)S(1)}) custom-call(f32[8,36,128]{2,1,0:T(8,128)} %all_to_all.52.rows_ref, f32[24,128]{1,0:T(8,128)} %get-tuple-element.35.scale_ref, f32[24,128]{1,0:T(8,128)} %get-tuple-element.33.stat_ref.own_ref, f32[2,1536,3072]{2,1,0:T(8,128)S(1)} %get-tuple-element.32.kernel_ref.pair_ref, ...), custom_call_target="tpu_custom_call" | custom-call | tf_op jit(solution)/shard_map/residual_grads/pallas_call | solution.py:314
  180.0 0.0 reduce-scatter.2.cloned.1.call-update
  180.0 42.4 %all_to_all.53 = bf16[16,192,512]{2,1,0:T(8,128)(2,1)S(1)} all-to-all(bf16[16,192,512]{2,1,0:T(8,128)(2,1)S(1)} %bitcast.5), channel_id=1, replica_groups=mesh['clip'=16,'cap'=8] {'clip'}, dimensions={0} | all-to-all | bytes 6291456 | tf_op jit(solution)/shard_map/all_to_all | solution.py:347
  222.4 1.2 convert_reduce_fusion
  223.6 0.0 reduce-scatter.2.cloned.1.call-done
  (1 shorter events, 0.0 us)
Async XLA Ops:
  7.2 49.8 %all-gather.6.cloned.1.call-start = ((), (), s32[]{:S(2)}) async-start(), calls=%async_computation.12 | async-start | bytes 3538944 | tf_op jit(solution)/shard_map/all_gather | solution.py:352
  9.0 117.7 %all-gather.4.cloned.1.call-start = ((), (), s32[]{:S(2)}) async-start(), calls=%async_computation.10 | async-start | bytes 3342336 | tf_op jit(solution)/shard_map/all_gather | solution.py:356
  56.9 166.7 %reduce-scatter.2.cloned.1.call-start = ((), (), s32[]{:S(2)}) async-start(), calls=%async_computation.11 | async-start | bytes 3538944 | tf_op jit(solution)/shard_map/reduce_scatter | solution.py:370
  79.7 44.9 %copy-start = (f32[1536,3072]{1,0:T(8,128)}, f32[1536,3072]{1,0:T(8,128)S(1)}, u32[]{:S(2)}) copy-start(f32[1536,3072]{1,0:T(8,128)S(1)} %get-tuple-element.24.kernel_ref.kernel_hbm_ref) | copy-start | bytes 56623108
Sparse Core Ops, SparseCore 0:
  10.3 30.4 all-gather.5
  57.0 46.3 all-gather.3
  180.1 32.2 reduce-scatter.1

commit v7 on v6

--- a/solution.py
+++ b/solution.py
@@ -310,7 +310,7 @@
 def residual_grads(row_parts, scale, own, pair, audio, text, dtype):
     rows, columns = pair.shape[1:]
     depth = audio.shape[2]
-    step = 256
+    step = audio.shape[1]
     return pl.pallas_call(
         residual_kernel,
         grid=(rows // step,),

time: 231 us -> 230 us (level)
  no operation moved by 1% of the time
where the time goes in v7:
time: 230 us
  blocking collectives  160 us (70%)
  Pallas kernels  51.2 us (22%)
  between operations  13.8 us (6%)
  other arithmetic  2.97 us (1%)
    all_to_all x8, blocking collectives, swap(): return lax.all_to_all(x, axis, 0, 0)  114 us
    all_to_all x1, blocking collectives, gather_a2a(): lax.all_to_all(spread, axis, 0, 0).reshape(n * x.shape[0], x.shape[1])  46.5 us
    pallas_call x1, Pallas kernels, residual_grads(): pl.pallas_call(residual_kernel, grid=(rows // step,), out_shape=(jax.Shap...  14.6 us
    pallas_call x1, Pallas kernels, student_softmax(): pl.pallas_call(student_kernel, grid=(1,), out_shape=(pltpu.VMEM((2, rows,...  12.8 us
    pallas_call x3, Pallas kernels, row_sums(): pl.pallas_call(body, out_shape=(jax.ShapeDtypeStruct((peers, rows // LANE...  7.7 us
    pallas_call x1, Pallas kernels, teacher_logits(): pl.pallas_call(logits_kernel, grid=(1,), out_shape=(pltpu.VMEM((rows, col...  7.39 us
    pallas_call x1, Pallas kernels, exp_columns(): pl.pallas_call(exp_kernel, out_shape=(pltpu.VMEM((rows, columns), jnp.flo...  4.65 us
  transfers between devices with their start and end apart: 3, of which 0 were waited for; matrix products, arithmetic and copies ran while one was open for 1% of the time, Pallas kernels for 9%

profile of v7, /device:TPU:0, one launch (start us, length us, event | category | flops | bytes accessed | tf_op | source)
XLA Modules:
  0.0 229.7 jit_solution(13228543036948286210)
XLA Ops:
  7.2 0.0 all-gather.6.cloned.1.call-start
  7.2 1.8 pad_maximum_fusion
  9.0 0.0 all-gather.6.cloned.1.call-update
  9.0 0.0 all-gather.4.cloned.1.call-start
  9.1 1.2 broadcast_in_dim.2
  10.3 46.5 %all_to_all.45 = bf16[16,192,512]{2,1,0:T(8,128)(2,1)S(1)} all-to-all(bf16[16,192,512]{2,1,0:T(8,128)(2,1)S(1)} %broadcast_in_dim.2), channel_id=1, replica_groups=mesh['clip'=16,'cap'=8] {'clip'}, dimensions={0} | all-to-all | bytes 6291456 | tf_op jit(solution)/shard_map/all_to_all | solution.py:343
  56.9 0.0 all-gather.4.cloned.1.call-update
  56.9 0.0 reduce-scatter.2.cloned.1.call-start
  56.9 0.0 all-gather.6.cloned.1.call-done
  57.0 7.4 %logits.1 = (f32[1536,3072]{1,0:T(8,128)S(1)}, f32[8,12,128]{2,1,0:T(8,128)S(1)}) custom-call(bf16[8,384,512]{2,1,0:T(8,128)(2,1)} %bitcast.6, bf16[3072,512]{1,0:T(8,128)(2,1)S(1)} %bitcast.4, bf16[16,128]{1,0:T(8,128)(2,1)S(1)} %slice.4.probe_ref), custom_call_target="tpu_custom_call" | custom-call | tf_op jit(solution)/shard_map/logits/pallas_call | solution.py:83
  64.4 10.7 %all_to_all.46.max_ref = f32[8,12,128]{2,1,0:T(8,128)S(1)} all-to-all(f32[8,12,128]{2,1,0:T(8,128)S(1)} %get-tuple-element.21), channel_id=1, replica_groups=mesh['clip'=16,'cap'=8] {'cap'}, dimensions={0} | all-to-all | bytes 98304 | tf_op jit(solution)/shard_map/all_to_all | solution.py:347
  75.1 4.6 %exp_columns.1 = (f32[1536,3072]{1,0:T(8,128)S(1)}, f32[16,24,128]{2,1,0:T(8,128)S(1)}) custom-call(f32[8,12,128]{2,1,0:T(8,128)S(1)} %all_to_all.46.max_ref, f32[1536,3072]{1,0:T(8,128)S(1)} %get-tuple-element.22.logits_ref), custom_call_target="tpu_custom_call", output_to_operand_aliasing={{0}: (1, {})} | custom-call | tf_op jit(solution)/shard_map/exp_columns/pallas_call | solution.py:123
  79.7 0.0 copy-start
  79.7 11.3 %all_to_all.47.parts_ref = f32[16,24,128]{2,1,0:T(8,128)S(1)} all-to-all(f32[16,24,128]{2,1,0:T(8,128)S(1)} %get-tuple-element.23), channel_id=1, replica_groups=mesh['clip'=16,'cap'=8] {'clip'}, dimensions={0} | all-to-all | bytes 393216 | tf_op jit(solution)/shard_map/all_to_all | solution.py:347
  91.1 2.1 row_sums.3
  93.2 8.0 %all_to_all.48.parts_ref = f32[8,12,128]{2,1,0:T(8,128)S(1)} all-to-all(f32[8,12,128]{2,1,0:T(8,128)S(1)} %get-tuple-element.25), channel_id=1, replica_groups=mesh['clip'=16,'cap'=8] {'cap'}, dimensions={0} | all-to-all | bytes 98304 | tf_op jit(solution)/shard_map/all_to_all | solution.py:347
  101.2 2.0 column_sums.2
  103.2 11.3 %all_to_all.49.parts_ref = f32[16,24,128]{2,1,0:T(8,128)S(1)} all-to-all(f32[16,24,128]{2,1,0:T(8,128)S(1)} %column_sums.2), channel_id=1, replica_groups=mesh['clip'=16,'cap'=8] {'clip'}, dimensions={0} | all-to-all | bytes 393216 | tf_op jit(solution)/shard_map/all_to_all | solution.py:347
  114.5 2.1 row_sums.4
  116.7 8.0 %all_to_all.50.parts_ref = f32[8,12,128]{2,1,0:T(8,128)S(1)} all-to-all(f32[8,12,128]{2,1,0:T(8,128)S(1)} %get-tuple-element.26), channel_id=1, replica_groups=mesh['clip'=16,'cap'=8] {'cap'}, dimensions={0} | all-to-all | bytes 98304 | tf_op jit(solution)/shard_map/all_to_all | solution.py:347
  124.7 0.0 copy-done
  124.7 2.0 column_sums.3
  126.7 0.0 all-gather.4.cloned.1.call-done.text_hbm_ref.text_ref
  126.7 11.6 %all_to_all.51.parts_ref = f32[16,24,128]{2,1,0:T(8,128)} all-to-all(f32[16,24,128]{2,1,0:T(8,128)S(1)} %column_sums.3), channel_id=1, replica_groups=mesh['clip'=16,'cap'=8] {'clip'}, dimensions={0} | all-to-all | bytes 393216 | tf_op jit(solution)/shard_map/all_to_all | solution.py:347
  138.3 12.8 %student_softmax.1 = (f32[2,1536,3072]{2,1,0:T(8,128)S(1)}, f32[24,128]{1,0:T(8,128)}) custom-call(bf16[8,384,512]{2,1,0:T(8,128)(2,1)} %bitcast.7, bf16[3072,512]{1,0:T(8,128)(2,1)} %all-gather.4.cloned.1.call-done.text_hbm_ref.text_ref, f32[1536,3072]{1,0:T(8,128)} %copy-done), custom_call_target="tpu_custom_call" | custom-call | tf_op jit(solution)/shard_map/student_softmax/pallas_call | solution.py:253
  151.1 3.4 %row_sums.5 = (f32[8,36,128]{2,1,0:T(8,128)}, f32[24,128]{1,0:T(8,128)}) custom-call(f32[16,24,128]{2,1,0:T(8,128)} %all_to_all.51.parts_ref, f32[2,1536,3072]{2,1,0:T(8,128)S(1)} %get-tuple-element.32.kernel_ref.pair_ref, f32[24,128]{1,0:T(8,128)} %get-tuple-element.33.stat_ref.own_ref), custom_call_target="tpu_custom_call" | custom-call | tf_op jit(solution)/shard_map/row_sums/pallas_call | solution.py:170
  154.5 10.5 %all_to_all.52.rows_ref = f32[8,36,128]{2,1,0:T(8,128)} all-to-all(f32[8,36,128]{2,1,0:T(8,128)} %get-tuple-element.34), channel_id=1, replica_groups=mesh['clip'=16,'cap'=8] {'cap'}, dimensions={0} | all-to-all | bytes 294912 | tf_op jit(solution)/shard_map/all_to_all | solution.py:347
  165.0 14.6 %residual_grads.1 = (f32[1536,512]{1,0:T(8,128)}, bf16[3072,512]{1,0:T(8,128)(2,1)S(1)}) custom-call(f32[8,36,128]{2,1,0:T(8,128)} %all_to_all.52.rows_ref, f32[24,128]{1,0:T(8,128)} %get-tuple-element.35.scale_ref, f32[24,128]{1,0:T(8,128)} %get-tuple-element.33.stat_ref.own_ref, f32[2,1536,3072]{2,1,0:T(8,128)S(1)} %get-tuple-element.32.kernel_ref.pair_ref, ...), custom_call_target="tpu_custom_call" | custom-call | tf_op jit(solution)/shard_map/residual_grads/pallas_call | solution.py:314
  179.6 0.0 reduce-scatter.2.cloned.1.call-update
  179.7 42.4 %all_to_all.53 = bf16[16,192,512]{2,1,0:T(8,128)(2,1)S(1)} all-to-all(bf16[16,192,512]{2,1,0:T(8,128)(2,1)S(1)} %bitcast.5), channel_id=1, replica_groups=mesh['clip'=16,'cap'=8] {'clip'}, dimensions={0} | all-to-all | bytes 6291456 | tf_op jit(solution)/shard_map/all_to_all | solution.py:347
  222.0 1.2 convert_reduce_fusion
  223.2 0.0 reduce-scatter.2.cloned.1.call-done
  (1 shorter events, 0.0 us)
Async XLA Ops:
  7.2 49.8 %all-gather.6.cloned.1.call-start = ((), (), s32[]{:S(2)}) async-start(), calls=%async_computation.12 | async-start | bytes 3538944 | tf_op jit(solution)/shard_map/all_gather | solution.py:352
  9.0 117.7 %all-gather.4.cloned.1.call-start = ((), (), s32[]{:S(2)}) async-start(), calls=%async_computation.10 | async-start | bytes 3342336 | tf_op jit(solution)/shard_map/all_gather | solution.py:356
  56.9 166.3 %reduce-scatter.2.cloned.1.call-start = ((), (), s32[]{:S(2)}) async-start(), calls=%async_computation.11 | async-start | bytes 3538944 | tf_op jit(solution)/shard_map/reduce_scatter | solution.py:370
  79.7 44.9 %copy-start = (f32[1536,3072]{1,0:T(8,128)}, f32[1536,3072]{1,0:T(8,128)S(1)}, u32[]{:S(2)}) copy-start(f32[1536,3072]{1,0:T(8,128)S(1)} %get-tuple-element.24.kernel_ref.kernel_hbm_ref) | copy-start | bytes 56623108
Sparse Core Ops, SparseCore 0:
  10.3 30.4 all-gather.5
  57.0 46.2 all-gather.3
  179.8 32.3 reduce-scatter.1

commit v8 on v6

--- a/solution.py
+++ b/solution.py
@@ -114,7 +114,7 @@
         kernel_ref[at, :] = k
         return acc + k
 
-    acc = lax.fori_loop(0, rows // 8, step, jnp.zeros((8, columns), jnp.float32), unroll=4)
+    acc = lax.fori_loop(0, rows // 8, step, jnp.zeros((8, columns), jnp.float32), unroll=8)
     put_columns(acc, sum_ref, out_ref)
 
 
@@ -151,7 +151,7 @@
         part_ref[at, :] = fold_lanes(kernel_ref[at, :] * scale, jnp.add)
         return 0
 
-    lax.fori_loop(0, rows // 8, step, 0, unroll=4)
+    lax.fori_loop(0, rows // 8, step, 0, unroll=8)
     for b in range(blocks):
         total = jnp.sum(lanes_of(part_ref, b), axis=0, keepdims=True)
         for k in range(out_ref.shape[0]):
@@ -189,7 +189,7 @@
         at = pl.ds(pl.multiple_of(i * 8, 8), 8)
         return acc + kernel_ref[at, :] * repeat_lanes(col_ref[at, :], columns // LANES)
 
-    acc = lax.fori_loop(0, rows // 8, step, jnp.zeros((8, columns), jnp.float32), unroll=4)
+    acc = lax.fori_loop(0, rows // 8, step, jnp.zeros((8, columns), jnp.float32), unroll=8)
     put_columns(acc, sum_ref, out_ref)
 
 

time: 231 us -> 230 us (level)
  transfers between devices with their start and end apart: 3 -> 3, of which waited for: 0 -> 0; matrix products, arithmetic and copies ran while one was open for 1% -> 1% of each run, Pallas kernels for 9% -> 8%
where the time goes in v8:
time: 230 us; the launch traced here: 229 us
  blocking collectives  160 us (70%)
  Pallas kernels  50.4 us (22%)
  between operations  13.8 us (6%)
  other arithmetic  2.97 us (1%)
    all_to_all x8, blocking collectives, swap(): return lax.all_to_all(x, axis, 0, 0)  114 us
    all_to_all x1, blocking collectives, gather_a2a(): lax.all_to_all(spread, axis, 0, 0).reshape(n * x.shape[0], x.shape[1])  46.5 us
    pallas_call x1, Pallas kernels, residual_grads(): pl.pallas_call(residual_kernel, grid=(rows // step,), out_shape=(jax.Shap...  15 us
    pallas_call x1, Pallas kernels, student_softmax(): pl.pallas_call(student_kernel, grid=(1,), out_shape=(pltpu.VMEM((2, rows,...  12.8 us
    pallas_call x1, Pallas kernels, teacher_logits(): pl.pallas_call(logits_kernel, grid=(1,), out_shape=(pltpu.VMEM((rows, col...  7.39 us
    pallas_call x3, Pallas kernels, row_sums(): pl.pallas_call(body, out_shape=(jax.ShapeDtypeStruct((peers, rows // LANE...  7.16 us
  transfers between devices with their start and end apart: 3, of which 0 were waited for; matrix products, arithmetic and copies ran while one was open for 1% of the time, Pallas kernels for 8%

profile of v8, /device:TPU:0, one launch (start us, length us, event | category | flops | bytes accessed | tf_op | source)
XLA Modules:
  0.0 228.9 jit_solution(5997994591924816933)
XLA Ops:
  7.2 0.0 all-gather.6.cloned.1.call-start
  7.2 1.8 pad_maximum_fusion
  9.0 0.0 all-gather.6.cloned.1.call-update
  9.0 0.0 all-gather.4.cloned.1.call-start
  9.1 1.2 broadcast_in_dim.2
  10.3 46.5 %all_to_all.45 = bf16[16,192,512]{2,1,0:T(8,128)(2,1)S(1)} all-to-all(bf16[16,192,512]{2,1,0:T(8,128)(2,1)S(1)} %broadcast_in_dim.2), channel_id=1, replica_groups=mesh['clip'=16,'cap'=8] {'clip'}, dimensions={0} | all-to-all | bytes 6291456 | tf_op jit(solution)/shard_map/all_to_all | solution.py:343
  56.9 0.0 all-gather.4.cloned.1.call-update
  56.9 0.0 reduce-scatter.2.cloned.1.call-start
  56.9 0.0 all-gather.6.cloned.1.call-done
  57.0 7.4 %logits.1 = (f32[1536,3072]{1,0:T(8,128)S(1)}, f32[8,12,128]{2,1,0:T(8,128)S(1)}) custom-call(bf16[8,384,512]{2,1,0:T(8,128)(2,1)} %bitcast.6, bf16[3072,512]{1,0:T(8,128)(2,1)S(1)} %bitcast.4, bf16[16,128]{1,0:T(8,128)(2,1)S(1)} %slice.4.probe_ref), custom_call_target="tpu_custom_call" | custom-call | tf_op jit(solution)/shard_map/logits/pallas_call | solution.py:83
  64.3 10.7 %all_to_all.46.max_ref = f32[8,12,128]{2,1,0:T(8,128)S(1)} all-to-all(f32[8,12,128]{2,1,0:T(8,128)S(1)} %get-tuple-element.21), channel_id=1, replica_groups=mesh['clip'=16,'cap'=8] {'cap'}, dimensions={0} | all-to-all | bytes 98304 | tf_op jit(solution)/shard_map/all_to_all | solution.py:347
  75.1 4.5 %exp_columns.1 = (f32[1536,3072]{1,0:T(8,128)S(1)}, f32[16,24,128]{2,1,0:T(8,128)S(1)}) custom-call(f32[8,12,128]{2,1,0:T(8,128)S(1)} %all_to_all.46.max_ref, f32[1536,3072]{1,0:T(8,128)S(1)} %get-tuple-element.22.logits_ref), custom_call_target="tpu_custom_call", output_to_operand_aliasing={{0}: (1, {})} | custom-call | tf_op jit(solution)/shard_map/exp_columns/pallas_call | solution.py:123
  79.6 0.0 copy-start
  79.6 11.3 %all_to_all.47.parts_ref = f32[16,24,128]{2,1,0:T(8,128)S(1)} all-to-all(f32[16,24,128]{2,1,0:T(8,128)S(1)} %get-tuple-element.23), channel_id=1, replica_groups=mesh['clip'=16,'cap'=8] {'clip'}, dimensions={0} | all-to-all | bytes 393216 | tf_op jit(solution)/shard_map/all_to_all | solution.py:347
  90.9 2.0 row_sums.3
  92.8 8.0 %all_to_all.48.parts_ref = f32[8,12,128]{2,1,0:T(8,128)S(1)} all-to-all(f32[8,12,128]{2,1,0:T(8,128)S(1)} %get-tuple-element.25), channel_id=1, replica_groups=mesh['clip'=16,'cap'=8] {'cap'}, dimensions={0} | all-to-all | bytes 98304 | tf_op jit(solution)/shard_map/all_to_all | solution.py:347
  100.8 1.8 column_sums.2
  102.6 11.3 %all_to_all.49.parts_ref = f32[16,24,128]{2,1,0:T(8,128)S(1)} all-to-all(f32[16,24,128]{2,1,0:T(8,128)S(1)} %column_sums.2), channel_id=1, replica_groups=mesh['clip'=16,'cap'=8] {'clip'}, dimensions={0} | all-to-all | bytes 393216 | tf_op jit(solution)/shard_map/all_to_all | solution.py:347
  113.9 2.0 row_sums.4
  115.9 8.0 %all_to_all.50.parts_ref = f32[8,12,128]{2,1,0:T(8,128)S(1)} all-to-all(f32[8,12,128]{2,1,0:T(8,128)S(1)} %get-tuple-element.26), channel_id=1, replica_groups=mesh['clip'=16,'cap'=8] {'cap'}, dimensions={0} | all-to-all | bytes 98304 | tf_op jit(solution)/shard_map/all_to_all | solution.py:347
  123.9 0.0 copy-done
  123.9 1.8 column_sums.3
  125.7 0.0 all-gather.4.cloned.1.call-done.text_hbm_ref.text_ref
  125.7 11.6 %all_to_all.51.parts_ref = f32[16,24,128]{2,1,0:T(8,128)} all-to-all(f32[16,24,128]{2,1,0:T(8,128)S(1)} %column_sums.3), channel_id=1, replica_groups=mesh['clip'=16,'cap'=8] {'clip'}, dimensions={0} | all-to-all | bytes 393216 | tf_op jit(solution)/shard_map/all_to_all | solution.py:347
  137.3 12.8 %student_softmax.1 = (f32[2,1536,3072]{2,1,0:T(8,128)S(1)}, f32[24,128]{1,0:T(8,128)}) custom-call(bf16[8,384,512]{2,1,0:T(8,128)(2,1)} %bitcast.7, bf16[3072,512]{1,0:T(8,128)(2,1)} %all-gather.4.cloned.1.call-done.text_hbm_ref.text_ref, f32[1536,3072]{1,0:T(8,128)} %copy-done), custom_call_target="tpu_custom_call" | custom-call | tf_op jit(solution)/shard_map/student_softmax/pallas_call | solution.py:253
  150.1 3.3 %row_sums.5 = (f32[8,36,128]{2,1,0:T(8,128)}, f32[24,128]{1,0:T(8,128)}) custom-call(f32[16,24,128]{2,1,0:T(8,128)} %all_to_all.51.parts_ref, f32[2,1536,3072]{2,1,0:T(8,128)S(1)} %get-tuple-element.32.kernel_ref.pair_ref, f32[24,128]{1,0:T(8,128)} %get-tuple-element.33.stat_ref.own_ref), custom_call_target="tpu_custom_call" | custom-call | tf_op jit(solution)/shard_map/row_sums/pallas_call | solution.py:170
  153.4 10.5 %all_to_all.52.rows_ref = f32[8,36,128]{2,1,0:T(8,128)} all-to-all(f32[8,36,128]{2,1,0:T(8,128)} %get-tuple-element.34), channel_id=1, replica_groups=mesh['clip'=16,'cap'=8] {'cap'}, dimensions={0} | all-to-all | bytes 294912 | tf_op jit(solution)/shard_map/all_to_all | solution.py:347
  163.8 15.0 %residual_grads.1 = (f32[1536,512]{1,0:T(8,128)}, bf16[3072,512]{1,0:T(8,128)(2,1)S(1)}) custom-call(f32[8,36,128]{2,1,0:T(8,128)} %all_to_all.52.rows_ref, f32[24,128]{1,0:T(8,128)} %get-tuple-element.35.scale_ref, f32[24,128]{1,0:T(8,128)} %get-tuple-element.33.stat_ref.own_ref, f32[2,1536,3072]{2,1,0:T(8,128)S(1)} %get-tuple-element.32.kernel_ref.pair_ref, ...), custom_call_target="tpu_custom_call" | custom-call | tf_op jit(solution)/shard_map/residual_grads/pallas_call | solution.py:314
  178.8 0.0 reduce-scatter.2.cloned.1.call-update
  178.9 42.4 %all_to_all.53 = bf16[16,192,512]{2,1,0:T(8,128)(2,1)S(1)} all-to-all(bf16[16,192,512]{2,1,0:T(8,128)(2,1)S(1)} %bitcast.5), channel_id=1, replica_groups=mesh['clip'=16,'cap'=8] {'clip'}, dimensions={0} | all-to-all | bytes 6291456 | tf_op jit(solution)/shard_map/all_to_all | solution.py:347
  221.2 1.2 convert_reduce_fusion
  222.4 0.0 reduce-scatter.2.cloned.1.call-done
  (1 shorter events, 0.0 us)
Async XLA Ops:
  7.2 49.8 %all-gather.6.cloned.1.call-start = ((), (), s32[]{:S(2)}) async-start(), calls=%async_computation.12 | async-start | bytes 3538944 | tf_op jit(solution)/shard_map/all_gather | solution.py:352
  9.0 116.7 %all-gather.4.cloned.1.call-start = ((), (), s32[]{:S(2)}) async-start(), calls=%async_computation.10 | async-start | bytes 3342336 | tf_op jit(solution)/shard_map/all_gather | solution.py:356
  56.9 165.5 %reduce-scatter.2.cloned.1.call-start = ((), (), s32[]{:S(2)}) async-start(), calls=%async_computation.11 | async-start | bytes 3538944 | tf_op jit(solution)/shard_map/reduce_scatter | solution.py:370
  79.6 44.3 %copy-start = (f32[1536,3072]{1,0:T(8,128)}, f32[1536,3072]{1,0:T(8,128)S(1)}, u32[]{:S(2)}) copy-start(f32[1536,3072]{1,0:T(8,128)S(1)} %get-tuple-element.24.kernel_ref.kernel_hbm_ref) | copy-start | bytes 56623108
Sparse Core Ops, SparseCore 0:
  10.3 30.4 all-gather.5
  57.0 46.2 all-gather.3
  179.0 32.2 reduce-scatter.1
